TPU v7x, 32 devices: a whole 2x2x4 slice. The times are simulated.
32 devices in a mesh: groups: 1, section: 32 (over z, y, x, core).
Axes of the slice: x: 2, y: 2, z: 4, core: 2. Of those that a mesh axis runs over, the one named last changes fastest.
Arguments:
- queries: bfloat16 [256, 4096], P(('groups', 'section')), may hold values from -170 to 170, as said below
- key_value_cache: bfloat16 [2, 32768, 512], P(None, ('groups', 'section')), may hold values from -6 to 6, as said below
- block_ids: int32 [256, 8], P(('groups', 'section')), may hold values from 0 to 511, as said below
- block_len: int32 [512], P(('groups', 'section')), may hold values from 1 to 64
- residual_in: bfloat16 [256, 2048], P(('groups', 'section')), may hold values from -6 to 6
- out_weight: bfloat16 [4096, 2048], P('section'), may hold values from -0.375 to 0.375
- norm_gain: float32 [2048], replicated, may hold values from 0.1 to 1.9
- expert_ids: int32 [256, 8], P(('groups', 'section')), may hold values from 0 to 31, all different within a row; in each aligned block of 8 rows (0 to 7, 8 to 15, ...) at most 2 rows name the same one
- route_weight: float32 [256, 8], P(('groups', 'section')), may hold values from 0.05 to 0.5
- w_gate: bfloat16 [32, 2048, 768], P('section'), may hold values from -0.125 to 0.125
- w_up: bfloat16 [32, 2048, 768], P('section'), may hold values from -0.125 to 0.125
- w_down: bfloat16 [32, 768, 2048], P('section'), may hold values from -0.21875 to 0.21875
Outputs:
- attn_proj: bfloat16 [256, 2048], P(('groups', 'section'))
- layer_out: bfloat16 [256, 2048], P(('groups', 'section'))
Inputs may be any that keep to these rules, and one draw needn't show every extreme that they name: queries lie within the printed range. key_value_cache lies within the printed range. `block_ids`: block b belongs to device b // 16. Row r's j-th block lies in the j-th of 8 equal ranges of the pool. A device's rows fall into runs of 4 rows in order (the last run may be shorter); no two blocks read by the rows of one run lie on the same device. `expert_ids`: each row names 8 different experts; among the rows of one device no expert is named more than 2 times.
All inputs are finite; a program needn't handle non-finite values.
Results may differ from a plain program's by a relative error of at most 0.008.
Values may be sent and summed in bfloat16 or wider, within the bound.
No kernel may reach another device: no remote copies, remote signals or barrier semaphores. Data moves between devices by JAX's collectives and lax.ppermute only.
A program may use at most 128 MiB of HBM per device.

v0:
```python
import jax
import jax.numpy as jnp
from jax import lax
from jax.sharding import PartitionSpec as P

D = 2048
QUERY_HEADS = 32
KEY_VALUE_HEADS = 4
HEAD_WIDTH = 128
TOPK = 8
CAP = 2
BLOCK_TOKENS = 64
PICKED_BLOCKS = 8


def shards(
    queries,
    key_value_cache,
    block_ids,
    block_len,
    residual_in,
    out_weight,
    norm_gain,
    expert_ids,
    route_weight,
    w_gate,
    w_up,
    w_down,
):
    devices = lax.axis_size("section")
    row_count = queries.shape[0]
    width = queries.shape[1]
    block_offset = block_len.shape[0]
    group_width = QUERY_HEADS // KEY_VALUE_HEADS
    run_length = devices // PICKED_BLOCKS
    slot_count_q = (row_count + run_length - 1) // run_length
    run_of = jnp.arange(row_count) // run_length
    holder = block_ids // block_offset
    device_ids = jnp.arange(devices, dtype=jnp.int32)
    is_hit = holder[None, :, :] == device_ids[:, None, None]
    row_pick = jnp.any(is_hit, axis=2)
    run_match = run_of[None, :] == jnp.arange(slot_count_q, dtype=jnp.int32)[:, None]
    place_query = row_pick[:, None, :] & run_match[None, :, :]
    send_query = jnp.einsum(
        "dsr,rw->dsw", place_query.astype(jnp.bfloat16), queries, preferred_element_type=jnp.float32
    ).astype(jnp.bfloat16)
    local_index = jnp.sum(
        jnp.where(is_hit, block_ids[None, :, :] - device_ids[:, None, None] * block_offset, 0),
        axis=2,
    )
    local_block = jnp.sum(jnp.where(place_query, local_index[:, None, :], 0), axis=2)
    send_block = jnp.where(jnp.any(place_query, axis=2), local_block, -1)
    cache_block_table = key_value_cache.reshape(
        2, block_offset, BLOCK_TOKENS, KEY_VALUE_HEADS * HEAD_WIDTH
    )
    query_input = lax.all_to_all(send_query, "section", split_axis=0, concat_axis=0, tiled=True)
    block_in = lax.all_to_all(send_block, "section", split_axis=0, concat_axis=0, tiled=True)
    lead_count = query_input.shape[0]
    slot_count = query_input.shape[1]
    flat_block = block_in.reshape(-1)
    safe_block = jnp.clip(flat_block, 0, block_offset - 1)
    picked_blocks = jnp.take(cache_block_table, safe_block, axis=1)
    key_matrix = picked_blocks[0].reshape(-1, BLOCK_TOKENS, KEY_VALUE_HEADS, HEAD_WIDTH)
    value_matrix = picked_blocks[1].reshape(-1, BLOCK_TOKENS, KEY_VALUE_HEADS, HEAD_WIDTH)
    query_head_rows = query_input.reshape(-1, KEY_VALUE_HEADS, group_width, HEAD_WIDTH)
    scores = jnp.einsum(
        "mkgd,mtkd->mkgt", query_head_rows, key_matrix, preferred_element_type=jnp.float32
    ) * HEAD_WIDTH ** (-0.5)
    lengths = jnp.take(block_len, safe_block)
    is_valid = (jnp.arange(BLOCK_TOKENS)[None, :] < lengths[:, None]) & (flat_block >= 0)[:, None]
    token_mask = is_valid[:, None, None, :]
    block_peak = jnp.max(jnp.where(token_mask, scores, -1e30), axis=-1)
    weights = jnp.where(token_mask, jnp.exp(scores - block_peak[..., None]), 0.0).astype(
        jnp.bfloat16
    )
    totals = jnp.sum(weights.astype(jnp.float32), axis=-1)
    weighted = jnp.einsum(
        "mkgt,mtkd->mkgd", weights, value_matrix, preferred_element_type=jnp.float32
    )
    peak_back, total_back, sum_back = (
        lax.all_to_all(
            block_peak.reshape(lead_count, slot_count, QUERY_HEADS),
            "section",
            split_axis=0,
            concat_axis=0,
            tiled=True,
        ),
        lax.all_to_all(
            totals.reshape(lead_count, slot_count, QUERY_HEADS),
            "section",
            split_axis=0,
            concat_axis=0,
            tiled=True,
        ),
        lax.all_to_all(
            weighted.reshape(lead_count, slot_count, width),
            "section",
            split_axis=0,
            concat_axis=0,
            tiled=True,
        ),
    )
    flat_source = (holder * slot_count_q + run_of[:, None]).reshape(-1)
    row_peak = jnp.take(peak_back.reshape(-1, QUERY_HEADS), flat_source, axis=0).reshape(
        row_count, PICKED_BLOCKS, QUERY_HEADS
    )
    row_total = jnp.take(total_back.reshape(-1, QUERY_HEADS), flat_source, axis=0).reshape(
        row_count, PICKED_BLOCKS, QUERY_HEADS
    )
    row_sum = jnp.take(sum_back.reshape(-1, width), flat_source, axis=0).reshape(
        row_count, PICKED_BLOCKS, QUERY_HEADS, HEAD_WIDTH
    )
    overall = jnp.max(row_peak, axis=1)
    factor = jnp.exp(row_peak - overall[:, None, :])
    numerator = jnp.sum(factor[..., None] * row_sum, axis=1)
    denominator = jnp.sum(factor * row_total, axis=1)
    attention = (numerator / denominator[..., None]).reshape(row_count, width).astype(jnp.bfloat16)
    projected = jnp.dot(
        attention,
        lax.all_gather(out_weight, "section", axis=0, tiled=True),
        preferred_element_type=jnp.float32,
    )
    attn_proj = projected.astype(jnp.bfloat16)
    stream = residual_in.astype(jnp.float32) + attn_proj.astype(jnp.float32)
    normed = (
        stream * lax.rsqrt(jnp.mean(stream * stream, axis=-1, keepdims=True) + 1e-06) * norm_gain
    ).astype(jnp.bfloat16)
    assign = row_count * TOPK
    flat_expert = expert_ids.reshape(-1)
    same_expert = flat_expert[:, None] == flat_expert[None, :]
    earlier = jnp.arange(assign)[:, None] > jnp.arange(assign)[None, :]
    slot_index = jnp.sum(same_expert & earlier, axis=1)
    per_device = w_gate.shape[0]
    slot_total = devices * per_device * CAP
    target = flat_expert * CAP + slot_index
    onehot_slots = jnp.arange(slot_total)[:, None] == target[None, :]
    place_rows = jnp.sum(onehot_slots.reshape(slot_total, row_count, TOPK), axis=2).astype(
        jnp.bfloat16
    )
    send_rows = (
        jnp.dot(place_rows, normed, preferred_element_type=jnp.float32)
        .astype(jnp.bfloat16)
        .reshape(devices, per_device, CAP, D)
    )
    arrived = lax.all_to_all(send_rows, "section", split_axis=0, concat_axis=0, tiled=True)
    gate_act = jnp.einsum("necd,edf->necf", arrived, w_gate, preferred_element_type=jnp.float32)
    up_act = jnp.einsum("necd,edf->necf", arrived, w_up, preferred_element_type=jnp.float32)
    hidden = (jax.nn.silu(gate_act) * up_act).astype(jnp.bfloat16)
    expert_out = jnp.einsum(
        "necf,efd->necd", hidden, w_down, preferred_element_type=jnp.float32
    ).astype(jnp.bfloat16)
    returned = lax.all_to_all(expert_out, "section", split_axis=0, concat_axis=0, tiled=True)
    combine = jnp.sum(
        jnp.where(onehot_slots, route_weight.reshape(-1)[None, :], 0.0).reshape(
            slot_total, row_count, TOPK
        ),
        axis=2,
    )
    moe_sum = jnp.dot(
        combine.T,
        returned.reshape(slot_total, D).astype(jnp.float32),
        precision=lax.Precision.HIGHEST,
    )
    layer_out = (stream + moe_sum).astype(jnp.bfloat16)
    return (attn_proj, layer_out)


def solution(mesh):
    placed = (
        P(("groups", "section"), None),
        P(None, ("groups", "section"), None),
        P(("groups", "section"), None),
        P(("groups", "section")),
        P(("groups", "section"), None),
        P("section", None),
        P(),
        P(("groups", "section"), None),
        P(("groups", "section"), None),
        P("section", None, None),
        P("section", None, None),
        P("section", None, None),
    )
    return jax.shard_map(
        shards,
        mesh=mesh,
        in_specs=placed,
        out_specs=(P(("groups", "section"), None), P(("groups", "section"), None)),
        check_vma=False,
    )
```

profile of v0, /device:TPU:0, one launch (start us, length us, event | category | flops | bytes accessed | tf_op | source)
XLA Modules:
  0.0 215.3 jit_solution(16772232777697774943)
XLA Ops:
  7.2 0.7 all-gather.2.cloned.1.call-update
  7.9 0.9 add_select_fusion
  8.8 0.1 fusion.60
  8.9 0.1 and_reduce_fusion
  9.0 0.8 select_reduce_fusion.2
  9.8 0.1 fusion.70
  9.9 0.7 copy.45
  10.6 7.3 %all-to-all-start = ((s32[32,1,2]{2,1,0:T(1,128)}), s32[32,1,2]{2,1,0:T(1,128)S(1)}, u32[]{:S(2)}, u32[]{:S(2)}) async-start(s32[32,1,2]{2,1,0:T(1,128)} %copy.45), calls=%async_computation | async-start | bytes 32768 | tf_op jit(solution)/shard_map/all_to_all | solution.py:57
  17.9 1.2 convolution_convert_fusion
  19.2 1.3 copy.46
  20.5 4.5 %all-to-all-done = s32[32,1,2]{2,1,0:T(1,128)S(1)} async-done(((s32[32,1,2]{2,1,0:T(1,128)}), s32[32,1,2]{2,1,0:T(1,128)S(1)}, u32[]{:S(2)}, u32[]{:S(2)}) %all-to-all-start) | async-done | bytes 288 | tf_op jit(solution)/shard_map/all_to_all | solution.py:57
  25.0 3.3 %all-to-all-start.1 = ((bf16[32,2,4096]{2,1,0:T(2,128)(2,1)}), bf16[32,2,4096]{2,1,0:T(2,128)(2,1)}, u32[]{:S(2)}, u32[]{:S(2)}) async-start(bf16[32,2,4096]{2,1,0:T(2,128)(2,1)} %copy.46), calls=%async_computation.1 | async-start | bytes 1048576 | tf_op jit(solution)/shard_map/all_to_all | solution.py:56
  28.4 0.1 fusion.86
  28.4 0.1 min.18
  28.5 0.1 min.16
  28.7 1.4 gather_fusion
  30.1 7.1 %gather_fusion.1 = bf16[64,2,64,512]{3,2,1,0:T(8,128)(2,1)} fusion(bf16[2,16,64,512]{3,2,1,0:T(8,128)(2,1)} %bitcast.124, s32[1024]{0:T(1024)S(1)} %pad_clamp_fusion.2), kind=kCustom, calls=%fused_computation.3 | custom fusion | bytes 16777472 | tf_op jit(solution)/shard_map/jit(_take)/gather | solution.py:62
  37.2 7.5 %select_bitcast_fusion = bf16[2,64,64,512]{3,2,0,1:T(8,128)(2,1)} fusion(bf16[64,2,64,512]{3,2,1,0:T(8,128)(2,1)} %gather_fusion.1, pred[64]{0:T(512)(128)(4,1)S(1)} %get-tuple-element.6), kind=kLoop, calls=%fused_computation.5 | loop fusion | flops 4194304 | bytes 16777280 | tf_op jit(solution)/shard_map/jit(_take)/select_n | solution.py:62
  44.7 6.0 %fusion.87 = (bf16[1,64,64,512]{3,2,0,1:T(8,128)(2,1)}, bf16[1,64,64,512]{3,2,0,1:T(8,128)(2,1)}) fusion(bf16[2,64,64,512]{3,2,0,1:T(8,128)(2,1)} %select_bitcast_fusion), kind=kLoop, calls=%fused_computation.127 | loop fusion | bytes 16777216 | tf_op jit(solution)/shard_map/slice | solution.py:63
  50.7 7.0 %reshape_squeeze.6 = bf16[64,64,4,128]{3,2,1,0:T(4,128)(2,1)} reshape(bf16[1,64,64,512]{3,2,0,1:T(8,128)(2,1)} %get-tuple-element.7) | data formatting | bytes 8388608 | tf_op jit(solution)/shard_map/reshape;squeeze | solution.py:63
  57.7 0.1 compare_reduce_fusion
  57.7 0.1 ge.45
  57.9 0.1 fusion.61
  58.0 2.2 %reshape.319 = bf16[64,4,8,128]{3,2,1,0:T(8,128)(2,1)} reshape(bf16[32,2,4096]{2,1,0:T(2,128)(2,1)} %all-to-all-done.1) | data formatting | bytes 1048576 | tf_op jit(solution)/shard_map/reshape | solution.py:65
  60.2 4.8 %select_reduce_fusion = (f32[64,4,8]{2,1,0:T(4,128)S(1)}, f32[64,4,8,64]{3,2,1,0:T(8,128)S(1)}) fusion(pred[64,64]{1,0:T(8,128)(4,1)S(1)} %fusion.61, bf16[64,4,8,128]{3,2,1,0:T(8,128)(2,1)} %reshape.319, bf16[64,64,4,128]{3,2,1,0:T(4,128)(2,1)} %reshape_squeeze.6), kind=kOutput, calls=%fused_computation.34 | convolution fusion | flops 33945600 | bytes 5255168 | tf_op jit(solution)/shard_map/mkgd,mtkd->mkgt/dot_general | solution.py:66
  65.0 1.0 copy-done.1
  65.9 0.8 convert_reduce_fusion
  66.7 0.8 reshape.328
  67.5 5.8 %all-to-all-start.4 = ((f32[32,2,32]{2,1,0:T(2,128)}), f32[32,2,32]{2,1,0:T(2,128)S(1)}, u32[]{:S(2)}, u32[]{:S(2)}) async-start(f32[32,2,32]{2,1,0:T(2,128)} %reshape.328), calls=%async_computation.4 | async-start | bytes 65536 | tf_op jit(solution)/shard_map/all_to_all | solution.py:88
  73.2 6.9 %reshape_squeeze.7 = bf16[64,64,4,128]{3,2,1,0:T(4,128)(2,1)} reshape(bf16[1,64,64,512]{3,2,0,1:T(8,128)(2,1)} %get-tuple-element.8) | data formatting | bytes 8388608 | tf_op jit(solution)/shard_map/reshape;squeeze | solution.py:64
  80.2 0.7 reshape.321
  80.9 5.8 %all-to-all-start.2 = ((f32[32,2,32]{2,1,0:T(2,128)}), f32[32,2,32]{2,1,0:T(2,128)S(1)}, u32[]{:S(2)}, u32[]{:S(2)}) async-start(f32[32,2,32]{2,1,0:T(2,128)} %reshape.321), calls=%async_computation.2 | async-start | bytes 65536 | tf_op jit(solution)/shard_map/all_to_all | solution.py:81
  86.8 4.8 %fusion = f32[64,4,8,128]{3,2,1,0:T(8,128)} fusion(bf16[64,64,4,128]{3,2,1,0:T(4,128)(2,1)} %reshape_squeeze.7, f32[64,4,8,64]{3,2,1,0:T(8,128)} %copy-done.1, f32[64,4,8]{2,1,0:T(4,128)S(1)} %get-tuple-element.11, pred[64,64]{1,0:T(8,128)(4,1)S(1)} %fusion.61), kind=kOutput, calls=%fused_computation.7 | convolution fusion | flops 33947648 | bytes 5779456 | tf_op jit(solution)/shard_map/mkgt,mtkd->mkgd/dot_general | solution.py:77
  91.6 2.8 %reshape.325 = f32[32,2,4096]{2,1,0:T(2,128)} reshape(f32[64,4,8,128]{3,2,1,0:T(8,128)} %fusion) | data formatting | bytes 2097152 | tf_op jit(solution)/shard_map/reshape | solution.py:96
  94.4 0.0 all-to-all-done.2
  94.5 6.1 %all-to-all-start.3 = ((f32[32,2,4096]{2,1,0:T(2,128)}), f32[32,2,4096]{2,1,0:T(2,128)}, u32[]{:S(2)}, u32[]{:S(2)}) async-start(f32[32,2,4096]{2,1,0:T(2,128)} %reshape.325), calls=%async_computation.3 | async-start | bytes 2097152 | tf_op jit(solution)/shard_map/all_to_all | solution.py:95
  100.6 0.1 compare_and_fusion
  100.6 0.1 reshape.323
  100.7 0.1 reshape.327
  100.8 0.1 eq.69
  100.9 0.2 convert_reduce_fusion.2
  101.1 0.1 reduce_sum.89
  101.2 0.1 convert_reduce_fusion.1
  101.3 0.6 gather_fusion.4
  101.9 0.6 gather_fusion.3
  102.5 0.8 fusion.55
  103.3 0.1 copy.48
  103.4 49.0 %all-to-all-done.3 = f32[32,2,4096]{2,1,0:T(2,128)} async-done(((f32[32,2,4096]{2,1,0:T(2,128)}), f32[32,2,4096]{2,1,0:T(2,128)}, u32[]{:S(2)}, u32[]{:S(2)}) %all-to-all-start.3) | async-done | bytes 1048608 | tf_op jit(solution)/shard_map/all_to_all | solution.py:95
  152.4 3.0 %reshape.326 = f32[64,4096]{1,0:T(8,128)} reshape(f32[32,2,4096]{2,1,0:T(2,128)} %all-to-all-done.3) | data formatting | bytes 2097152 | tf_op jit(solution)/shard_map/reshape | solution.py:110
  155.4 3.7 %gather_fusion.2 = f32[64,4096]{1,0:T(8,128)} fusion(f32[64,4096]{1,0:T(8,128)} %reshape.326, s32[1024]{0:T(1024)S(1)} %pad_clamp_fusion), kind=kCustom, calls=%fused_computation.4 | custom fusion | bytes 2097408 | tf_op jit(solution)/shard_map/jit(_take)/gather | solution.py:110
  159.1 1.6 fusion.36
  160.7 0.1 fusion.54
  160.9 8.2 %multiply_reduce_fusion = (f32[8]{0:T(128)S(1)}, bf16[8,2048]{1,0:T(8,128)(2,1)S(1)}) fusion(bf16[8,2048]{1,0:T(8,128)(2,1)S(1)} %copy-done.2, bf16[4096,2048]{1,0:T(8,128)(2,1)} %all-gather.2.cloned.1.call-done, bf16[1,8,32,128]{3,2,1,0:T(8,128)(2,1)S(1)} %fusion.54), kind=kOutput, calls=%fused_computation.50 | convolution fusion | flops 134316032 | bytes 16908320 | tf_op jit(solution)/shard_map/dot_general | solution.py:118
  169.1 0.3 convolution_convert_fusion.1
  169.4 0.9 reshape.331
  170.2 13.3 %all_to_all.36 = bf16[32,1,2,2048]{3,2,1,0:T(2,128)(2,1)S(1)} all-to-all(bf16[32,1,2,2048]{3,2,1,0:T(2,128)(2,1)} %bitcast.127), channel_id=1, replica_groups=mesh['groups'=1,'section'=32] {'section'}, dimensions={0} | all-to-all | bytes 524288 | tf_op jit(solution)/shard_map/all_to_all | solution.py:145
  183.6 3.3 %fusion.20 = f32[32,1,2,768]{3,0,2,1:T(8,128)} fusion(bf16[1,2048,768]{2,1,0:T(8,128)(2,1)} %param.23, bf16[32,1,2,2048]{3,2,1,0:T(2,128)(2,1)S(1)} %all_to_all.36), kind=kOutput, calls=%fused_computation.24 | convolution fusion | flops 201326592 | bytes 3604480 | tf_op jit(solution)/shard_map/necd,edf->necf/dot_general | solution.py:146
  186.8 4.0 %fusion.13 = bf16[32,1,2,2048]{3,0,2,1:T(8,128)(2,1)} fusion(bf16[1,768,2048]{2,1,0:T(8,128)(2,1)S(1)} %copy-done, bf16[1,2048,768]{2,1,0:T(8,128)(2,1)} %param.24, bf16[32,1,2,2048]{3,2,1,0:T(2,128)(2,1)S(1)} %all_to_all.36, f32[32,1,2,768]{3,0,2,1:T(8,128)} %fusion.20), kind=kOutput, calls=%fused_computation.19 | convolution fusion | flops 403079168 | bytes 7012352 | tf_op jit(solution)/shard_map/necf,efd->necd/dot_general | solution.py:149
  190.8 1.9 copy.52
  192.7 2.6 %all-to-all-start.6 = ((bf16[32,1,2,2048]{3,2,1,0:T(2,128)(2,1)}), bf16[32,1,2,2048]{3,2,1,0:T(2,128)(2,1)S(1)}, u32[]{:S(2)}, u32[]{:S(2)}) async-start(bf16[32,1,2,2048]{3,2,1,0:T(2,128)(2,1)} %copy.52), calls=%async_computation.6 | async-start | bytes 524288 | tf_op jit(solution)/shard_map/all_to_all | solution.py:152
  195.3 0.1 select_reduce_fusion.1
  195.4 10.5 %all-to-all-done.6 = bf16[32,1,2,2048]{3,2,1,0:T(2,128)(2,1)S(1)} async-done(((bf16[32,1,2,2048]{3,2,1,0:T(2,128)(2,1)}), bf16[32,1,2,2048]{3,2,1,0:T(2,128)(2,1)S(1)}, u32[]{:S(2)}, u32[]{:S(2)}) %all-to-all-start.6) | async-done | bytes 262176 | tf_op jit(solution)/shard_map/all_to_all | solution.py:152
  205.9 0.8 reshape.337
  206.7 1.8 fusion.16
  (33 shorter events, 0.2 us)
Async XLA Ops:
  7.2 179.7 %copy-start = (bf16[1,768,2048]{2,1,0:T(8,128)(2,1)S(1)}, bf16[1,768,2048]{2,1,0:T(8,128)(2,1)}, u32[]{:S(2)}) copy-start(bf16[1,768,2048]{2,1,0:T(8,128)(2,1)} %param.25) | copy-start | bytes 9437188
  7.2 153.7 %all-gather.2.cloned.1.call-start = ((), (), s32[]{:S(2)}) async-start(), calls=%async_computation.7 | async-start | bytes 17301504 | tf_op jit(solution)/shard_map/all_gather | solution.py:120
  10.6 14.4 %all-to-all-start = ((s32[32,1,2]{2,1,0:T(1,128)}), s32[32,1,2]{2,1,0:T(1,128)S(1)}, u32[]{:S(2)}, u32[]{:S(2)}) async-start(s32[32,1,2]{2,1,0:T(1,128)} %copy.45), calls=%async_computation | async-start | bytes 32768 | tf_op jit(solution)/shard_map/all_to_all | solution.py:57
  25.0 32.9 %all-to-all-start.1 = ((bf16[32,2,4096]{2,1,0:T(2,128)(2,1)}), bf16[32,2,4096]{2,1,0:T(2,128)(2,1)}, u32[]{:S(2)}, u32[]{:S(2)}) async-start(bf16[32,2,4096]{2,1,0:T(2,128)(2,1)} %copy.46), calls=%async_computation.1 | async-start | bytes 1048576 | tf_op jit(solution)/shard_map/all_to_all | solution.py:56
  65.0 1.0 copy-start.1
  67.5 13.5 %all-to-all-start.4 = ((f32[32,2,32]{2,1,0:T(2,128)}), f32[32,2,32]{2,1,0:T(2,128)S(1)}, u32[]{:S(2)}, u32[]{:S(2)}) async-start(f32[32,2,32]{2,1,0:T(2,128)} %reshape.328), calls=%async_computation.4 | async-start | bytes 65536 | tf_op jit(solution)/shard_map/all_to_all | solution.py:88
  80.9 13.5 %all-to-all-start.2 = ((f32[32,2,32]{2,1,0:T(2,128)}), f32[32,2,32]{2,1,0:T(2,128)S(1)}, u32[]{:S(2)}, u32[]{:S(2)}) async-start(f32[32,2,32]{2,1,0:T(2,128)} %reshape.321), calls=%async_computation.2 | async-start | bytes 65536 | tf_op jit(solution)/shard_map/all_to_all | solution.py:81
  86.8 13.8 %copy-start.4 = (s32[8,8]{1,0:T(8,128)S(1)}, s32[8,8]{1,0:T(8,128)}, u32[]{:S(2)}) copy-start(s32[8,8]{1,0:T(8,128)} %param.16) | copy-start | bytes 772
  86.8 14.0 %copy-start.5 = (s32[8,8]{1,0:T(8,128)S(1)}, s32[8,8]{1,0:T(8,128)}, u32[]{:S(2)}) copy-start(s32[8,8]{1,0:T(8,128)} %param.21) | copy-start | bytes 772
  94.5 57.9 %all-to-all-start.3 = ((f32[32,2,4096]{2,1,0:T(2,128)}), f32[32,2,4096]{2,1,0:T(2,128)}, u32[]{:S(2)}, u32[]{:S(2)}) async-start(f32[32,2,4096]{2,1,0:T(2,128)} %reshape.325), calls=%async_computation.3 | async-start | bytes 2097152 | tf_op jit(solution)/shard_map/all_to_all | solution.py:95
  155.4 5.5 %copy-start.2 = (bf16[8,2048]{1,0:T(8,128)(2,1)S(1)}, bf16[8,2048]{1,0:T(8,128)(2,1)}, u32[]{:S(2)}) copy-start(bf16[8,2048]{1,0:T(8,128)(2,1)} %param.18) | copy-start | bytes 98308
  160.8 8.2 %copy-start.6 = (f32[2048]{0:T(1024)S(1)}, f32[2048]{0:T(1024)}, u32[]{:S(2)}) copy-start(f32[2048]{0:T(1024)} %param.20) | copy-start | bytes 24580
  169.0 37.6 %copy-start.3 = (bf16[8,2048]{1,0:T(8,128)(2,1)}, bf16[8,2048]{1,0:T(8,128)(2,1)S(1)}, u32[]{:S(2)}) copy-start(bf16[8,2048]{1,0:T(8,128)(2,1)S(1)} %get-tuple-element.16) | copy-start | bytes 98308
  186.8 8.5 %copy-start.7 = (f32[8,8]{1,0:T(8,128)S(1)}, f32[8,8]{1,0:T(8,128)}, u32[]{:S(2)}) copy-start(f32[8,8]{1,0:T(8,128)} %param.22) | copy-start | bytes 772
  192.7 13.2 %all-to-all-start.6 = ((bf16[32,1,2,2048]{3,2,1,0:T(2,128)(2,1)}), bf16[32,1,2,2048]{3,2,1,0:T(2,128)(2,1)S(1)}, u32[]{:S(2)}, u32[]{:S(2)}) async-start(bf16[32,1,2,2048]{3,2,1,0:T(2,128)(2,1)} %copy.52), calls=%async_computation.6 | async-start | bytes 524288 | tf_op jit(solution)/shard_map/all_to_all | solution.py:152
Sparse Core Ops, SparseCore 0:
  10.8 146.8 all-gather.1
where the time goes:
time: 217 us; the launch traced here: 215 us
  waiting for transfers between devices  64.7 us (30%)
  local copies, waits for them, and re-layouts  50.3 us (23%)
  starting transfers between devices  31 us (14%)
  matrix products  28.2 us (13%)
  between operations  14.4 us (7%)
  other arithmetic  13.4 us (6%)
  blocking collectives  13.3 us (6%)
    all_to_all x1, waiting for transfers between devices, shards(): lax.all_to_all(weighted.reshape(lead_count, slot_count, width), 'section'...  49 us
    all_to_all x1, blocking collectives, shards(): lax.all_to_all(send_rows, 'section', split_axis=0, concat_axis=0, tiled=T...  13.3 us
    all_to_all x1, waiting for transfers between devices, shards(): lax.all_to_all(expert_out, 'section', split_axis=0, concat_axis=0, tiled=...  10.5 us
    dot_general x1, matrix products, shards(): jnp.dot(attention, lax.all_gather(out_weight, 'section', axis=0, tiled=Tr...  8.15 us
    select_n x1, other arithmetic, shards(): picked_blocks = jnp.take(cache_block_table, safe_block, axis=1)  7.48 us
    all_to_all x1, starting transfers between devices, shards(): lax.all_to_all(send_block, 'section', split_axis=0, concat_axis=0, tiled=...  7.33 us
    gather x1, local copies, waits for them, and re-layouts, shards(): picked_blocks = jnp.take(cache_block_table, safe_block, axis=1)  7.12 us
    another operation x1, local copies, waits for them, and re-layouts, shards(): picked_blocks[0].reshape(-1, BLOCK_TOKENS, KEY_VALUE_HEADS, HEAD_WIDTH)  7 us
  transfers between devices with their start and end apart: 7, of which 3 were waited for; matrix products, arithmetic and copies ran while one was open for 32% of the time, Pallas kernels for 0%

commit v1 on v0

v1 whole, which is shorter than its diff:
```python
import functools

import jax
import jax.numpy as jnp
from jax import lax
from jax.experimental import pallas as pl
from jax.experimental.pallas import tpu as pltpu
from jax.sharding import PartitionSpec as P

HEADS = 32
KV_HEADS = 4
WIDTH = 128
CAP = 2
BLOCK_TOKENS = 64
LANES = 128
GROUP = 2
STATS = 8
NEG = -1e30
BF = jnp.bfloat16
F32 = jnp.float32

VM = pl.BlockSpec(memory_space=pltpu.VMEM)
SM = pl.BlockSpec(memory_space=pltpu.SMEM)


def call(kernel, out_shape, in_specs, scratch, name, flops=0, nbytes=0, outs=None):
    return pl.pallas_call(
        kernel,
        out_shape=out_shape,
        in_specs=in_specs,
        out_specs=outs if outs is not None else jax.tree.map(lambda _: VM, out_shape),
        scratch_shapes=scratch,
        name=name,
        cost_estimate=pl.CostEstimate(flops=flops, bytes_accessed=nbytes, transcendentals=0),
    )


def pack_kernel(run, slots, blocks, ids, q, out, qs, meta):
    rows = q.shape[0]
    picks = ids.shape[1]
    for h in range(HEADS):
        qs[pl.ds(h, rows, stride=HEADS), :] = q[:, h * WIDTH:(h + 1) * WIDTH].astype(F32)
    meta[...] = jnp.zeros_like(meta)
    if rows * picks != out.shape[0] * slots:
        out[...] = jnp.zeros_like(out)
    lane = lax.broadcasted_iota(jnp.int32, (1, LANES), 1)
    for r in range(rows):
        tile = qs[r * HEADS:(r + 1) * HEADS, :].astype(BF)
        slot = r // run
        for j in range(picks):
            b = ids[r, j]
            dev = lax.div(b, blocks)
            local = b - dev * blocks
            out[dev, slot * HEADS:(slot + 1) * HEADS, :] = tile
            meta[dev, slot:slot + 1, :] = jnp.where(
                lane == 0, local + 1, jnp.where(lane == 1, r % run, 0)
            ).astype(F32)
    out[:, slots * HEADS:, :] = meta[...].astype(BF)


def attend_kernel(n, slots, g, hg, lens, x, kv, out, qf, qb, mf, bias, sc, wb, st):
    blocks = lens.shape[0]
    tokens = kv.shape[1]
    pairs = n * slots
    per = pairs // g
    cnt = n // g
    ngrp = n // g
    qrows = slots * HEADS
    gw = HEADS // KV_HEADS

    def unpack(d, _):
        base = pl.multiple_of(d * qrows, qrows)
        qf[pl.ds(base, qrows), :] = x[d, 0:qrows, :].astype(F32)
        mb = pl.multiple_of(d * 8, 8)
        mf[pl.ds(mb, 8), :] = x[d, qrows:qrows + 8, :].astype(F32)
        return 0

    lax.fori_loop(0, n, unpack, 0, unroll=4)

    def heads(h, _):
        parts = []
        for i in range(g):
            for q in range(slots):
                parts.append(qf[pl.ds(i * qrows + q * HEADS + h, cnt, stride=g * qrows), :])
        base = pl.multiple_of(h * pairs, pairs)
        qb[pl.ds(base, pairs), :] = jnp.concatenate(parts, axis=0).astype(BF)
        return 0

    lax.fori_loop(0, HEADS, heads, 0, unroll=4)

    parts = []
    for i in range(g):
        for q in range(slots):
            parts.append(mf[pl.ds(i * 8 + q, cnt, stride=g * 8), :])
    mp = jnp.concatenate(parts, axis=0)
    blk = mp[:, 0:1].astype(jnp.int32) - 1
    rr = mp[:, 1:2]
    length = jnp.zeros_like(blk)
    for b in range(blocks):
        length = jnp.where(blk == b, lens[b], length)
    first = blk * BLOCK_TOKENS
    last = first + length
    tok = lax.broadcasted_iota(jnp.int32, (pairs, tokens), 1)
    bias[...] = jnp.where((tok >= first) & (tok < last), 0.0, NEG)
    st[...] = jnp.zeros_like(st)
    lane = lax.broadcasted_iota(jnp.int32, (pairs, HEADS * STATS), 1)

    def kv_head(k, _):
        off = pl.multiple_of(k * WIDTH, WIDTH)
        qbase = pl.multiple_of(k * (gw * pairs), gw * pairs)
        sc[...] = lax.dot_general(
            qb[pl.ds(qbase, gw * pairs), :], kv[0, :, pl.ds(off, WIDTH)],
            (((1,), (1,)), ((), ())), preferred_element_type=F32)

        def soft(hh, _):
            base = pl.multiple_of(hh * pairs, pairs)
            s = sc[pl.ds(base, pairs), :] * (WIDTH ** -0.5) + bias[...]
            m = jnp.max(s, axis=-1, keepdims=True)
            m = jnp.maximum(m, -1e20).astype(BF).astype(F32)
            w = jnp.exp(s - m).astype(BF)
            wb[pl.ds(base, pairs), :] = w
            l = jnp.sum(w.astype(F32), axis=-1, keepdims=True)
            hi = l.astype(BF).astype(F32)
            h = k * gw + hh
            at = lax.rem(h, hg) * (ngrp * STATS) + lax.div(h, hg) * STATS
            st[...] = jnp.where(lane == at, m, jnp.where(
                lane == at + 1, hi, jnp.where(
                    lane == at + 2, l - hi, jnp.where(lane == at + 3, rr, st[...]))))
            return 0

        lax.fori_loop(0, gw, soft, 0)
        o = jnp.dot(wb[...], kv[1, :, pl.ds(off, WIDTH)], preferred_element_type=F32)
        for hh in range(gw):
            h = k * gw + hh
            grp = lax.div(h, hg)
            if gw % hg == 0:
                inner = hh % hg
                for i in range(g):
                    r0 = hh * pairs + i * per
                    out[grp * g + i, inner * per:(inner + 1) * per, :] = o[r0:r0 + per, :].astype(BF)
            else:
                raise ValueError("group heads")
        return 0

    lax.fori_loop(0, KV_HEADS, kv_head, 0)

    tt = jnp.concatenate(
        [jnp.transpose(st[:, a:a + LANES]) for a in range(0, HEADS * STATS, LANES)], axis=0)
    span = ngrp * STATS
    copies = LANES // (hg * per)
    for i in range(g):
        row = jnp.concatenate(
            [tt[hh * span:(hh + 1) * span, i * per:(i + 1) * per] for hh in range(hg)] * copies, axis=1)
        for grp in range(ngrp):
            out[grp * g + i, hg * per:, :] = row[grp * STATS:(grp + 1) * STATS, :].astype(BF)


def project_kernel(n, slots, g, hg, run, rows, x, wo, wo2, out, sf, cm, ws):
    pairs = n * slots
    per = pairs // g
    span = hg * per
    cnt = n // g
    fw = wo.shape[0]
    par = lax.rem(lax.axis_index("section"), 2)
    ws[pl.ds(pl.multiple_of(par * fw, fw), fw), :] = wo[...]
    ws[pl.ds(pl.multiple_of((1 - par) * fw, fw), fw), :] = wo2[...]
    sf[...] = x[:, span:, :].astype(F32).reshape(n * STATS, LANES)
    m = sf[pl.ds(0, n, stride=STATS), :]
    l = sf[pl.ds(1, n, stride=STATS), :] + sf[pl.ds(2, n, stride=STATS), :]
    rid = sf[pl.ds(3, n, stride=STATS), :]
    peak = jnp.zeros_like(m)
    for r in range(run):
        mine = rid == r
        top = jnp.max(jnp.where(mine, m, -3e38), axis=0, keepdims=True)
        peak = jnp.where(mine, top, peak)
    f = jnp.exp(m - peak)
    fl = f * l
    den = jnp.ones_like(m)
    for r in range(run):
        mine = rid == r
        tot = jnp.sum(jnp.where(mine, fl, 0.0), axis=0, keepdims=True)
        den = jnp.where(mine, tot, den)
    c = f / den
    lane = lax.broadcasted_iota(jnp.int32, (n, LANES), 1)
    inner = lax.rem(lane, span)
    hh = lax.div(inner, per)
    pl_ = lax.rem(inner, per)
    q = lax.div(pl_, cnt)
    s = lax.rem(pl_, cnt)
    local = rows * cnt
    target = hh * local + s * rows + q * run + rid.astype(jnp.int32)
    dpt = LANES // span
    total = hg * local
    row = lax.broadcasted_iota(jnp.int32, (total, LANES), 0)
    side = lax.div(lax.broadcasted_iota(jnp.int32, (1, LANES), 1), span)
    for t in range(n // dpt):
        blk_c = c[t * dpt:t * dpt + 1, :]
        blk_t = target[t * dpt:t * dpt + 1, :]
        for u in range(1, dpt):
            d = t * dpt + u
            blk_c = jnp.where(side == u, c[d:d + 1, :], blk_c)
            blk_t = jnp.where(side == u, target[d:d + 1, :], blk_t)
        cm[:, t * LANES:(t + 1) * LANES] = jnp.where(row == blk_t, blk_c, 0.0).astype(BF)
    a = x[:, 0:span, :].reshape(n * span, LANES)
    att = jnp.dot(cm[...], a, preferred_element_type=F32).astype(BF)
    att = jnp.concatenate([att[i * local:(i + 1) * local, :] for i in range(hg)], axis=1)
    for col in range(0, ws.shape[1], 512):
        p = jnp.dot(att, ws[:, col:col + 512], preferred_element_type=F32)
        out[:, :, col:col + 512] = p.reshape(cnt, rows, 512).astype(BF)


def norm_kernel(eid, slot, x, res, gain, proj, out, nf):
    rows, width = res.shape
    acc = x[0].astype(F32)
    for i in range(1, x.shape[0]):
        acc = acc + x[i].astype(F32)
    p = acc.astype(BF)
    proj[...] = p
    stream = res[...].astype(F32) + p.astype(F32)
    ms = jnp.mean(stream * stream, axis=-1, keepdims=True)
    nrm = stream * lax.rsqrt(ms + 1e-06) * gain[...]
    tiles = width // LANES
    for c in range(tiles):
        nf[pl.ds(c, rows, stride=tiles), :] = nrm[:, c * LANES:(c + 1) * LANES]
    if rows * eid.shape[1] != out.shape[0] * CAP:
        out[...] = jnp.zeros_like(out)
    for r in range(rows):
        tile = nf[r * tiles:(r + 1) * tiles, :].astype(BF)
        for k in range(eid.shape[1]):
            out[eid[r, k], slot[r, k]] = tile


def expert_kernel(x, wg, wu, wd, out, xf, xb, of, gb, ub, db, sg, su, sd):
    n, cap, tiles, _ = x.shape
    m = n * cap
    width, ffe = wg.shape[0], wg.shape[1]
    kc = width // 4
    fc = ffe // 3
    gate = [pltpu.make_async_copy(wg.at[pl.ds(i * kc, kc)], gb.at[pl.ds(i * kc, kc)], sg.at[i]) for i in range(4)]
    up = [pltpu.make_async_copy(wu.at[pl.ds(i * kc, kc)], ub.at[pl.ds(i * kc, kc)], su.at[i]) for i in range(4)]
    down = [pltpu.make_async_copy(wd.at[pl.ds(i * fc, fc)], db.at[pl.ds(i * fc, fc)], sd.at[i]) for i in range(3)]
    for a, b in zip(gate, up):
        a.start()
        b.start()
    for a in down:
        a.start()
    xf[...] = x[...].astype(F32).reshape(m * tiles, LANES)
    for c in range(tiles):
        xb[:, c * LANES:(c + 1) * LANES] = xf[pl.ds(c, m, stride=tiles), :].astype(BF)
    ga = jnp.zeros((m, ffe), F32)
    ua = jnp.zeros((m, ffe), F32)
    for i in range(4):
        xs = xb[:, i * kc:(i + 1) * kc]
        gate[i].wait()
        ga = ga + jnp.dot(xs, gb[i * kc:(i + 1) * kc, :], preferred_element_type=F32)
        up[i].wait()
        ua = ua + jnp.dot(xs, ub[i * kc:(i + 1) * kc, :], preferred_element_type=F32)
    h = (ga / (1.0 + jnp.exp(-ga)) * ua).astype(BF)
    for a in down:
        a.wait()
    for c in range(0, width, 512):
        o = jnp.dot(h, db[:, c:c + 512], preferred_element_type=F32)
        for t in range(4):
            of[pl.ds(c // LANES + t, m, stride=tiles), :] = o[:, t * LANES:(t + 1) * LANES]
    out[...] = of[...].astype(BF).reshape(n, cap, tiles, LANES)


def finish_kernel(eid, slot, rw, x, res, proj, out, acc):
    rows, width = res.shape
    tiles = width // LANES
    for r in range(rows):
        a = jnp.zeros((tiles, LANES), F32)
        for k in range(eid.shape[1]):
            a = a + rw[r, k] * x[eid[r, k], slot[r, k]].astype(F32)
        acc[r * tiles:(r + 1) * tiles, :] = a
    for c in range(tiles):
        sl = slice(c * LANES, (c + 1) * LANES)
        stream = res[:, sl].astype(F32) + proj[:, sl].astype(F32)
        out[:, sl] = (stream + acc[pl.ds(c, rows, stride=tiles), :]).astype(BF)


def shards(
    queries,
    key_value_cache,
    block_ids,
    block_len,
    residual_in,
    out_weight,
    norm_gain,
    expert_ids,
    route_weight,
    w_gate,
    w_up,
    w_down,
):
    n = lax.axis_size("section")
    rows, qwidth = queries.shape
    picks = block_ids.shape[1]
    blocks = block_len.shape[0]
    width = residual_in.shape[1]
    tokens = key_value_cache.shape[1]
    run = n // picks
    slots = (rows + run - 1) // run
    g = GROUP
    fw = out_weight.shape[0]
    hg = g * fw // WIDTH
    pairs = n * slots
    per = pairs // g
    span = hg * per
    cnt = n // g
    tiles = width // LANES
    gw = HEADS // KV_HEADS
    a2a = functools.partial(
        lax.all_to_all, axis_name="section", split_axis=0, concat_axis=0, tiled=True)
    sds = jax.ShapeDtypeStruct

    other_weight = lax.ppermute(out_weight, "section", [(i, i ^ 1) for i in range(n)])
    flat = expert_ids.reshape(-1)
    order = jnp.arange(flat.shape[0])
    slot = jnp.sum(
        (flat[:, None] == flat[None, :]) & (order[:, None] > order[None, :]), axis=1
    ).astype(jnp.int32).reshape(expert_ids.shape)

    chunk = slots * HEADS + 8
    sent = call(
        functools.partial(pack_kernel, run, slots, blocks),
        sds((n, chunk, LANES), BF), [SM, VM],
        [pltpu.VMEM((rows * HEADS, LANES), F32), pltpu.VMEM((n, 8, LANES), F32)],
        "pack", nbytes=n * chunk * LANES * 2,
    )(block_ids, queries)
    asked = a2a(sent)
    parts = call(
        functools.partial(attend_kernel, n, slots, g, hg),
        sds((n, span + STATS, LANES), BF), [SM, VM, VM],
        [
            pltpu.VMEM((pairs * HEADS, LANES), F32),
            pltpu.VMEM((pairs * HEADS, LANES), BF),
            pltpu.VMEM((n * 8, LANES), F32),
            pltpu.VMEM((pairs, tokens), F32),
            pltpu.VMEM((gw * pairs, tokens), F32),
            pltpu.VMEM((gw * pairs, tokens), BF),
            pltpu.VMEM((pairs, HEADS * STATS), F32),
        ],
        "attend", flops=4 * HEADS * pairs * tokens * WIDTH, nbytes=1 << 22,
    )(block_len, asked, key_value_cache)
    back = a2a(parts)
    local = rows * cnt
    partial = call(
        functools.partial(project_kernel, n, slots, g, hg, run, rows),
        sds((cnt, rows, width), BF), [VM, VM, VM],
        [
            pltpu.VMEM((n * STATS, LANES), F32),
            pltpu.VMEM((hg * local, n * span), BF),
            pltpu.VMEM((g * fw, width), BF),
        ],
        "project", flops=2 * local * g * fw * width, nbytes=1 << 21,
    )(back, out_weight, other_weight)
    summed = a2a(partial, axis_index_groups=[[s * g + i for s in range(cnt)] for i in range(g)])
    experts = n * w_gate.shape[0]
    attn_proj, routed = call(
        norm_kernel,
        (sds((rows, width), BF), sds((experts, CAP, tiles, LANES), BF)), [SM, SM, VM, VM, VM],
        [pltpu.VMEM((rows * tiles, LANES), F32)],
        "norm", nbytes=1 << 20,
    )(expert_ids, slot, summed, residual_in, norm_gain.reshape(1, width))
    arrived = a2a(routed)
    ffe = w_gate.shape[2]
    hbm = pl.BlockSpec(memory_space=pl.ANY)
    slots_in = n * CAP

    def run_expert(xin, wg, wu, wd):
        return call(
            expert_kernel,
            sds((n, CAP, tiles, LANES), BF), [VM, hbm, hbm, hbm],
            [
                pltpu.VMEM((slots_in * tiles, LANES), F32),
                pltpu.VMEM((slots_in, width), BF),
                pltpu.VMEM((slots_in * tiles, LANES), F32),
                pltpu.VMEM((width, ffe), BF),
                pltpu.VMEM((width, ffe), BF),
                pltpu.VMEM((ffe, width), BF),
                pltpu.SemaphoreType.DMA((4,)),
                pltpu.SemaphoreType.DMA((4,)),
                pltpu.SemaphoreType.DMA((3,)),
            ],
            "experts", flops=6 * slots_in * width * ffe, nbytes=6 * width * ffe,
        )(xin, wg, wu, wd)

    per_device = w_gate.shape[0]
    if per_device == 1:
        done = run_expert(arrived, w_gate[0], w_up[0], w_down[0])
    else:
        split = arrived.reshape(n, per_device, CAP, tiles, LANES)
        done = jnp.stack(
            [run_expert(split[:, e], w_gate[e], w_up[e], w_down[e]) for e in range(per_device)], axis=1
        ).reshape(arrived.shape)
    returned = a2a(done)
    layer_out = call(
        finish_kernel,
        sds((rows, width), BF), [SM, SM, SM, VM, VM, VM],
        [pltpu.VMEM((rows * tiles, LANES), F32)],
        "finish", nbytes=1 << 19,
    )(expert_ids, slot, route_weight, returned, residual_in, attn_proj)
    return (attn_proj, layer_out)


def solution(mesh):
    both = P(("groups", "section"), None)
    placed = (
        both,
        P(None, ("groups", "section"), None),
        both,
        P(("groups", "section")),
        both,
        P("section", None),
        P(),
        both,
        both,
        P("section", None, None),
        P("section", None, None),
        P("section", None, None),
    )
    return jax.shard_map(
        shards,
        mesh=mesh,
        in_specs=placed,
        out_specs=(both, both),
        check_vma=False,
    )
```

time: 217 us -> 128 us (0.59)
  local copies, waits for them, and re-layouts: 50.3 us -> 2.43 us
  blocking collectives: 13.3 us -> 52 us
  waiting for transfers between devices: 64.7 us -> 30.7 us
  Pallas kernels: 0 us -> 33.4 us
  matrix products: 28.2 us -> 0 us
  starting transfers between devices: 31 us -> 7.73 us
  between operations: 14.4 us -> 0.68 us
  other arithmetic: 13.4 us -> 0.18 us
    all_to_all x1 -> x3, blocking collectives: 13.3 us -> 52 us  [the longest x1 24.2 us: shards(): asked = a2a(sent)]
    all_to_all x6 -> x2, waiting for transfers between devices: 64 us -> 29 us  [the longest x1 14.8 us: shards(): back = a2a(parts)]
    pallas_call x0 -> x6, Pallas kernels: none -> 33.4 us  [the longest x1 18.3 us: shards(): call(functools.partial(attend_kernel, n, slots, g, hg), sds((n, span + ST...]
    dot_general x8 -> x0, matrix products: 28.2 us -> none  [the longest x1 8.15 us: shards(): jnp.dot(attention, lax.all_gather(out_weight, 'section', axis=0, tiled=Tr...]
    all_to_all x6 -> x2, starting transfers between devices: 30.9 us -> 7.41 us  [the longest x1 4.22 us: shards(): a2a(partial, axis_index_groups=[[s * g + i for s in range(cnt)] for i in...]
    another operation x2 -> x0, local copies, waits for them, and re-layouts: 13.9 us -> none  [the longest x1 7 us: shards(): picked_blocks[0].reshape(-1, BLOCK_TOKENS, KEY_VALUE_HEADS, HEAD_WIDTH)]
    gather x5 -> x0, local copies, waits for them, and re-layouts: 13.5 us -> none  [the longest x1 7.12 us: shards(): picked_blocks = jnp.take(cache_block_table, safe_block, axis=1)]
    reshape x9 -> x1, local copies, waits for them, and re-layouts: 11.4 us -> 0.69 us  [shards(): slot = jnp.sum((flat[:, None] == flat[None, :]) & (order[:, None] > order...]
  transfers between devices with their start and end apart: 7 -> 3, of which waited for: 3 -> 3; matrix products, arithmetic and copies ran while one was open for 32% -> 1% of each run, Pallas kernels for 0% -> 0%
where the time goes in v1:
time: 128 us; the launch traced here: 127 us
  blocking collectives  52 us (41%)
  Pallas kernels  33.4 us (26%)
  waiting for transfers between devices  30.7 us (24%)
  starting transfers between devices  7.73 us (6%)
  local copies, waits for them, and re-layouts  2.43 us (2%)
    all_to_all x1, blocking collectives, shards(): asked = a2a(sent)  24.2 us
    pallas_call x1, Pallas kernels, shards(): call(functools.partial(attend_kernel, n, slots, g, hg), sds((n, span + ST...  18.3 us
    all_to_all x1, waiting for transfers between devices, shards(): back = a2a(parts)  14.8 us
    all_to_all x1, waiting for transfers between devices, shards(): a2a(partial, axis_index_groups=[[s * g + i for s in range(cnt)] for i in...  14.2 us
    all_to_all x1, blocking collectives, shards(): returned = a2a(done)  13.9 us
    all_to_all x1, blocking collectives, shards(): arrived = a2a(routed)  13.9 us
    pallas_call x1, Pallas kernels, run_expert(): call(expert_kernel, sds((n, CAP, tiles, LANES), BF), [VM, hbm, hbm, hbm],...  6.21 us
    all_to_all x1, starting transfers between devices, shards(): a2a(partial, axis_index_groups=[[s * g + i for s in range(cnt)] for i in...  4.22 us
  transfers between devices with their start and end apart: 3, of which 3 were waited for; matrix products, arithmetic and copies ran while one was open for 1% of the time, Pallas kernels for 0%

profile of v1, /device:TPU:0, one launch (start us, length us, event | category | flops | bytes accessed | tf_op | source)
XLA Modules:
  0.0 127.1 jit_solution(14725631534990883964)
XLA Ops:
  0.6 2.0 %pack.1 = bf16[32,72,128]{2,1,0:T(8,128)(2,1)} custom-call(s32[8,8]{1,0:T(8,128)} %ids.1, bf16[8,4096]{1,0:T(8,128)(2,1)} %q.1), custom_call_target="tpu_custom_call" | custom-call | bytes 589824 | tf_op jit(solution)/shard_map/pack/pallas_call | solution.py:325
  2.6 0.0 copy-start.2
  2.6 24.2 %all_to_all.25.x = bf16[32,72,128]{2,1,0:T(8,128)(2,1)} all-to-all(bf16[32,72,128]{2,1,0:T(8,128)(2,1)} %pack.1), channel_id=1, replica_groups=mesh['groups'=1,'section'=32] {'section'}, dimensions={0} | all-to-all | bytes 1179648 | tf_op jit(solution)/shard_map/all_to_all | solution.py:331
  26.9 18.3 %attend.1 = bf16[32,72,128]{2,1,0:T(8,128)(2,1)} custom-call(s32[16]{0:T(128)} %lens.1, bf16[32,72,128]{2,1,0:T(8,128)(2,1)} %all_to_all.25.x, bf16[2,1024,512]{2,1,0:T(8,128)(2,1)} %kv.1), custom_call_target="tpu_custom_call" | custom-call | flops 1073741824 | bytes 4194304 | tf_op jit(solution)/shard_map/attend/pallas_call | solution.py:332
  45.1 0.0 copy-start.4
  45.2 3.2 %all-to-all-start.1 = ((bf16[32,72,128]{2,1,0:T(8,128)(2,1)}), bf16[32,72,128]{2,1,0:T(8,128)(2,1)S(1)}, u32[]{:S(2)}, u32[]{:S(2)}) async-start(bf16[32,72,128]{2,1,0:T(8,128)(2,1)} %attend.1), calls=%async_computation.1 | async-start | bytes 1179648 | tf_op jit(solution)/shard_map/all_to_all | solution.py:346
  48.4 0.0 copy-done.2
  48.4 0.3 collective-permute-start
  48.7 1.7 %collective-permute-done.wo2 = bf16[128,2048]{1,0:T(8,128)(2,1)S(1)} collective-permute-done((bf16[128,2048]{1,0:T(8,128)(2,1)S(1)}, bf16[128,2048]{1,0:T(8,128)(2,1)S(1)}, u32[]{:S(2)}, u32[]{:S(2)}) %collective-permute-start) | collective-permute-done | bytes 524320 | tf_op jit(solution)/shard_map/ppermute | solution.py:317
  50.3 0.0 copy-start.3
  50.3 14.8 %all-to-all-done.1.x = bf16[32,72,128]{2,1,0:T(8,128)(2,1)S(1)} async-done(((bf16[32,72,128]{2,1,0:T(8,128)(2,1)}), bf16[32,72,128]{2,1,0:T(8,128)(2,1)S(1)}, u32[]{:S(2)}, u32[]{:S(2)}) %all-to-all-start.1) | async-done | bytes 589856 | tf_op jit(solution)/shard_map/all_to_all | solution.py:346
  65.2 0.0 copy-done.3
  65.2 0.0 copy-start
  65.2 0.8 copy-done
  66.0 3.1 %project.1 = bf16[16,8,2048]{2,1,0:T(8,128)(2,1)} custom-call(bf16[32,72,128]{2,1,0:T(8,128)(2,1)} %copy-done, bf16[128,2048]{1,0:T(8,128)(2,1)} %wo.1, bf16[128,2048]{1,0:T(8,128)(2,1)} %copy-done.3), custom_call_target="tpu_custom_call" | custom-call | flops 134217728 | bytes 2097152 | tf_op jit(solution)/shard_map/project/pallas_call | solution.py:348
  69.1 4.2 %all-to-all-start.2 = ((bf16[16,8,2048]{2,1,0:T(8,128)(2,1)}), bf16[16,8,2048]{2,1,0:T(8,128)(2,1)S(1)}, u32[]{:S(2)}, u32[]{:S(2)}) async-start(bf16[16,8,2048]{2,1,0:T(8,128)(2,1)} %project.1), calls=%async_computation.2 | async-start | bytes 1048576 | tf_op jit(solution)/shard_map/all_to_all | solution.py:358
  73.3 0.0 copy-done.4
  73.3 0.1 eq.15
  73.4 0.2 convert_reduce_fusion
  73.6 0.7 reshape.12.slot
  74.3 14.2 %all-to-all-done.2.x = bf16[16,8,2048]{2,1,0:T(8,128)(2,1)S(1)} async-done(((bf16[16,8,2048]{2,1,0:T(8,128)(2,1)}), bf16[16,8,2048]{2,1,0:T(8,128)(2,1)S(1)}, u32[]{:S(2)}, u32[]{:S(2)}) %all-to-all-start.2) | async-done | bytes 524320 | tf_op jit(solution)/shard_map/all_to_all | solution.py:358
  88.5 0.0 copy-start.1
  88.5 0.8 copy-done.1
  89.3 2.0 %norm.1 = (bf16[8,2048]{1,0:T(8,128)(2,1)}, bf16[32,2,16,128]{3,2,1,0:T(8,128)(2,1)}) custom-call(s32[8,8]{1,0:T(8,128)} %eid.3, s32[8,8]{1,0:T(8,128)} %reshape.12.slot, bf16[16,8,2048]{2,1,0:T(8,128)(2,1)} %copy-done.1, bf16[8,2048]{1,0:T(8,128)(2,1)} %res.3, f32[1,2048]{1,0:T(1,128)} %bitcast.7), custom_call_target="tpu_custom_call" | custom-call | bytes 1048576 | tf_op jit(solution)/shard_map/norm/pallas_call | solution.py:360
  91.3 13.9 %all_to_all.26.x = bf16[32,2,16,128]{3,2,1,0:T(8,128)(2,1)} all-to-all(bf16[32,2,16,128]{3,2,1,0:T(8,128)(2,1)} %get-tuple-element.5), channel_id=1, replica_groups=mesh['groups'=1,'section'=32] {'section'}, dimensions={0} | all-to-all | bytes 524288 | tf_op jit(solution)/shard_map/all_to_all | solution.py:366
  105.2 6.2 %experts.1 = bf16[32,2,16,128]{3,2,1,0:T(8,128)(2,1)} custom-call(bf16[32,2,16,128]{3,2,1,0:T(8,128)(2,1)} %all_to_all.26.x, bf16[2048,768]{1,0:T(8,128)(2,1)} %bitcast.4, bf16[2048,768]{1,0:T(8,128)(2,1)} %bitcast.5, bf16[768,2048]{1,0:T(8,128)(2,1)} %bitcast.6), custom_call_target="tpu_custom_call" | custom-call | flops 603979776 | bytes 9437184 | tf_op jit(solution)/shard_map/experts/pallas_call | solution.py:372
  111.4 13.9 %all_to_all.27.x = bf16[32,2,16,128]{3,2,1,0:T(8,128)(2,1)} all-to-all(bf16[32,2,16,128]{3,2,1,0:T(8,128)(2,1)} %experts.1), channel_id=1, replica_groups=mesh['groups'=1,'section'=32] {'section'}, dimensions={0} | all-to-all | bytes 524288 | tf_op jit(solution)/shard_map/all_to_all | solution.py:397
  125.3 1.8 %finish.1 = bf16[8,2048]{1,0:T(8,128)(2,1)} custom-call(s32[8,8]{1,0:T(8,128)} %eid.3, s32[8,8]{1,0:T(8,128)} %reshape.12.slot, f32[8,8]{1,0:T(8,128)} %rw.1, bf16[32,2,16,128]{3,2,1,0:T(8,128)(2,1)} %all_to_all.27.x, bf16[8,2048]{1,0:T(8,128)(2,1)} %res.3, bf16[8,2048]{1,0:T(8,128)(2,1)} %get-tuple-element.2.proj), custom_call_target="tpu_custom_call" | custom-call | bytes 524288 | tf_op jit(solution)/shard_map/finish/pallas_call | solution.py:398
Async XLA Ops:
  2.6 45.7 %copy-start.2 = (bf16[128,2048]{1,0:T(8,128)(2,1)S(1)}, bf16[128,2048]{1,0:T(8,128)(2,1)}, u32[]{:S(2)}) copy-start(bf16[128,2048]{1,0:T(8,128)(2,1)} %wo.1) | copy-start | bytes 1572868
  45.1 28.2 %copy-start.4 = (s32[8,8]{1,0:T(8,128)S(1)}, s32[8,8]{1,0:T(8,128)}, u32[]{:S(2)}) copy-start(s32[8,8]{1,0:T(8,128)} %eid.3) | copy-start | bytes 772
  45.2 20.0 %all-to-all-start.1 = ((bf16[32,72,128]{2,1,0:T(8,128)(2,1)}), bf16[32,72,128]{2,1,0:T(8,128)(2,1)S(1)}, u32[]{:S(2)}, u32[]{:S(2)}) async-start(bf16[32,72,128]{2,1,0:T(8,128)(2,1)} %attend.1), calls=%async_computation.1 | async-start | bytes 1179648 | tf_op jit(solution)/shard_map/all_to_all | solution.py:346
  48.4 2.0 %collective-permute-start = (bf16[128,2048]{1,0:T(8,128)(2,1)S(1)}, bf16[128,2048]{1,0:T(8,128)(2,1)S(1)}, u32[]{:S(2)}, u32[]{:S(2)}) collective-permute-start(bf16[128,2048]{1,0:T(8,128)(2,1)S(1)} %copy-done.2), channel_id=1, source_target_pairs={{0,1},{1,0},{2,3},{3,2},{4,5},{5,4},{6,7},{7,6},{8,9},{9,8},{10,11... | collective-permute-start | bytes 1572872 | tf_op jit(solution)/shard_map/ppermute | solution.py:317
  50.3 14.8 %copy-start.3 = (bf16[128,2048]{1,0:T(8,128)(2,1)}, bf16[128,2048]{1,0:T(8,128)(2,1)S(1)}, u32[]{:S(2)}) copy-start(bf16[128,2048]{1,0:T(8,128)(2,1)S(1)} %collective-permute-done.wo2) | copy-start | bytes 1572868
  65.2 0.8 copy-start
  69.1 19.4 %all-to-all-start.2 = ((bf16[16,8,2048]{2,1,0:T(8,128)(2,1)}), bf16[16,8,2048]{2,1,0:T(8,128)(2,1)S(1)}, u32[]{:S(2)}, u32[]{:S(2)}) async-start(bf16[16,8,2048]{2,1,0:T(8,128)(2,1)} %project.1), calls=%async_computation.2 | async-start | bytes 1048576 | tf_op jit(solution)/shard_map/all_to_all | solution.py:358
  88.5 0.8 copy-start.1

commit v2 on v1

v2 whole, which is shorter than its diff:
```python
import functools

import jax
import jax.numpy as jnp
from jax import lax
from jax.experimental import pallas as pl
from jax.experimental.pallas import tpu as pltpu
from jax.sharding import PartitionSpec as P


HEADS = 32
KV_HEADS = 4
WIDTH = 128
CAP = 2
BLOCK_TOKENS = 64
LANES = 128
GROUP = 4
STATS = 8
BATCH = 16
NEG = -1e30
COST = 1 << 26
GATE_PARTS = 3
DOWN_PARTS = 4
BF = jnp.bfloat16
F32 = jnp.float32

VM = pl.BlockSpec(memory_space=pltpu.VMEM)
SM = pl.BlockSpec(memory_space=pltpu.SMEM)
HB = pl.BlockSpec(memory_space=pltpu.HBM)
ANY = pl.BlockSpec(memory_space=pl.ANY)


def call(kernel, out_shape, in_specs, scratch, flops=0, nbytes=0, room=8):
    return pl.pallas_call(
        kernel,
        out_shape=out_shape,
        in_specs=in_specs,
        out_specs=jax.tree.map(lambda _: VM, out_shape),
        scratch_shapes=scratch,
        compiler_params=pltpu.CompilerParams(vmem_limit_bytes=room << 20),
        cost_estimate=pl.CostEstimate(flops=flops, bytes_accessed=nbytes, transcendentals=0),
    )


def stage_kernel(count, *refs):
    sem = refs[-1]
    outs = refs[-1 - count:-1]
    copies = [pltpu.make_async_copy(refs[i], outs[i], sem.at[i]) for i in range(count)]
    for c in copies:
        c.start()
    for c in copies:
        c.wait()


def stage(*arrays, after=()):
    count = len(arrays)
    nbytes = sum(a.size * a.dtype.itemsize for a in arrays)
    return call(
        functools.partial(stage_kernel, count),
        tuple(jax.ShapeDtypeStruct(a.shape, a.dtype) for a in arrays),
        [ANY] * (count + len(after)), [pltpu.SemaphoreType.DMA((count,))],
        nbytes=nbytes,
    )(*arrays, *after)


def gather_kernel(*refs):
    sem = refs[-1]
    out = refs[-2]
    parts = refs[:-2]
    fw = parts[0].shape[0]
    me = lax.rem(lax.axis_index("section"), len(parts))
    copies = []
    for i, part in enumerate(parts):
        at = pl.multiple_of(lax.bitwise_xor(me, i) * fw, fw)
        copies.append(pltpu.make_async_copy(part, out.at[pl.ds(at, fw)], sem.at[i]))
    for c in copies:
        c.start()
    for c in copies:
        c.wait()


def pack_kernel(run, slots, blocks, ids_in, q_in, out, ids, q, qs, meta, sem):
    rows = q.shape[0]
    picks = ids.shape[1]
    get_ids = pltpu.make_async_copy(ids_in, ids, sem.at[0])
    get_q = pltpu.make_async_copy(q_in, q, sem.at[1])
    get_ids.start()
    get_q.start()
    get_q.wait()
    for h in range(HEADS):
        qs[pl.ds(h, rows, stride=HEADS), :] = q[:, h * WIDTH:(h + 1) * WIDTH].astype(F32)
    meta[...] = jnp.zeros_like(meta)
    get_ids.wait()
    if rows * picks != out.shape[0] * slots:
        out[...] = jnp.zeros_like(out)
    lane = lax.broadcasted_iota(jnp.int32, (1, LANES), 1)
    for r in range(rows):
        tile = qs[r * HEADS:(r + 1) * HEADS, :].astype(BF)
        slot = r // run
        for j in range(picks):
            b = ids[r, j]
            dev = lax.div(b, blocks)
            local = b - dev * blocks
            out[dev, slot * HEADS:(slot + 1) * HEADS, :] = tile
            meta[dev, slot:slot + 1, :] = jnp.where(
                lane == 0, local + 1, jnp.where(lane == 1, r % run, 0)
            ).astype(F32)
    out[:, slots * HEADS:, :] = meta[...].astype(BF)


def attend_kernel(n, slots, g, hg, lens_in, x, kv, out, lens, mv, ms, of, mx, sg, sem):
    get_lens = pltpu.make_async_copy(lens_in, lens, sem.at[1])
    get_lens.start()
    pairs = n * slots
    per = pairs // g
    cnt = n // g
    ngrp = n // g
    qrows = slots * HEADS
    gw = HEADS // KV_HEADS
    span = hg * per

    mv[...] = x[:, qrows:qrows + 8, :].astype(F32).reshape(n * 8, LANES).astype(jnp.int32)
    table = pltpu.make_async_copy(mv, ms, sem.at[0])
    table.start()
    sg[...] = jnp.zeros_like(sg)
    table.wait()
    get_lens.wait()
    lane = lax.broadcasted_iota(jnp.int32, (HEADS, LANES), 1)
    column = lax.broadcasted_iota(jnp.int32, (HEADS, KV_HEADS * BLOCK_TOKENS), 1)
    owner = lax.div(lax.broadcasted_iota(jnp.int32, column.shape, 0), gw)
    tok = jnp.where(lax.div(column, BLOCK_TOKENS) == owner, lax.rem(column, BLOCK_TOKENS), BLOCK_TOKENS)

    def some(step, carry):
        todo = []
        for d in range(BATCH):
            dev = step * BATCH + d
            for q in range(slots):
                blk = ms[dev * 8 + q, 0] - 1
                safe = jnp.maximum(blk, 0)
                length = jnp.where(blk >= 0, lens[safe], 0)
                base = pl.multiple_of(safe * BLOCK_TOKENS, BLOCK_TOKENS)
                pos = lax.rem(dev, g) * per + q * cnt + lax.div(dev, g)
                todo.append((dev, q, length, base, pos, ms[dev * 8 + q, 1]))
        scores = []
        for dev, q, length, base, pos, rr in todo:
            kb = kv[0, pl.ds(base, BLOCK_TOKENS), :]
            kc = jnp.concatenate([kb[:, k * WIDTH:(k + 1) * WIDTH] for k in range(KV_HEADS)], axis=0)
            scores.append(lax.dot_general(
                x[dev, q * HEADS:(q + 1) * HEADS, :], kc,
                (((1,), (1,)), ((), ())), preferred_element_type=F32))
        soft = []
        for s, (dev, q, length, base, pos, rr) in zip(scores, todo):
            s = jnp.where(tok < length, s * (WIDTH ** -0.5), NEG)
            m = jnp.max(s, axis=-1, keepdims=True)
            w = jnp.where(tok < length, jnp.exp(s - m), 0.0).astype(BF)
            l = jnp.sum(w.astype(F32), axis=-1, keepdims=True)
            soft.append((m, w, l))
        for (m, w, l), (dev, q, length, base, pos, rr) in zip(soft, todo):
            vb = kv[1, pl.ds(base, BLOCK_TOKENS), :]
            vc = jnp.concatenate([vb[:, k * WIDTH:(k + 1) * WIDTH] for k in range(KV_HEADS)], axis=0)
            of[pl.ds(pl.multiple_of(pos * HEADS, HEADS), HEADS), :] = jnp.dot(
                w, vc, preferred_element_type=F32)
        top, tot, who = carry
        for (m, w, l), (dev, q, length, base, pos, rr) in zip(soft, todo):
            here = lane == pos
            top = jnp.where(here, m, top)
            tot = jnp.where(here, l, tot)
            who = jnp.where(here, rr.astype(F32), who)
        return top, tot, who

    zero = jnp.zeros((HEADS, LANES), F32)
    top, tot, who = lax.fori_loop(0, n // BATCH, some, (zero, zero, zero))

    def heads(h, _):
        grp = lax.div(h, hg)
        at = pl.multiple_of(lax.rem(h, hg) * per, per)
        for i in range(g):
            rows = of[pl.ds(i * per * HEADS + h, per, stride=HEADS), :].astype(BF)
            out[grp * g + i, pl.ds(at, per), :] = rows
        return 0

    lax.fori_loop(0, HEADS, heads, 0, unroll=4)

    hi = top.astype(BF).astype(F32)
    mid = (top - hi).astype(BF).astype(F32)
    big = tot.astype(BF).astype(F32)
    copies = LANES // span
    for t, v in enumerate((hi, mid, top - hi - mid, big, tot - big, who)):
        mx[...] = v
        for i in range(g):
            row = jnp.concatenate(
                [mx[pl.ds(hh, ngrp, stride=hg), :][:, i * per:(i + 1) * per] for hh in range(hg)] * copies, axis=1)
            sg[pl.ds(i * STATS + t, ngrp, stride=g * STATS), :] = row
    out[:, span:, :] = sg[...].reshape(n, STATS, LANES).astype(BF)


def attend(n, slots, g, hg, block_len, asked, key_value_cache):
    pairs = n * slots
    span = hg * (pairs // g)
    sds = jax.ShapeDtypeStruct
    return call(
        functools.partial(attend_kernel, n, slots, g, hg),
        sds((n, span + STATS, LANES), BF), [HB, VM, VM],
        [
            pltpu.SMEM(block_len.shape, jnp.int32),
            pltpu.VMEM((n * 8, LANES), jnp.int32),
            pltpu.SMEM((n * 8, LANES), jnp.int32),
            pltpu.VMEM((pairs * HEADS, LANES), F32),
            pltpu.VMEM((HEADS, LANES), F32),
            pltpu.VMEM((n * STATS, LANES), F32),
            pltpu.SemaphoreType.DMA((2,)),
        ],
        flops=4 * HEADS * pairs * BLOCK_TOKENS * WIDTH, nbytes=COST,
    )(block_len, asked, key_value_cache)


def project_kernel(n, slots, g, hg, run, rows, x, ws, out, sf, cm):
    pairs = n * slots
    per = pairs // g
    span = hg * per
    cnt = n // g
    sf[...] = x[:, span:, :].astype(F32).reshape(n * STATS, LANES)
    m = (sf[pl.ds(0, n, stride=STATS), :] + sf[pl.ds(1, n, stride=STATS), :]
         + sf[pl.ds(2, n, stride=STATS), :])
    l = sf[pl.ds(3, n, stride=STATS), :] + sf[pl.ds(4, n, stride=STATS), :]
    rid = sf[pl.ds(5, n, stride=STATS), :]
    peak = jnp.zeros_like(m)
    for r in range(run):
        mine = rid == r
        top = jnp.max(jnp.where(mine, m, -3e38), axis=0, keepdims=True)
        peak = jnp.where(mine, top, peak)
    f = jnp.exp(m - peak)
    fl = f * l
    den = jnp.ones_like(m)
    for r in range(run):
        mine = rid == r
        tot = jnp.sum(jnp.where(mine, fl, 0.0), axis=0, keepdims=True)
        den = jnp.where(mine, tot, den)
    c = f / den
    lane = lax.broadcasted_iota(jnp.int32, (n, LANES), 1)
    inner = lax.rem(lane, span)
    hh = lax.div(inner, per)
    pl_ = lax.rem(inner, per)
    q = lax.div(pl_, cnt)
    s = lax.rem(pl_, cnt)
    local = rows * cnt
    target = hh * local + s * rows + q * run + rid.astype(jnp.int32)
    dpt = LANES // span
    total = hg * local
    row = lax.broadcasted_iota(jnp.int32, (total, LANES), 0)
    side = lax.div(lax.broadcasted_iota(jnp.int32, (1, LANES), 1), span)
    for t in range(n // dpt):
        blk_c = c[t * dpt:t * dpt + 1, :]
        blk_t = target[t * dpt:t * dpt + 1, :]
        for u in range(1, dpt):
            d = t * dpt + u
            blk_c = jnp.where(side == u, c[d:d + 1, :], blk_c)
            blk_t = jnp.where(side == u, target[d:d + 1, :], blk_t)
        cm[:, t * LANES:(t + 1) * LANES] = jnp.where(row == blk_t, blk_c, 0.0).astype(BF)
    a = x[:, 0:span, :].reshape(n * span, LANES)
    att = jnp.dot(cm[...], a, preferred_element_type=F32).astype(BF)
    att = jnp.concatenate([att[i * local:(i + 1) * local, :] for i in range(hg)], axis=1)
    for col in range(0, ws.shape[1], 512):
        p = jnp.dot(att, ws[:, col:col + 512], preferred_element_type=F32)
        out[:, :, col:col + 512] = p.reshape(cnt, rows, 512).astype(BF)


def norm_kernel(eid, slot, x, res, gain, proj, out, nf):
    rows, width = res.shape
    acc = x[0].astype(F32)
    for i in range(1, x.shape[0]):
        acc = acc + x[i].astype(F32)
    p = acc.astype(BF)
    proj[...] = p
    stream = res[...].astype(F32) + p.astype(F32)
    ms = jnp.mean(stream * stream, axis=-1, keepdims=True)
    nrm = stream * lax.rsqrt(ms + 1e-06) * gain[...]
    tiles = width // LANES
    for c in range(tiles):
        nf[pl.ds(c, rows, stride=tiles), :] = nrm[:, c * LANES:(c + 1) * LANES]
    if rows * eid.shape[1] != out.shape[0] * CAP:
        out[...] = jnp.zeros_like(out)
    for r in range(rows):
        tile = nf[r * tiles:(r + 1) * tiles, :].astype(BF)
        for k in range(eid.shape[1]):
            out[eid[r, k], slot[r, k]] = tile


def expert_kernel(x, wu, wg, wd, out, xf, xb, of, gb, db, sg, sd):
    n, cap, tiles, _ = x.shape
    m = n * cap
    width, ffe = wu.shape
    gc = ffe // GATE_PARTS
    dc = width // DOWN_PARTS
    gate = [pltpu.make_async_copy(
        wg.at[:, pl.ds(i * gc, gc)], gb.at[:, pl.ds(i * gc, gc)], sg.at[i]) for i in range(GATE_PARTS)]
    down = [pltpu.make_async_copy(
        wd.at[:, pl.ds(i * dc, dc)], db.at[:, pl.ds(i * dc, dc)], sd.at[i]) for i in range(DOWN_PARTS)]
    for c in gate + down:
        c.start()
    xf[...] = x[...].astype(F32).reshape(m * tiles, LANES)
    for c in range(tiles):
        xb[:, c * LANES:(c + 1) * LANES] = xf[pl.ds(c, m, stride=tiles), :].astype(BF)
    ua = jnp.dot(xb[...], wu[...], preferred_element_type=F32)
    parts = []
    for i, c in enumerate(gate):
        c.wait()
        ga = jnp.dot(xb[...], gb[:, i * gc:(i + 1) * gc], preferred_element_type=F32)
        parts.append((ga / (1.0 + jnp.exp(-ga)) * ua[:, i * gc:(i + 1) * gc]).astype(BF))
    h = jnp.concatenate(parts, axis=1)
    for i, c in enumerate(down):
        c.wait()
        o = jnp.dot(h, db[:, i * dc:(i + 1) * dc], preferred_element_type=F32)
        for t in range(dc // LANES):
            of[pl.ds(i * dc // LANES + t, m, stride=tiles), :] = o[:, t * LANES:(t + 1) * LANES]
    out[...] = of[...].astype(BF).reshape(n, cap, tiles, LANES)


def finish_kernel(eid, slot, rw, x, res, proj, out, acc):
    rows, width = res.shape
    tiles = width // LANES
    for r in range(rows):
        a = jnp.zeros((tiles, LANES), F32)
        for k in range(eid.shape[1]):
            a = a + rw[r, k] * x[eid[r, k], slot[r, k]].astype(F32)
        acc[r * tiles:(r + 1) * tiles, :] = a
    for c in range(tiles):
        sl = slice(c * LANES, (c + 1) * LANES)
        stream = res[:, sl].astype(F32) + proj[:, sl].astype(F32)
        out[:, sl] = (stream + acc[pl.ds(c, rows, stride=tiles), :]).astype(BF)


def shards(
    queries,
    key_value_cache,
    block_ids,
    block_len,
    residual_in,
    out_weight,
    norm_gain,
    expert_ids,
    route_weight,
    w_gate,
    w_up,
    w_down,
):
    n = lax.axis_size("section")
    rows, _ = queries.shape
    picks = block_ids.shape[1]
    blocks = block_len.shape[0]
    width = residual_in.shape[1]
    run = n // picks
    slots = (rows + run - 1) // run
    g = GROUP
    fw = out_weight.shape[0]
    hg = g * fw // WIDTH
    pairs = n * slots
    per = pairs // g
    span = hg * per
    cnt = n // g
    tiles = width // LANES
    a2a = functools.partial(
        lax.all_to_all, axis_name="section", split_axis=0, concat_axis=0, tiled=True)
    sds = jax.ShapeDtypeStruct

    pieces = [out_weight]
    step = g // 2
    while step:
        pieces = pieces + [
            lax.ppermute(p, "section", [(i, i ^ step) for i in range(n)]) for p in pieces]
        step //= 2
    order = [0]
    step = g // 2
    while step:
        order = order + [o ^ step for o in order]
        step //= 2
    pieces = [pieces[order.index(i)] for i in range(g)]
    wide_weight = call(
        gather_kernel, sds((g * fw, width), BF), [ANY] * g,
        [pltpu.SemaphoreType.DMA((g,))], nbytes=g * fw * width * 4,
    )(*pieces)
    (cache,) = stage(key_value_cache)
    flat = expert_ids.reshape(-1)
    place = jnp.arange(flat.shape[0])
    slot = jnp.sum(
        (flat[:, None] == flat[None, :]) & (place[:, None] > place[None, :]), axis=1
    ).astype(jnp.int32).reshape(expert_ids.shape)

    chunk = slots * HEADS + 8
    sent = call(
        functools.partial(pack_kernel, run, slots, blocks),
        sds((n, chunk, LANES), BF), [HB, HB],
        [
            pltpu.SMEM(block_ids.shape, jnp.int32),
            pltpu.VMEM(queries.shape, BF),
            pltpu.VMEM((rows * HEADS, LANES), F32),
            pltpu.VMEM((n, 8, LANES), F32),
            pltpu.SemaphoreType.DMA((2,)),
        ],
        nbytes=COST, room=60,
    )(block_ids, queries)
    asked = a2a(sent)
    parts = attend(n, slots, g, hg, block_len, asked, cache)
    back = a2a(parts)
    local = rows * cnt
    partial = call(
        functools.partial(project_kernel, n, slots, g, hg, run, rows),
        sds((cnt, rows, width), BF), [VM, VM],
        [
            pltpu.VMEM((n * STATS, LANES), F32),
            pltpu.VMEM((hg * local, n * span), BF),
        ],
        flops=2 * local * g * fw * width, nbytes=COST,
    )(back, wide_weight)
    summed = a2a(partial, axis_index_groups=[[s * g + i for s in range(cnt)] for i in range(g)])
    experts = n * w_gate.shape[0]
    attn_proj, routed = call(
        norm_kernel,
        (sds((rows, width), BF), sds((experts, CAP, tiles, LANES), BF)), [SM, SM, VM, VM, VM],
        [pltpu.VMEM((rows * tiles, LANES), F32)],
        nbytes=COST,
    )(expert_ids, slot, summed, residual_in, norm_gain.reshape(1, width))
    arrived = a2a(routed)
    (up_w,) = stage(w_up, after=(attn_proj,))
    ffe = w_gate.shape[2]
    slots_in = n * CAP

    def run_expert(xin, wu, wg, wd):
        return call(
            expert_kernel,
            sds((n, CAP, tiles, LANES), BF), [VM, VM, ANY, ANY],
            [
                pltpu.VMEM((slots_in * tiles, LANES), F32),
                pltpu.VMEM((slots_in, width), BF),
                pltpu.VMEM((slots_in * tiles, LANES), F32),
                pltpu.VMEM((width, ffe), BF),
                pltpu.VMEM((ffe, width), BF),
                pltpu.SemaphoreType.DMA((GATE_PARTS,)),
                pltpu.SemaphoreType.DMA((DOWN_PARTS,)),
            ],
            room=49, flops=6 * slots_in * width * ffe, nbytes=6 * width * ffe,
        )(xin, wu, wg, wd)

    per_device = w_gate.shape[0]
    if per_device == 1:
        done = run_expert(arrived, up_w[0], w_gate[0], w_down[0])
    else:
        split = arrived.reshape(n, per_device, CAP, tiles, LANES)
        done = jnp.stack(
            [run_expert(split[:, e], up_w[e], w_gate[e], w_down[e]) for e in range(per_device)], axis=1
        ).reshape(arrived.shape)
    returned = a2a(done)
    layer_out = call(
        finish_kernel,
        sds((rows, width), BF), [SM, SM, SM, VM, VM, VM],
        [pltpu.VMEM((rows * tiles, LANES), F32)],
        nbytes=1 << 19,
    )(expert_ids, slot, route_weight, returned, residual_in, attn_proj)
    return (attn_proj, layer_out)


def solution(mesh):
    both = P(("groups", "section"), None)
    placed = (
        both,
        P(None, ("groups", "section"), None),
        both,
        P(("groups", "section")),
        both,
        P("section", None),
        P(),
        both,
        both,
        P("section", None, None),
        P("section", None, None),
        P("section", None, None),
    )

    return jax.shard_map(
        shards,
        mesh=mesh,
        in_specs=placed,
        out_specs=(both, both),
        check_vma=False,
    )
```

time: 128 us -> 110 us (0.86)
  blocking collectives: 52 us -> 12.8 us
  waiting for transfers between devices: 30.7 us -> 52 us
  Pallas kernels: 33.4 us -> 18.2 us
  starting transfers between devices: 7.73 us -> 20.5 us
  local copies, waits for them, and re-layouts: 2.43 us -> 4.42 us
    all_to_all x2 -> x0, blocking collectives: 38.1 us -> none  [the longest x1 24.2 us: shards(): asked = a2a(sent)]
    all_to_all x0 -> x2, waiting for transfers between devices: none -> 22.7 us  [the longest x1 15 us: shards(): asked = a2a(sent)]
    ppermute x1 -> x3, waiting for transfers between devices: 1.66 us -> 20.4 us  [shards(): lax.ppermute(p, 'section', [(i, i ^ step) for i in range(n)])]
    all_to_all x1, waiting for transfers between devices: 14.8 us -> 0.01 us  [shards(): back = a2a(parts)]
    pallas_call x2 -> x5, Pallas kernels: 24.5 us -> 11.5 us  [the longest x1 7.13 us: attend(): call(functools.partial(attend_kernel, n, slots, g, hg), sds((n, span + ST...]
    all_to_all x0 -> x2, starting transfers between devices: none -> 10 us  [the longest x1 7.33 us: shards(): asked = a2a(sent)]
    all_to_all x1, waiting for transfers between devices: 14.2 us -> 8.88 us  [shards(): a2a(partial, axis_index_groups=[[s * g + i for s in range(cnt)] for i in...]
    unnamed x10 -> x20, local copies, waits for them, and re-layouts: 1.66 us -> 4.27 us
  transfers between devices with their start and end apart: 3 -> 7, of which waited for: 3 -> 5; matrix products, arithmetic and copies ran while one was open for 1% -> 0% of each run, Pallas kernels for 0% -> 1%
where the time goes in v2:
time: 110 us; the launch traced here: 109 us
  waiting for transfers between devices  52 us (47%)
  starting transfers between devices  20.5 us (19%)
  Pallas kernels  18.2 us (17%)
  blocking collectives  12.8 us (12%)
  local copies, waits for them, and re-layouts  4.42 us (4%)
    ppermute x3, waiting for transfers between devices, shards(): lax.ppermute(p, 'section', [(i, i ^ step) for i in range(n)])  20.4 us
    all_to_all x1, waiting for transfers between devices, shards(): asked = a2a(sent)  15 us
    all_to_all x1, blocking collectives, shards(): returned = a2a(done)  12.8 us
    all_to_all x1, waiting for transfers between devices, shards(): a2a(partial, axis_index_groups=[[s * g + i for s in range(cnt)] for i in...  8.88 us
    all_to_all x1, waiting for transfers between devices, shards(): arrived = a2a(routed)  7.69 us
    all_to_all x1, starting transfers between devices, shards(): asked = a2a(sent)  7.33 us
    pallas_call x1, Pallas kernels, attend(): call(functools.partial(attend_kernel, n, slots, g, hg), sds((n, span + ST...  7.13 us
    all_to_all x1, starting transfers between devices, shards(): a2a(partial, axis_index_groups=[[s * g + i for s in range(cnt)] for i in...  5.49 us
  transfers between devices with their start and end apart: 7, of which 5 were waited for; matrix products, arithmetic and copies ran while one was open for 0% of the time, Pallas kernels for 1%

profile of v2, /device:TPU:0, one launch (start us, length us, event | category | flops | bytes accessed | tf_op | source)
XLA Modules:
  0.0 109.0 jit_solution(461888359394146653)
XLA Ops:
  0.6 0.0 copy-start.9
  0.6 2.0 %shard_map.131 = bf16[32,72,128]{2,1,0:T(8,128)(2,1)} custom-call(s32[8,8]{1,0:T(8,128)} %ids_in.1, bf16[8,4096]{1,0:T(8,128)(2,1)} %q_in.1), custom_call_target="tpu_custom_call" | custom-call | bytes 67108864 | tf_op jit(solution)/shard_map/pallas_call | solution.py:390
  2.7 7.3 %all-to-all-start = ((bf16[32,72,128]{2,1,0:T(8,128)(2,1)}), bf16[32,72,128]{2,1,0:T(8,128)(2,1)S(1)}, u32[]{:S(2)}, u32[]{:S(2)}) async-start(bf16[32,72,128]{2,1,0:T(8,128)(2,1)} %shard_map.131), calls=%async_computation | async-start | bytes 1179648 | tf_op jit(solution)/shard_map/all_to_all | solution.py:402
  10.0 0.0 copy-start.1
  10.0 1.6 %copy-done.1 = bf16[2,1024,512]{2,1,0:T(8,128)(2,1)S(1)} copy-done((bf16[2,1024,512]{2,1,0:T(8,128)(2,1)S(1)}, bf16[2,1024,512]{2,1,0:T(8,128)(2,1)}, u32[]{:S(2)}) %copy-start.1) | copy-done | bytes 2097176
  11.6 0.1 shard_map.132.kv
  11.8 0.0 copy-start.2
  11.8 15.0 %all-to-all-done.x = bf16[32,72,128]{2,1,0:T(8,128)(2,1)S(1)} async-done(((bf16[32,72,128]{2,1,0:T(8,128)(2,1)}), bf16[32,72,128]{2,1,0:T(8,128)(2,1)S(1)}, u32[]{:S(2)}, u32[]{:S(2)}) %all-to-all-start) | async-done | bytes 589856 | tf_op jit(solution)/shard_map/all_to_all | solution.py:402
  26.8 0.0 copy-done.9
  26.8 7.1 %shard_map.133 = bf16[32,72,128]{2,1,0:T(8,128)(2,1)} custom-call(s32[16]{0:T(128)S(1)} %copy-done.9, bf16[32,72,128]{2,1,0:T(8,128)(2,1)S(1)} %all-to-all-done.x, bf16[2,1024,512]{2,1,0:T(8,128)(2,1)S(1)} %shard_map.132.kv), custom_call_target="tpu_custom_call" | custom-call | flops 67108864 | bytes 67108864 | tf_op jit(solution)/shard_map/pallas_call | solution.py:201
  33.9 3.2 %all-to-all-start.1 = ((bf16[32,72,128]{2,1,0:T(8,128)(2,1)}), bf16[32,72,128]{2,1,0:T(8,128)(2,1)S(1)}, u32[]{:S(2)}, u32[]{:S(2)}) async-start(bf16[32,72,128]{2,1,0:T(8,128)(2,1)} %shard_map.133), calls=%async_computation.1 | async-start | bytes 1179648 | tf_op jit(solution)/shard_map/all_to_all | solution.py:404
  37.2 0.0 copy-done.2
  37.2 0.0 copy-start.6
  37.2 0.0 copy-start.5
  37.2 0.0 copy-start.7
  37.2 1.8 %collective-permute-start.1 = (bf16[128,2048]{1,0:T(8,128)(2,1)S(1)}, bf16[128,2048]{1,0:T(8,128)(2,1)S(1)}, u32[]{:S(2)}, u32[]{:S(2)}) collective-permute-start(bf16[128,2048]{1,0:T(8,128)(2,1)S(1)} %copy-done.2), channel_id=1, source_target_pairs={{0,2},{1,3},{2,0},{3,1},{4,6},{5,7},{6,4},{7,5},{8,10},{9,11},{10,... | collective-permute-start | bytes 1572872 | tf_op jit(solution)/shard_map/ppermute | solution.py:370
  39.0 0.0 collective-permute-start
  39.0 18.5 %collective-permute-done.1.refs_2_ = bf16[128,2048]{1,0:T(8,128)(2,1)S(1)} collective-permute-done((bf16[128,2048]{1,0:T(8,128)(2,1)S(1)}, bf16[128,2048]{1,0:T(8,128)(2,1)S(1)}, u32[]{:S(2)}, u32[]{:S(2)}) %collective-permute-start.1) | collective-permute-done | bytes 524320 | tf_op jit(solution)/shard_map/ppermute | solution.py:370
  57.5 0.0 collective-permute-start.2
  57.5 0.0 collective-permute-done.refs_1_
  57.5 1.9 %collective-permute-done.2.refs_3_ = bf16[128,2048]{1,0:T(8,128)(2,1)S(1)} collective-permute-done((bf16[128,2048]{1,0:T(8,128)(2,1)S(1)}, bf16[128,2048]{1,0:T(8,128)(2,1)S(1)}, u32[]{:S(2)}, u32[]{:S(2)}) %collective-permute-start.2) | collective-permute-done | bytes 524320 | tf_op jit(solution)/shard_map/ppermute | solution.py:370
  59.5 0.2 shard_map.134.ws
  59.6 0.0 all-to-all-done.1.x
  59.7 1.7 %shard_map.135 = bf16[8,8,2048]{2,1,0:T(8,128)(2,1)} custom-call(bf16[32,72,128]{2,1,0:T(8,128)(2,1)S(1)} %all-to-all-done.1.x, bf16[512,2048]{1,0:T(8,128)(2,1)S(1)} %shard_map.134.ws), custom_call_target="tpu_custom_call" | custom-call | flops 134217728 | bytes 67108864 | tf_op jit(solution)/shard_map/pallas_call | solution.py:406
  61.3 5.5 %all-to-all-start.2 = ((bf16[8,8,2048]{2,1,0:T(8,128)(2,1)}), bf16[8,8,2048]{2,1,0:T(8,128)(2,1)S(1)}, u32[]{:S(2)}, u32[]{:S(2)}) async-start(bf16[8,8,2048]{2,1,0:T(8,128)(2,1)} %shard_map.135), calls=%async_computation.2 | async-start | bytes 524288 | tf_op jit(solution)/shard_map/all_to_all | solution.py:415
  66.8 0.0 copy-done.6
  66.8 0.1 eq.15
  66.9 0.2 convert_reduce_fusion
  67.1 0.1 reshape.12.slot
  67.2 8.9 %all-to-all-done.2.x = bf16[8,8,2048]{2,1,0:T(8,128)(2,1)S(1)} async-done(((bf16[8,8,2048]{2,1,0:T(8,128)(2,1)}), bf16[8,8,2048]{2,1,0:T(8,128)(2,1)S(1)}, u32[]{:S(2)}, u32[]{:S(2)}) %all-to-all-start.2) | async-done | bytes 262176 | tf_op jit(solution)/shard_map/all_to_all | solution.py:415
  76.0 0.0 copy-done.5
  76.1 0.0 copy-done.7
  76.1 1.6 %shard_map.136 = (bf16[8,2048]{1,0:T(8,128)(2,1)}, bf16[32,2,16,128]{3,2,1,0:T(8,128)(2,1)}) custom-call(s32[8,8]{1,0:T(8,128)S(1)} %copy-done.6, s32[8,8]{1,0:T(8,128)S(1)} %reshape.12.slot, bf16[8,8,2048]{2,1,0:T(8,128)(2,1)S(1)} %all-to-all-done.2.x, bf16[8,2048]{1,0:T(8,128)(2,1)S(1)} %copy-done.5, f32[1,2048]{1,0:T(1,128)S(1)} %bitcast.5), custom_call_target="tpu_custom_call" | custom-call | bytes 67108864 | tf_op jit(solution)/shard_map/pallas_call | solution.py:417
  77.6 2.7 %all-to-all-start.3 = ((bf16[32,2,16,128]{3,2,1,0:T(8,128)(2,1)}), bf16[32,2,16,128]{3,2,1,0:T(8,128)(2,1)S(1)}, u32[]{:S(2)}, u32[]{:S(2)}) async-start(bf16[32,2,16,128]{3,2,1,0:T(8,128)(2,1)} %get-tuple-element.5), calls=%async_computation.3 | async-start | bytes 524288 | tf_op jit(solution)/shard_map/all_to_all | solution.py:423
  80.3 0.0 copy-start
  80.3 1.9 %copy-done = bf16[1,2048,768]{2,1,0:T(8,128)(2,1)S(1)} copy-done((bf16[1,2048,768]{2,1,0:T(8,128)(2,1)S(1)}, bf16[1,2048,768]{2,1,0:T(8,128)(2,1)}, u32[]{:S(2)}) %copy-start) | copy-done | bytes 3145752
  82.2 0.0 copy-start.3
  82.2 0.8 copy-done.3
  83.0 0.2 shard_map.137
  83.2 7.7 %all-to-all-done.3.x = bf16[32,2,16,128]{3,2,1,0:T(8,128)(2,1)S(1)} async-done(((bf16[32,2,16,128]{3,2,1,0:T(8,128)(2,1)}), bf16[32,2,16,128]{3,2,1,0:T(8,128)(2,1)S(1)}, u32[]{:S(2)}, u32[]{:S(2)}) %all-to-all-start.3) | async-done | bytes 262176 | tf_op jit(solution)/shard_map/all_to_all | solution.py:423
  90.9 0.0 copy-start.4
  90.9 0.0 copy-start.8
  90.9 3.8 %shard_map.138 = bf16[32,2,16,128]{3,2,1,0:T(8,128)(2,1)S(1)} custom-call(bf16[32,2,16,128]{3,2,1,0:T(8,128)(2,1)S(1)} %all-to-all-done.3.x, bf16[2048,768]{1,0:T(8,128)(2,1)S(1)} %bitcast.4, bf16[2048,768]{1,0:T(8,128)(2,1)} %bitcast.6, bf16[768,2048]{1,0:T(8,128)(2,1)} %bitcast.7), custom_call_target="tpu_custom_call" | custom-call | flops 603979776 | bytes 9437184 | tf_op jit(solution)/shard_map/pallas_call | solution.py:429
  94.7 12.8 %all_to_all.25.x = bf16[32,2,16,128]{3,2,1,0:T(8,128)(2,1)S(1)} all-to-all(bf16[32,2,16,128]{3,2,1,0:T(8,128)(2,1)S(1)} %shard_map.138), channel_id=1, replica_groups=mesh['groups'=1,'section'=32] {'section'}, dimensions={0} | all-to-all | bytes 524288 | tf_op jit(solution)/shard_map/all_to_all | solution.py:452
  107.5 0.0 copy-done.4
  107.5 0.0 copy-done.8
  107.5 1.5 %shard_map.139 = bf16[8,2048]{1,0:T(8,128)(2,1)} custom-call(s32[8,8]{1,0:T(8,128)S(1)} %copy-done.6, s32[8,8]{1,0:T(8,128)S(1)} %reshape.12.slot, f32[8,8]{1,0:T(8,128)S(1)} %copy-done.8, bf16[32,2,16,128]{3,2,1,0:T(8,128)(2,1)S(1)} %all_to_all.25.x, bf16[8,2048]{1,0:T(8,128)(2,1)S(1)} %copy-done.5, bf16[8,2048]{1,0:T(8,128)(2,1)S(1)} %copy-done.4), custom_call_target="tpu_custom_call" | custom-call | bytes 524288 | tf_op jit(solution)/shard_map/pallas_call | solution.py:453
Async XLA Ops:
  0.6 26.2 %copy-start.9 = (s32[16]{0:T(128)S(1)}, s32[16]{0:T(128)}, u32[]{:S(2)}) copy-start(s32[16]{0:T(128)} %lens_in.1) | copy-start | bytes 196
  2.7 24.1 %all-to-all-start = ((bf16[32,72,128]{2,1,0:T(8,128)(2,1)}), bf16[32,72,128]{2,1,0:T(8,128)(2,1)S(1)}, u32[]{:S(2)}, u32[]{:S(2)}) async-start(bf16[32,72,128]{2,1,0:T(8,128)(2,1)} %shard_map.131), calls=%async_computation | async-start | bytes 1179648 | tf_op jit(solution)/shard_map/all_to_all | solution.py:402
  10.0 1.6 %copy-start.1 = (bf16[2,1024,512]{2,1,0:T(8,128)(2,1)S(1)}, bf16[2,1024,512]{2,1,0:T(8,128)(2,1)}, u32[]{:S(2)}) copy-start(bf16[2,1024,512]{2,1,0:T(8,128)(2,1)} %refs_0_.3) | copy-start | bytes 6291460
  11.8 25.4 %copy-start.2 = (bf16[128,2048]{1,0:T(8,128)(2,1)S(1)}, bf16[128,2048]{1,0:T(8,128)(2,1)}, u32[]{:S(2)}) copy-start(bf16[128,2048]{1,0:T(8,128)(2,1)} %refs_0_.4) | copy-start | bytes 1572868
  33.9 25.7 %all-to-all-start.1 = ((bf16[32,72,128]{2,1,0:T(8,128)(2,1)}), bf16[32,72,128]{2,1,0:T(8,128)(2,1)S(1)}, u32[]{:S(2)}, u32[]{:S(2)}) async-start(bf16[32,72,128]{2,1,0:T(8,128)(2,1)} %shard_map.133), calls=%async_computation.1 | async-start | bytes 1179648 | tf_op jit(solution)/shard_map/all_to_all | solution.py:404
  37.2 29.7 %copy-start.6 = (s32[8,8]{1,0:T(8,128)S(1)}, s32[8,8]{1,0:T(8,128)}, u32[]{:S(2)}) copy-start(s32[8,8]{1,0:T(8,128)} %eid.3) | copy-start | bytes 772
  37.2 38.9 %copy-start.5 = (bf16[8,2048]{1,0:T(8,128)(2,1)S(1)}, bf16[8,2048]{1,0:T(8,128)(2,1)}, u32[]{:S(2)}) copy-start(bf16[8,2048]{1,0:T(8,128)(2,1)} %res.3) | copy-start | bytes 98308
  37.2 38.9 %copy-start.7 = (f32[2048]{0:T(1024)S(1)}, f32[2048]{0:T(1024)}, u32[]{:S(2)}) copy-start(f32[2048]{0:T(1024)} %param.18) | copy-start | bytes 24580
  37.2 20.3 %collective-permute-start.1 = (bf16[128,2048]{1,0:T(8,128)(2,1)S(1)}, bf16[128,2048]{1,0:T(8,128)(2,1)S(1)}, u32[]{:S(2)}, u32[]{:S(2)}) collective-permute-start(bf16[128,2048]{1,0:T(8,128)(2,1)S(1)} %copy-done.2), channel_id=1, source_target_pairs={{0,2},{1,3},{2,0},{3,1},{4,6},{5,7},{6,4},{7,5},{8,10},{9,11},{10,... | collective-permute-start | bytes 1572872 | tf_op jit(solution)/shard_map/ppermute | solution.py:370
  39.0 18.5 %collective-permute-start = (bf16[128,2048]{1,0:T(8,128)(2,1)S(1)}, bf16[128,2048]{1,0:T(8,128)(2,1)S(1)}, u32[]{:S(2)}, u32[]{:S(2)}) collective-permute-start(bf16[128,2048]{1,0:T(8,128)(2,1)S(1)} %copy-done.2), channel_id=1, source_target_pairs={{0,1},{1,0},{2,3},{3,2},{4,5},{5,4},{6,7},{7,6},{8,9},{9,8},{10,11... | collective-permute-start | bytes 1572872 | tf_op jit(solution)/shard_map/ppermute | solution.py:370
  57.5 1.9 %collective-permute-start.2 = (bf16[128,2048]{1,0:T(8,128)(2,1)S(1)}, bf16[128,2048]{1,0:T(8,128)(2,1)S(1)}, u32[]{:S(2)}, u32[]{:S(2)}) collective-permute-start(bf16[128,2048]{1,0:T(8,128)(2,1)S(1)} %collective-permute-done.1.refs_2_), channel_id=1, source_target_pairs={{0,1},{1,0},{2,3},{3,2},{4,5},{5,4},{6,7},{7,6},{8,9},{9,8},{10,11... | collective-permute-start | bytes 1572872 | tf_op jit(solution)/shard_map/ppermute | solution.py:370
  61.3 14.7 %all-to-all-start.2 = ((bf16[8,8,2048]{2,1,0:T(8,128)(2,1)}), bf16[8,8,2048]{2,1,0:T(8,128)(2,1)S(1)}, u32[]{:S(2)}, u32[]{:S(2)}) async-start(bf16[8,8,2048]{2,1,0:T(8,128)(2,1)} %shard_map.135), calls=%async_computation.2 | async-start | bytes 524288 | tf_op jit(solution)/shard_map/all_to_all | solution.py:415
  77.6 13.3 %all-to-all-start.3 = ((bf16[32,2,16,128]{3,2,1,0:T(8,128)(2,1)}), bf16[32,2,16,128]{3,2,1,0:T(8,128)(2,1)S(1)}, u32[]{:S(2)}, u32[]{:S(2)}) async-start(bf16[32,2,16,128]{3,2,1,0:T(8,128)(2,1)} %get-tuple-element.5), calls=%async_computation.3 | async-start | bytes 524288 | tf_op jit(solution)/shard_map/all_to_all | solution.py:423
  80.3 1.9 %copy-start = (bf16[1,2048,768]{2,1,0:T(8,128)(2,1)S(1)}, bf16[1,2048,768]{2,1,0:T(8,128)(2,1)}, u32[]{:S(2)}) copy-start(bf16[1,2048,768]{2,1,0:T(8,128)(2,1)} %refs_0_.5) | copy-start | bytes 9437188
  82.2 0.8 copy-start.3
  90.9 16.6 %copy-start.4 = (bf16[8,2048]{1,0:T(8,128)(2,1)S(1)}, bf16[8,2048]{1,0:T(8,128)(2,1)}, u32[]{:S(2)}) copy-start(bf16[8,2048]{1,0:T(8,128)(2,1)} %get-tuple-element.2.refs_1_.proj) | copy-start | bytes 98308
  90.9 16.6 %copy-start.8 = (f32[8,8]{1,0:T(8,128)S(1)}, f32[8,8]{1,0:T(8,128)}, u32[]{:S(2)}) copy-start(f32[8,8]{1,0:T(8,128)} %rw.1) | copy-start | bytes 772

commit v3 on v2

--- a/solution.py
+++ b/solution.py
@@ -14,11 +14,12 @@
 CAP = 2
 BLOCK_TOKENS = 64
 LANES = 128
-GROUP = 4
+GROUP = 8
 STATS = 8
 BATCH = 16
 NEG = -1e30
 COST = 1 << 26
+PROJECT_ROOM = 16
 GATE_PARTS = 3
 DOWN_PARTS = 4
 BF = jnp.bfloat16
@@ -30,12 +31,12 @@
 ANY = pl.BlockSpec(memory_space=pl.ANY)
 
 
-def call(kernel, out_shape, in_specs, scratch, flops=0, nbytes=0, room=8):
+def call(kernel, out_shape, in_specs, scratch, flops=0, nbytes=0, room=8, out=None):
     return pl.pallas_call(
         kernel,
         out_shape=out_shape,
         in_specs=in_specs,
-        out_specs=jax.tree.map(lambda _: VM, out_shape),
+        out_specs=out if out is not None else jax.tree.map(lambda _: VM, out_shape),
         scratch_shapes=scratch,
         compiler_params=pltpu.CompilerParams(vmem_limit_bytes=room << 20),
         cost_estimate=pl.CostEstimate(flops=flops, bytes_accessed=nbytes, transcendentals=0),
@@ -61,22 +62,6 @@
         [ANY] * (count + len(after)), [pltpu.SemaphoreType.DMA((count,))],
         nbytes=nbytes,
     )(*arrays, *after)
-
-
-def gather_kernel(*refs):
-    sem = refs[-1]
-    out = refs[-2]
-    parts = refs[:-2]
-    fw = parts[0].shape[0]
-    me = lax.rem(lax.axis_index("section"), len(parts))
-    copies = []
-    for i, part in enumerate(parts):
-        at = pl.multiple_of(lax.bitwise_xor(me, i) * fw, fw)
-        copies.append(pltpu.make_async_copy(part, out.at[pl.ds(at, fw)], sem.at[i]))
-    for c in copies:
-        c.start()
-    for c in copies:
-        c.wait()
 
 
 def pack_kernel(run, slots, blocks, ids_in, q_in, out, ids, q, qs, meta, sem):
@@ -108,7 +93,7 @@
     out[:, slots * HEADS:, :] = meta[...].astype(BF)
 
 
-def attend_kernel(n, slots, g, hg, lens_in, x, kv, out, lens, mv, ms, of, mx, sg, sem):
+def attend_kernel(n, slots, g, hg, lens_in, x, kv, out, lens, mv, ms, of, mx, sg, ob, sem, so):
     get_lens = pltpu.make_async_copy(lens_in, lens, sem.at[1])
     get_lens.start()
     pairs = n * slots
@@ -119,12 +104,15 @@
     gw = HEADS // KV_HEADS
     span = hg * per
 
-    mv[...] = x[:, qrows:qrows + 8, :].astype(F32).reshape(n * 8, LANES).astype(jnp.int32)
+    sg[...] = x[:, qrows:qrows + 8, :].astype(F32).reshape(n * 8, LANES)
+    for q in range(slots):
+        mv[q * 8:(q + 1) * 8, 0:n] = jnp.transpose(
+            sg[pl.ds(q, n, stride=8), :])[0:8, :].astype(jnp.int32)
     table = pltpu.make_async_copy(mv, ms, sem.at[0])
     table.start()
-    sg[...] = jnp.zeros_like(sg)
     table.wait()
     get_lens.wait()
+    sg[...] = jnp.zeros_like(sg)
     lane = lax.broadcasted_iota(jnp.int32, (HEADS, LANES), 1)
     column = lax.broadcasted_iota(jnp.int32, (HEADS, KV_HEADS * BLOCK_TOKENS), 1)
     owner = lax.div(lax.broadcasted_iota(jnp.int32, column.shape, 0), gw)
@@ -135,12 +123,12 @@
         for d in range(BATCH):
             dev = step * BATCH + d
             for q in range(slots):
-                blk = ms[dev * 8 + q, 0] - 1
+                blk = ms[q * 8, dev] - 1
                 safe = jnp.maximum(blk, 0)
                 length = jnp.where(blk >= 0, lens[safe], 0)
                 base = pl.multiple_of(safe * BLOCK_TOKENS, BLOCK_TOKENS)
                 pos = lax.rem(dev, g) * per + q * cnt + lax.div(dev, g)
-                todo.append((dev, q, length, base, pos, ms[dev * 8 + q, 1]))
+                todo.append((dev, q, length, base, pos, ms[q * 8 + 1, dev]))
         scores = []
         for dev, q, length, base, pos, rr in todo:
             kb = kv[0, pl.ds(base, BLOCK_TOKENS), :]
@@ -158,29 +146,20 @@
         for (m, w, l), (dev, q, length, base, pos, rr) in zip(soft, todo):
             vb = kv[1, pl.ds(base, BLOCK_TOKENS), :]
             vc = jnp.concatenate([vb[:, k * WIDTH:(k + 1) * WIDTH] for k in range(KV_HEADS)], axis=0)
-            of[pl.ds(pl.multiple_of(pos * HEADS, HEADS), HEADS), :] = jnp.dot(
+            of[pl.ds(pos, HEADS, stride=pairs), :] = jnp.dot(
                 w, vc, preferred_element_type=F32)
         top, tot, who = carry
         for (m, w, l), (dev, q, length, base, pos, rr) in zip(soft, todo):
             here = lane == pos
             top = jnp.where(here, m, top)
             tot = jnp.where(here, l, tot)
-            who = jnp.where(here, rr.astype(F32), who)
+            who = jnp.where(here[0:1], rr.astype(F32), who)
         return top, tot, who
 
     zero = jnp.zeros((HEADS, LANES), F32)
-    top, tot, who = lax.fori_loop(0, n // BATCH, some, (zero, zero, zero))
-
-    def heads(h, _):
-        grp = lax.div(h, hg)
-        at = pl.multiple_of(lax.rem(h, hg) * per, per)
-        for i in range(g):
-            rows = of[pl.ds(i * per * HEADS + h, per, stride=HEADS), :].astype(BF)
-            out[grp * g + i, pl.ds(at, per), :] = rows
-        return 0
-
-    lax.fori_loop(0, HEADS, heads, 0, unroll=4)
-
+    top, tot, who = lax.fori_loop(0, n // BATCH, some, (zero, zero, zero[0:1]))
+
+    who = jnp.broadcast_to(who, top.shape)
     hi = top.astype(BF).astype(F32)
     mid = (top - hi).astype(BF).astype(F32)
     big = tot.astype(BF).astype(F32)
@@ -191,7 +170,19 @@
             row = jnp.concatenate(
                 [mx[pl.ds(hh, ngrp, stride=hg), :][:, i * per:(i + 1) * per] for hh in range(hg)] * copies, axis=1)
             sg[pl.ds(i * STATS + t, ngrp, stride=g * STATS), :] = row
-    out[:, span:, :] = sg[...].reshape(n, STATS, LANES).astype(BF)
+    ob[:, span:, :] = sg[...].reshape(n, STATS, LANES).astype(BF)
+    sends = []
+    for grp in range(ngrp):
+        for hh in range(hg):
+            h = grp * hg + hh
+            for i in range(g):
+                at = h * pairs + i * per
+                ob[grp * g + i, hh * per:(hh + 1) * per, :] = of[at:at + per, :].astype(BF)
+        sends.append(pltpu.make_async_copy(
+            ob.at[pl.ds(grp * g, g)], out.at[pl.ds(grp * g, g)], so.at[grp]))
+        sends[-1].start()
+    for c in sends:
+        c.wait()
 
 
 def attend(n, slots, g, hg, block_len, asked, key_value_cache):
@@ -203,18 +194,31 @@
         sds((n, span + STATS, LANES), BF), [HB, VM, VM],
         [
             pltpu.SMEM(block_len.shape, jnp.int32),
-            pltpu.VMEM((n * 8, LANES), jnp.int32),
-            pltpu.SMEM((n * 8, LANES), jnp.int32),
+            pltpu.VMEM((slots * 8, LANES), jnp.int32),
+            pltpu.SMEM((slots * 8, LANES), jnp.int32),
             pltpu.VMEM((pairs * HEADS, LANES), F32),
             pltpu.VMEM((HEADS, LANES), F32),
             pltpu.VMEM((n * STATS, LANES), F32),
+            pltpu.VMEM((n, span + STATS, LANES), BF),
             pltpu.SemaphoreType.DMA((2,)),
+            pltpu.SemaphoreType.DMA((n // g,)),
         ],
-        flops=4 * HEADS * pairs * BLOCK_TOKENS * WIDTH, nbytes=COST,
+        out=ANY, flops=4 * HEADS * pairs * BLOCK_TOKENS * WIDTH, nbytes=COST,
     )(block_len, asked, key_value_cache)
 
 
-def project_kernel(n, slots, g, hg, run, rows, x, ws, out, sf, cm):
+def project_kernel(n, slots, g, hg, run, rows, x, *refs):
+    pieces = refs[:g]
+    outs = refs[g:g + n // g]
+    sf, cm, ws, sp, sem = refs[g + n // g:]
+    fw = pieces[0].shape[0]
+    me = lax.rem(lax.axis_index("section"), g)
+    mine_group = lax.div(lax.axis_index("section"), g)
+    loads = []
+    for i, piece in enumerate(pieces):
+        at = pl.multiple_of(lax.bitwise_xor(me, i) * fw, fw)
+        loads.append(pltpu.make_async_copy(piece, ws.at[pl.ds(at, fw)], sem.at[i]))
+        loads[-1].start()
     pairs = n * slots
     per = pairs // g
     span = hg * per
@@ -260,16 +264,23 @@
     a = x[:, 0:span, :].reshape(n * span, LANES)
     att = jnp.dot(cm[...], a, preferred_element_type=F32).astype(BF)
     att = jnp.concatenate([att[i * local:(i + 1) * local, :] for i in range(hg)], axis=1)
+    for c in loads:
+        c.wait()
     for col in range(0, ws.shape[1], 512):
         p = jnp.dot(att, ws[:, col:col + 512], preferred_element_type=F32)
-        out[:, :, col:col + 512] = p.reshape(cnt, rows, 512).astype(BF)
-
-
-def norm_kernel(eid, slot, x, res, gain, proj, out, nf):
+        for s_ in range(cnt):
+            sp[s_, :, col:col + 512] = p[s_ * rows:(s_ + 1) * rows]
+    for j, out in enumerate(outs):
+        out[...] = sp[lax.bitwise_xor(mine_group, j)].astype(BF)
+
+
+def norm_kernel(count, eid, slot, *refs):
+    x = refs[:count]
+    res, gain, proj, out, nf = refs[count:]
     rows, width = res.shape
-    acc = x[0].astype(F32)
-    for i in range(1, x.shape[0]):
-        acc = acc + x[i].astype(F32)
+    acc = x[0][...].astype(F32)
+    for i in range(1, count):
+        acc = acc + x[i][...].astype(F32)
     p = acc.astype(BF)
     proj[...] = p
     stream = res[...].astype(F32) + p.astype(F32)
@@ -363,22 +374,14 @@
         lax.all_to_all, axis_name="section", split_axis=0, concat_axis=0, tiled=True)
     sds = jax.ShapeDtypeStruct
 
-    pieces = [out_weight]
-    step = g // 2
-    while step:
-        pieces = pieces + [
-            lax.ppermute(p, "section", [(i, i ^ step) for i in range(n)]) for p in pieces]
-        step //= 2
-    order = [0]
-    step = g // 2
-    while step:
-        order = order + [o ^ step for o in order]
-        step //= 2
-    pieces = [pieces[order.index(i)] for i in range(g)]
-    wide_weight = call(
-        gather_kernel, sds((g * fw, width), BF), [ANY] * g,
-        [pltpu.SemaphoreType.DMA((g,))], nbytes=g * fw * width * 4,
-    )(*pieces)
+    pieces = [None] * g
+    for far in range(0, g, 2):
+        if far:
+            pieces[far] = lax.ppermute(out_weight, "section", [(i, i ^ far) for i in range(n)])
+        else:
+            pieces[0] = out_weight
+    for far in range(0, g, 2):
+        pieces[far + 1] = lax.ppermute(pieces[far], "section", [(i, i ^ 1) for i in range(n)])
     (cache,) = stage(key_value_cache)
     flat = expert_ids.reshape(-1)
     place = jnp.arange(flat.shape[0])
@@ -405,21 +408,26 @@
     local = rows * cnt
     partial = call(
         functools.partial(project_kernel, n, slots, g, hg, run, rows),
-        sds((cnt, rows, width), BF), [VM, VM],
+        (sds((rows, width), BF),) * cnt, [VM] + [ANY] * g,
         [
             pltpu.VMEM((n * STATS, LANES), F32),
             pltpu.VMEM((hg * local, n * span), BF),
+            pltpu.VMEM((g * fw, width), BF),
+            pltpu.VMEM((cnt, rows, width), F32),
+            pltpu.SemaphoreType.DMA((g,)),
         ],
-        flops=2 * local * g * fw * width, nbytes=COST,
-    )(back, wide_weight)
-    summed = a2a(partial, axis_index_groups=[[s * g + i for s in range(cnt)] for i in range(g)])
+        flops=2 * local * g * fw * width, nbytes=COST, room=PROJECT_ROOM,
+    )(back, *pieces)
+    summed = [partial[0]]
+    for j in range(1, cnt):
+        summed.append(lax.ppermute(partial[j], "section", [(i, i ^ (j * g)) for i in range(n)]))
     experts = n * w_gate.shape[0]
     attn_proj, routed = call(
-        norm_kernel,
-        (sds((rows, width), BF), sds((experts, CAP, tiles, LANES), BF)), [SM, SM, VM, VM, VM],
+        functools.partial(norm_kernel, cnt),
+        (sds((rows, width), BF), sds((experts, CAP, tiles, LANES), BF)), [SM, SM] + [VM] * (cnt + 2),
         [pltpu.VMEM((rows * tiles, LANES), F32)],
         nbytes=COST,
-    )(expert_ids, slot, summed, residual_in, norm_gain.reshape(1, width))
+    )(expert_ids, slot, *summed, residual_in, norm_gain.reshape(1, width))
     arrived = a2a(routed)
     (up_w,) = stage(w_up, after=(attn_proj,))
     ffe = w_gate.shape[2]

time: 110 us -> 116 us (1.055)
  waiting for transfers between devices: 52 us -> 58 us
    ppermute x3 -> x10, waiting for transfers between devices: 20.4 us -> 35.3 us  [the longest x3 28.4 us: shards(): lax.ppermute(out_weight, 'section', [(i, i ^ far) for i in range(n)])]
    all_to_all x1 -> x0, waiting for transfers between devices: 8.88 us -> none  [shards(): a2a(partial, axis_index_groups=[[s * g + i for s in range(cnt)] for i in...]
    ppermute x3 -> x10, starting transfers between devices: 1.84 us -> 8.52 us  [the longest x3 4.45 us: shards(): lax.ppermute(partial[j], 'section', [(i, i ^ j * g) for i in range(n)])]
    all_to_all x1 -> x0, starting transfers between devices: 5.49 us -> none  [shards(): a2a(partial, axis_index_groups=[[s * g + i for s in range(cnt)] for i in...]
    pallas_call x1, Pallas kernels: 7.13 us -> 5.39 us  [attend(): call(functools.partial(attend_kernel, n, slots, g, hg), sds((n, span + ST...]
    pallas_call x3 -> x2, Pallas kernels: 3.45 us -> 4.12 us  [the longest x1 2.53 us: shards(): call(functools.partial(project_kernel, n, slots, g, hg, run, rows), (sds(...]
  transfers between devices with their start and end apart: 7 -> 13, of which waited for: 5 -> 7; matrix products, arithmetic and copies ran while one was open for 0% -> 0% of each run, Pallas kernels for 1% -> 0%
where the time goes in v3:
time: 116 us; the launch traced here: 115 us
  waiting for transfers between devices  58 us (50%)
  starting transfers between devices  21.6 us (19%)
  Pallas kernels  17.2 us (15%)
  blocking collectives  12.7 us (11%)
  local copies, waits for them, and re-layouts  4.42 us (4%)
    ppermute x3, waiting for transfers between devices, shards(): lax.ppermute(out_weight, 'section', [(i, i ^ far) for i in range(n)])  28.4 us
    all_to_all x1, waiting for transfers between devices, shards(): asked = a2a(sent)  15 us
    all_to_all x1, blocking collectives, shards(): returned = a2a(done)  12.7 us
    all_to_all x1, waiting for transfers between devices, shards(): arrived = a2a(routed)  7.69 us
    all_to_all x1, starting transfers between devices, shards(): asked = a2a(sent)  7.33 us
    pallas_call x1, Pallas kernels, attend(): call(functools.partial(attend_kernel, n, slots, g, hg), sds((n, span + ST...  5.39 us
    ppermute x3, waiting for transfers between devices, shards(): lax.ppermute(partial[j], 'section', [(i, i ^ j * g) for i in range(n)])  4.95 us
    ppermute x3, starting transfers between devices, shards(): lax.ppermute(partial[j], 'section', [(i, i ^ j * g) for i in range(n)])  4.45 us
  transfers between devices with their start and end apart: 13, of which 7 were waited for; matrix products, arithmetic and copies ran while one was open for 0% of the time, Pallas kernels for 0%

profile of v3, /device:TPU:0, one launch (start us, length us, event | category | flops | bytes accessed | tf_op | source)
XLA Modules:
  0.0 114.9 jit_solution(3147509469584435541)
XLA Ops:
  0.6 0.0 copy-start.9
  0.6 2.0 %shard_map.131 = bf16[32,72,128]{2,1,0:T(8,128)(2,1)} custom-call(s32[8,8]{1,0:T(8,128)} %ids_in.1, bf16[8,4096]{1,0:T(8,128)(2,1)} %q_in.1), custom_call_target="tpu_custom_call" | custom-call | bytes 67108864 | tf_op jit(solution)/shard_map/pallas_call | solution.py:393
  2.7 7.3 %all-to-all-start = ((bf16[32,72,128]{2,1,0:T(8,128)(2,1)}), bf16[32,72,128]{2,1,0:T(8,128)(2,1)S(1)}, u32[]{:S(2)}, u32[]{:S(2)}) async-start(bf16[32,72,128]{2,1,0:T(8,128)(2,1)} %shard_map.131), calls=%async_computation | async-start | bytes 1179648 | tf_op jit(solution)/shard_map/all_to_all | solution.py:405
  10.0 0.0 copy-start.1
  10.0 1.6 %copy-done.1 = bf16[2,1024,512]{2,1,0:T(8,128)(2,1)S(1)} copy-done((bf16[2,1024,512]{2,1,0:T(8,128)(2,1)S(1)}, bf16[2,1024,512]{2,1,0:T(8,128)(2,1)}, u32[]{:S(2)}) %copy-start.1) | copy-done | bytes 2097176
  11.6 0.1 shard_map.132.kv
  11.8 0.0 copy-start.2
  11.8 0.0 copy-start.6
  11.8 15.0 %all-to-all-done.x = bf16[32,72,128]{2,1,0:T(8,128)(2,1)S(1)} async-done(((bf16[32,72,128]{2,1,0:T(8,128)(2,1)}), bf16[32,72,128]{2,1,0:T(8,128)(2,1)S(1)}, u32[]{:S(2)}, u32[]{:S(2)}) %all-to-all-start) | async-done | bytes 589856 | tf_op jit(solution)/shard_map/all_to_all | solution.py:405
  26.8 0.0 copy-done.9
  26.8 5.4 %shard_map.133 = bf16[32,72,128]{2,1,0:T(8,128)(2,1)} custom-call(s32[16]{0:T(128)S(1)} %copy-done.9, bf16[32,72,128]{2,1,0:T(8,128)(2,1)S(1)} %all-to-all-done.x, bf16[2,1024,512]{2,1,0:T(8,128)(2,1)S(1)} %shard_map.132.kv), custom_call_target="tpu_custom_call" | custom-call | flops 67108864 | bytes 67108864 | tf_op jit(solution)/shard_map/pallas_call | solution.py:192
  32.2 0.0 copy-start.5
  32.2 0.0 copy-start.7
  32.2 3.2 %all-to-all-start.1 = ((bf16[32,72,128]{2,1,0:T(8,128)(2,1)}), bf16[32,72,128]{2,1,0:T(8,128)(2,1)S(1)}, u32[]{:S(2)}, u32[]{:S(2)}) async-start(bf16[32,72,128]{2,1,0:T(8,128)(2,1)} %shard_map.133), calls=%async_computation.1 | async-start | bytes 1179648 | tf_op jit(solution)/shard_map/all_to_all | solution.py:407
  35.5 0.0 copy-done.2
  35.5 1.8 %collective-permute-start.1 = (bf16[128,2048]{1,0:T(8,128)(2,1)S(1)}, bf16[128,2048]{1,0:T(8,128)(2,1)S(1)}, u32[]{:S(2)}, u32[]{:S(2)}) collective-permute-start(bf16[128,2048]{1,0:T(8,128)(2,1)S(1)} %copy-done.2), channel_id=1, source_target_pairs={{0,2},{1,3},{2,0},{3,1},{4,6},{5,7},{6,4},{7,5},{8,10},{9,11},{10,... | collective-permute-start | bytes 1572872 | tf_op jit(solution)/shard_map/ppermute | solution.py:380
  37.3 1.5 %collective-permute-start.3 = (bf16[128,2048]{1,0:T(8,128)(2,1)S(1)}, bf16[128,2048]{1,0:T(8,128)(2,1)S(1)}, u32[]{:S(2)}, u32[]{:S(2)}) collective-permute-start(bf16[128,2048]{1,0:T(8,128)(2,1)S(1)} %copy-done.2), channel_id=1, source_target_pairs={{0,4},{1,5},{2,6},{3,7},{4,0},{5,1},{6,2},{7,3},{8,12},{9,13},{10,... | collective-permute-start | bytes 1572872 | tf_op jit(solution)/shard_map/ppermute | solution.py:380
  38.8 0.3 collective-permute-start.5
  39.0 0.0 collective-permute-start
  39.0 17.4 %collective-permute-done.1.refs_2_ = bf16[128,2048]{1,0:T(8,128)(2,1)S(1)} collective-permute-done((bf16[128,2048]{1,0:T(8,128)(2,1)S(1)}, bf16[128,2048]{1,0:T(8,128)(2,1)S(1)}, u32[]{:S(2)}, u32[]{:S(2)}) %collective-permute-start.1) | collective-permute-done | bytes 524320 | tf_op jit(solution)/shard_map/ppermute | solution.py:380
  56.4 0.0 collective-permute-start.2
  56.4 0.0 collective-permute-done.3.refs_4_
  56.4 0.5 collective-permute-start.4
  56.9 11.0 %collective-permute-done.5.refs_6_ = bf16[128,2048]{1,0:T(8,128)(2,1)S(1)} collective-permute-done((bf16[128,2048]{1,0:T(8,128)(2,1)S(1)}, bf16[128,2048]{1,0:T(8,128)(2,1)S(1)}, u32[]{:S(2)}, u32[]{:S(2)}) %collective-permute-start.5) | collective-permute-done | bytes 524320 | tf_op jit(solution)/shard_map/ppermute | solution.py:380
  68.0 0.0 collective-permute-start.6
  68.0 0.0 copy-done.6
  68.0 0.1 eq.15
  68.1 0.0 collective-permute-done.refs_1_
  68.1 0.0 collective-permute-done.2.refs_3_
  68.1 0.0 collective-permute-done.4.refs_5_
  68.1 1.9 %collective-permute-done.6.refs_7_ = bf16[128,2048]{1,0:T(8,128)(2,1)} collective-permute-done((bf16[128,2048]{1,0:T(8,128)(2,1)S(1)}, bf16[128,2048]{1,0:T(8,128)(2,1)}, u32[]{:S(2)}, u32[]{:S(2)}) %collective-permute-start.6) | collective-permute-done | bytes 524320 | tf_op jit(solution)/shard_map/ppermute | solution.py:384
  70.0 0.0 all-to-all-done.1.x
  70.0 2.5 %shard_map.134 = (bf16[8,2048]{1,0:T(8,128)(2,1)S(1)}, bf16[8,2048]{1,0:T(8,128)(2,1)S(1)}, bf16[8,2048]{1,0:T(8,128)(2,1)S(1)}, bf16[8,2048]{1,0:T(8,128)(2,1)S(1)}) custom-call(bf16[32,72,128]{2,1,0:T(8,128)(2,1)S(1)} %all-to-all-done.1.x, bf16[128,2048]{1,0:T(8,128)(2,1)S(1)} %copy-done.2, bf16[128,2048]{1,0:T(8,128)(2,1)S(1)} %collective-permute-done.refs_1_, ...), custom_call_target="tpu_custom_call" | custom-call | flops 134217728 | bytes 67108864 | tf_op jit(solution)/shard_map/pallas_call | solution.py:409
  72.6 1.5 %collective-permute-start.7 = (bf16[8,2048]{1,0:T(8,128)(2,1)S(1)}, bf16[8,2048]{1,0:T(8,128)(2,1)S(1)}, u32[]{:S(2)}, u32[]{:S(2)}) collective-permute-start(bf16[8,2048]{1,0:T(8,128)(2,1)S(1)} %get-tuple-element.9), channel_id=1, source_target_pairs={{0,8},{1,9},{2,10},{3,11},{4,12},{5,13},{6,14},{7,15},{8,0},{9,1},... | collective-permute-start | bytes 98312 | tf_op jit(solution)/shard_map/ppermute | solution.py:423
  74.1 2.4 %collective-permute-start.8 = (bf16[8,2048]{1,0:T(8,128)(2,1)S(1)}, bf16[8,2048]{1,0:T(8,128)(2,1)S(1)}, u32[]{:S(2)}, u32[]{:S(2)}) collective-permute-start(bf16[8,2048]{1,0:T(8,128)(2,1)S(1)} %get-tuple-element.10), channel_id=1, source_target_pairs={{0,16},{1,17},{2,18},{3,19},{4,20},{5,21},{6,22},{7,23},{8,24},{9,... | collective-permute-start | bytes 98312 | tf_op jit(solution)/shard_map/ppermute | solution.py:423
  76.5 0.5 collective-permute-start.9
  77.0 0.2 convert_reduce_fusion
  77.2 0.1 reshape.12.slot
  77.3 0.0 collective-permute-done.7.refs_1_
  77.3 2.3 %collective-permute-done.8.refs_2_ = bf16[8,2048]{1,0:T(8,128)(2,1)S(1)} collective-permute-done((bf16[8,2048]{1,0:T(8,128)(2,1)S(1)}, bf16[8,2048]{1,0:T(8,128)(2,1)S(1)}, u32[]{:S(2)}, u32[]{:S(2)}) %collective-permute-start.8) | collective-permute-done | bytes 32800 | tf_op jit(solution)/shard_map/ppermute | solution.py:423
  79.6 2.6 %collective-permute-done.9.refs_3_ = bf16[8,2048]{1,0:T(8,128)(2,1)S(1)} collective-permute-done((bf16[8,2048]{1,0:T(8,128)(2,1)S(1)}, bf16[8,2048]{1,0:T(8,128)(2,1)S(1)}, u32[]{:S(2)}, u32[]{:S(2)}) %collective-permute-start.9) | collective-permute-done | bytes 32800 | tf_op jit(solution)/shard_map/ppermute | solution.py:423
  82.2 0.0 copy-done.5
  82.2 0.0 copy-done.7
  82.2 1.6 %shard_map.135 = (bf16[8,2048]{1,0:T(8,128)(2,1)}, bf16[32,2,16,128]{3,2,1,0:T(8,128)(2,1)}) custom-call(s32[8,8]{1,0:T(8,128)S(1)} %copy-done.6, s32[8,8]{1,0:T(8,128)S(1)} %reshape.12.slot, bf16[8,2048]{1,0:T(8,128)(2,1)S(1)} %get-tuple-element.8.refs_0_, bf16[8,2048]{1,0:T(8,128)(2,1)S(1)} %collective-permute-done.7.refs_1_, ...), custom_call_target="tpu_custom_call" | custom-call | bytes 67108864 | tf_op jit(solution)/shard_map/pallas_call | solution.py:425
  83.8 2.6 %all-to-all-start.2 = ((bf16[32,2,16,128]{3,2,1,0:T(8,128)(2,1)}), bf16[32,2,16,128]{3,2,1,0:T(8,128)(2,1)S(1)}, u32[]{:S(2)}, u32[]{:S(2)}) async-start(bf16[32,2,16,128]{3,2,1,0:T(8,128)(2,1)} %get-tuple-element.13), calls=%async_computation.2 | async-start | bytes 524288 | tf_op jit(solution)/shard_map/all_to_all | solution.py:431
  86.4 0.0 copy-start
  86.4 1.9 %copy-done = bf16[1,2048,768]{2,1,0:T(8,128)(2,1)S(1)} copy-done((bf16[1,2048,768]{2,1,0:T(8,128)(2,1)S(1)}, bf16[1,2048,768]{2,1,0:T(8,128)(2,1)}, u32[]{:S(2)}) %copy-start) | copy-done | bytes 3145752
  88.3 0.0 copy-start.3
  88.3 0.8 copy-done.3
  89.1 0.2 shard_map.136
  89.3 7.7 %all-to-all-done.2.x = bf16[32,2,16,128]{3,2,1,0:T(8,128)(2,1)S(1)} async-done(((bf16[32,2,16,128]{3,2,1,0:T(8,128)(2,1)}), bf16[32,2,16,128]{3,2,1,0:T(8,128)(2,1)S(1)}, u32[]{:S(2)}, u32[]{:S(2)}) %all-to-all-start.2) | async-done | bytes 262176 | tf_op jit(solution)/shard_map/all_to_all | solution.py:431
  97.0 0.0 copy-start.4
  97.0 0.0 copy-start.8
  97.0 3.8 %shard_map.137 = bf16[32,2,16,128]{3,2,1,0:T(8,128)(2,1)S(1)} custom-call(bf16[32,2,16,128]{3,2,1,0:T(8,128)(2,1)S(1)} %all-to-all-done.2.x, bf16[2048,768]{1,0:T(8,128)(2,1)S(1)} %bitcast.4, bf16[2048,768]{1,0:T(8,128)(2,1)} %bitcast.6, bf16[768,2048]{1,0:T(8,128)(2,1)} %bitcast.7), custom_call_target="tpu_custom_call" | custom-call | flops 603979776 | bytes 9437184 | tf_op jit(solution)/shard_map/pallas_call | solution.py:437
  100.8 12.7 %all_to_all.20.x = bf16[32,2,16,128]{3,2,1,0:T(8,128)(2,1)S(1)} all-to-all(bf16[32,2,16,128]{3,2,1,0:T(8,128)(2,1)S(1)} %shard_map.137), channel_id=1, replica_groups=mesh['groups'=1,'section'=32] {'section'}, dimensions={0} | all-to-all | bytes 524288 | tf_op jit(solution)/shard_map/all_to_all | solution.py:460
  113.4 0.0 copy-done.4
  113.4 0.0 copy-done.8
  113.4 1.5 %shard_map.138 = bf16[8,2048]{1,0:T(8,128)(2,1)} custom-call(s32[8,8]{1,0:T(8,128)S(1)} %copy-done.6, s32[8,8]{1,0:T(8,128)S(1)} %reshape.12.slot, f32[8,8]{1,0:T(8,128)S(1)} %copy-done.8, bf16[32,2,16,128]{3,2,1,0:T(8,128)(2,1)S(1)} %all_to_all.20.x, bf16[8,2048]{1,0:T(8,128)(2,1)S(1)} %copy-done.5, bf16[8,2048]{1,0:T(8,128)(2,1)S(1)} %copy-done.4), custom_call_target="tpu_custom_call" | custom-call | bytes 524288 | tf_op jit(solution)/shard_map/pallas_call | solution.py:461
Async XLA Ops:
  0.6 26.2 %copy-start.9 = (s32[16]{0:T(128)S(1)}, s32[16]{0:T(128)}, u32[]{:S(2)}) copy-start(s32[16]{0:T(128)} %lens_in.1) | copy-start | bytes 196
  2.7 24.1 %all-to-all-start = ((bf16[32,72,128]{2,1,0:T(8,128)(2,1)}), bf16[32,72,128]{2,1,0:T(8,128)(2,1)S(1)}, u32[]{:S(2)}, u32[]{:S(2)}) async-start(bf16[32,72,128]{2,1,0:T(8,128)(2,1)} %shard_map.131), calls=%async_computation | async-start | bytes 1179648 | tf_op jit(solution)/shard_map/all_to_all | solution.py:405
  10.0 1.6 %copy-start.1 = (bf16[2,1024,512]{2,1,0:T(8,128)(2,1)S(1)}, bf16[2,1024,512]{2,1,0:T(8,128)(2,1)}, u32[]{:S(2)}) copy-start(bf16[2,1024,512]{2,1,0:T(8,128)(2,1)} %refs_0_.3) | copy-start | bytes 6291460
  11.8 23.7 %copy-start.2 = (bf16[128,2048]{1,0:T(8,128)(2,1)S(1)}, bf16[128,2048]{1,0:T(8,128)(2,1)}, u32[]{:S(2)}) copy-start(bf16[128,2048]{1,0:T(8,128)(2,1)} %refs_0_.4) | copy-start | bytes 1572868
  11.8 56.2 %copy-start.6 = (s32[8,8]{1,0:T(8,128)S(1)}, s32[8,8]{1,0:T(8,128)}, u32[]{:S(2)}) copy-start(s32[8,8]{1,0:T(8,128)} %eid.3) | copy-start | bytes 772
  32.2 50.0 %copy-start.5 = (bf16[8,2048]{1,0:T(8,128)(2,1)S(1)}, bf16[8,2048]{1,0:T(8,128)(2,1)}, u32[]{:S(2)}) copy-start(bf16[8,2048]{1,0:T(8,128)(2,1)} %res.1) | copy-start | bytes 98308
  32.2 50.0 %copy-start.7 = (f32[2048]{0:T(1024)S(1)}, f32[2048]{0:T(1024)}, u32[]{:S(2)}) copy-start(f32[2048]{0:T(1024)} %param.18) | copy-start | bytes 24580
  32.2 37.8 %all-to-all-start.1 = ((bf16[32,72,128]{2,1,0:T(8,128)(2,1)}), bf16[32,72,128]{2,1,0:T(8,128)(2,1)S(1)}, u32[]{:S(2)}, u32[]{:S(2)}) async-start(bf16[32,72,128]{2,1,0:T(8,128)(2,1)} %shard_map.133), calls=%async_computation.1 | async-start | bytes 1179648 | tf_op jit(solution)/shard_map/all_to_all | solution.py:407
  35.5 20.9 %collective-permute-start.1 = (bf16[128,2048]{1,0:T(8,128)(2,1)S(1)}, bf16[128,2048]{1,0:T(8,128)(2,1)S(1)}, u32[]{:S(2)}, u32[]{:S(2)}) collective-permute-start(bf16[128,2048]{1,0:T(8,128)(2,1)S(1)} %copy-done.2), channel_id=1, source_target_pairs={{0,2},{1,3},{2,0},{3,1},{4,6},{5,7},{6,4},{7,5},{8,10},{9,11},{10,... | collective-permute-start | bytes 1572872 | tf_op jit(solution)/shard_map/ppermute | solution.py:380
  37.3 19.1 %collective-permute-start.3 = (bf16[128,2048]{1,0:T(8,128)(2,1)S(1)}, bf16[128,2048]{1,0:T(8,128)(2,1)S(1)}, u32[]{:S(2)}, u32[]{:S(2)}) collective-permute-start(bf16[128,2048]{1,0:T(8,128)(2,1)S(1)} %copy-done.2), channel_id=1, source_target_pairs={{0,4},{1,5},{2,6},{3,7},{4,0},{5,1},{6,2},{7,3},{8,12},{9,13},{10,... | collective-permute-start | bytes 1572872 | tf_op jit(solution)/shard_map/ppermute | solution.py:380
  38.8 29.2 %collective-permute-start.5 = (bf16[128,2048]{1,0:T(8,128)(2,1)S(1)}, bf16[128,2048]{1,0:T(8,128)(2,1)S(1)}, u32[]{:S(2)}, u32[]{:S(2)}) collective-permute-start(bf16[128,2048]{1,0:T(8,128)(2,1)S(1)} %copy-done.2), channel_id=1, source_target_pairs={{0,6},{1,7},{2,4},{3,5},{4,2},{5,3},{6,0},{7,1},{8,14},{9,15},{10,... | collective-permute-start | bytes 1572872 | tf_op jit(solution)/shard_map/ppermute | solution.py:380
  39.0 29.0 %collective-permute-start = (bf16[128,2048]{1,0:T(8,128)(2,1)S(1)}, bf16[128,2048]{1,0:T(8,128)(2,1)S(1)}, u32[]{:S(2)}, u32[]{:S(2)}) collective-permute-start(bf16[128,2048]{1,0:T(8,128)(2,1)S(1)} %copy-done.2), channel_id=1, source_target_pairs={{0,1},{1,0},{2,3},{3,2},{4,5},{5,4},{6,7},{7,6},{8,9},{9,8},{10,11... | collective-permute-start | bytes 1572872 | tf_op jit(solution)/shard_map/ppermute | solution.py:384
  56.4 11.7 %collective-permute-start.2 = (bf16[128,2048]{1,0:T(8,128)(2,1)S(1)}, bf16[128,2048]{1,0:T(8,128)(2,1)}, u32[]{:S(2)}, u32[]{:S(2)}) collective-permute-start(bf16[128,2048]{1,0:T(8,128)(2,1)S(1)} %collective-permute-done.1.refs_2_), channel_id=1, source_target_pairs={{0,1},{1,0},{2,3},{3,2},{4,5},{5,4},{6,7},{7,6},{8,9},{9,8},{10,11... | collective-permute-start | bytes 1572872 | tf_op jit(solution)/shard_map/ppermute | solution.py:384
  56.4 11.7 %collective-permute-start.4 = (bf16[128,2048]{1,0:T(8,128)(2,1)S(1)}, bf16[128,2048]{1,0:T(8,128)(2,1)}, u32[]{:S(2)}, u32[]{:S(2)}) collective-permute-start(bf16[128,2048]{1,0:T(8,128)(2,1)S(1)} %collective-permute-done.3.refs_4_), channel_id=1, source_target_pairs={{0,1},{1,0},{2,3},{3,2},{4,5},{5,4},{6,7},{7,6},{8,9},{9,8},{10,11... | collective-permute-start | bytes 1572872 | tf_op jit(solution)/shard_map/ppermute | solution.py:384
  68.0 2.0 %collective-permute-start.6 = (bf16[128,2048]{1,0:T(8,128)(2,1)S(1)}, bf16[128,2048]{1,0:T(8,128)(2,1)}, u32[]{:S(2)}, u32[]{:S(2)}) collective-permute-start(bf16[128,2048]{1,0:T(8,128)(2,1)S(1)} %collective-permute-done.5.refs_6_), channel_id=1, source_target_pairs={{0,1},{1,0},{2,3},{3,2},{4,5},{5,4},{6,7},{7,6},{8,9},{9,8},{10,11... | collective-permute-start | bytes 1572872 | tf_op jit(solution)/shard_map/ppermute | solution.py:384
  72.6 4.7 %collective-permute-start.7 = (bf16[8,2048]{1,0:T(8,128)(2,1)S(1)}, bf16[8,2048]{1,0:T(8,128)(2,1)S(1)}, u32[]{:S(2)}, u32[]{:S(2)}) collective-permute-start(bf16[8,2048]{1,0:T(8,128)(2,1)S(1)} %get-tuple-element.9), channel_id=1, source_target_pairs={{0,8},{1,9},{2,10},{3,11},{4,12},{5,13},{6,14},{7,15},{8,0},{9,1},... | collective-permute-start | bytes 98312 | tf_op jit(solution)/shard_map/ppermute | solution.py:423
  74.1 5.5 %collective-permute-start.8 = (bf16[8,2048]{1,0:T(8,128)(2,1)S(1)}, bf16[8,2048]{1,0:T(8,128)(2,1)S(1)}, u32[]{:S(2)}, u32[]{:S(2)}) collective-permute-start(bf16[8,2048]{1,0:T(8,128)(2,1)S(1)} %get-tuple-element.10), channel_id=1, source_target_pairs={{0,16},{1,17},{2,18},{3,19},{4,20},{5,21},{6,22},{7,23},{8,24},{9,... | collective-permute-start | bytes 98312 | tf_op jit(solution)/shard_map/ppermute | solution.py:423
  76.5 5.7 %collective-permute-start.9 = (bf16[8,2048]{1,0:T(8,128)(2,1)S(1)}, bf16[8,2048]{1,0:T(8,128)(2,1)S(1)}, u32[]{:S(2)}, u32[]{:S(2)}) collective-permute-start(bf16[8,2048]{1,0:T(8,128)(2,1)S(1)} %get-tuple-element.11), channel_id=1, source_target_pairs={{0,24},{1,25},{2,26},{3,27},{4,28},{5,29},{6,30},{7,31},{8,16},{9,... | collective-permute-start | bytes 98312 | tf_op jit(solution)/shard_map/ppermute | solution.py:423
  83.8 13.2 %all-to-all-start.2 = ((bf16[32,2,16,128]{3,2,1,0:T(8,128)(2,1)}), bf16[32,2,16,128]{3,2,1,0:T(8,128)(2,1)S(1)}, u32[]{:S(2)}, u32[]{:S(2)}) async-start(bf16[32,2,16,128]{3,2,1,0:T(8,128)(2,1)} %get-tuple-element.13), calls=%async_computation.2 | async-start | bytes 524288 | tf_op jit(solution)/shard_map/all_to_all | solution.py:431
  86.4 1.9 %copy-start = (bf16[1,2048,768]{2,1,0:T(8,128)(2,1)S(1)}, bf16[1,2048,768]{2,1,0:T(8,128)(2,1)}, u32[]{:S(2)}) copy-start(bf16[1,2048,768]{2,1,0:T(8,128)(2,1)} %refs_0_.5) | copy-start | bytes 9437188
  88.3 0.8 copy-start.3
  97.0 16.5 %copy-start.4 = (bf16[8,2048]{1,0:T(8,128)(2,1)S(1)}, bf16[8,2048]{1,0:T(8,128)(2,1)}, u32[]{:S(2)}) copy-start(bf16[8,2048]{1,0:T(8,128)(2,1)} %get-tuple-element.6.refs_1_.proj) | copy-start | bytes 98308
  97.0 16.5 %copy-start.8 = (f32[8,8]{1,0:T(8,128)S(1)}, f32[8,8]{1,0:T(8,128)}, u32[]{:S(2)}) copy-start(f32[8,8]{1,0:T(8,128)} %rw.1) | copy-start | bytes 772

commit v4 on v3

--- a/solution.py
+++ b/solution.py
@@ -16,7 +16,7 @@
 LANES = 128
 GROUP = 8
 STATS = 8
-BATCH = 16
+CLASSES = 4
 NEG = -1e30
 COST = 1 << 26
 PROJECT_ROOM = 16
@@ -93,13 +93,12 @@
     out[:, slots * HEADS:, :] = meta[...].astype(BF)
 
 
-def attend_kernel(n, slots, g, hg, lens_in, x, kv, out, lens, mv, ms, of, mx, sg, ob, sem, so):
+def attend_kernel(n, slots, g, hg, lens_in, x, kv, out, lens, mv, ms, sg, ob, sem, so, st):
     get_lens = pltpu.make_async_copy(lens_in, lens, sem.at[1])
     get_lens.start()
-    pairs = n * slots
-    per = pairs // g
     cnt = n // g
     ngrp = n // g
+    per = slots * cnt
     qrows = slots * HEADS
     gw = HEADS // KV_HEADS
     span = hg * per
@@ -110,79 +109,88 @@
             sg[pl.ds(q, n, stride=8), :])[0:8, :].astype(jnp.int32)
     table = pltpu.make_async_copy(mv, ms, sem.at[0])
     table.start()
-    table.wait()
-    get_lens.wait()
     sg[...] = jnp.zeros_like(sg)
     lane = lax.broadcasted_iota(jnp.int32, (HEADS, LANES), 1)
+    spot = lax.rem(lax.div(lane, hg), per)
+    own = lax.rem(lane, hg) == lax.rem(lax.broadcasted_iota(jnp.int32, lane.shape, 0), hg)
     column = lax.broadcasted_iota(jnp.int32, (HEADS, KV_HEADS * BLOCK_TOKENS), 1)
     owner = lax.div(lax.broadcasted_iota(jnp.int32, column.shape, 0), gw)
     tok = jnp.where(lax.div(column, BLOCK_TOKENS) == owner, lax.rem(column, BLOCK_TOKENS), BLOCK_TOKENS)
+    table.wait()
+    get_lens.wait()
+
+    def send(step, grp):
+        first = grp * g + step * CLASSES
+        return pltpu.make_async_copy(
+            ob.at[pl.ds(first, CLASSES), 0:span], out.at[pl.ds(first, CLASSES), 0:span], so.at[step, grp])
+
+    def lump(v):
+        v = jnp.where(own, v, 0.0)
+        return jnp.concatenate(
+            [jnp.sum(v[a:a + hg], axis=0, keepdims=True) for a in range(0, HEADS, hg)], axis=0)
 
     def some(step, carry):
         todo = []
-        for d in range(BATCH):
-            dev = step * BATCH + d
+        for c in range(CLASSES):
+            i = step * CLASSES + c
             for q in range(slots):
-                blk = ms[q * 8, dev] - 1
-                safe = jnp.maximum(blk, 0)
-                length = jnp.where(blk >= 0, lens[safe], 0)
-                base = pl.multiple_of(safe * BLOCK_TOKENS, BLOCK_TOKENS)
-                pos = lax.rem(dev, g) * per + q * cnt + lax.div(dev, g)
-                todo.append((dev, q, length, base, pos, ms[q * 8 + 1, dev]))
+                for s in range(cnt):
+                    dev = s * g + i
+                    blk = ms[q * 8, dev] - 1
+                    safe = jnp.maximum(blk, 0)
+                    length = jnp.where(blk >= 0, lens[safe], 0)
+                    base = pl.multiple_of(safe * BLOCK_TOKENS, BLOCK_TOKENS)
+                    todo.append((dev, q, length, base, c, q * cnt + s, ms[q * 8 + 1, dev]))
         scores = []
-        for dev, q, length, base, pos, rr in todo:
+        for dev, q, length, base, c, at, rr in todo:
             kb = kv[0, pl.ds(base, BLOCK_TOKENS), :]
             kc = jnp.concatenate([kb[:, k * WIDTH:(k + 1) * WIDTH] for k in range(KV_HEADS)], axis=0)
             scores.append(lax.dot_general(
                 x[dev, q * HEADS:(q + 1) * HEADS, :], kc,
                 (((1,), (1,)), ((), ())), preferred_element_type=F32))
         soft = []
-        for s, (dev, q, length, base, pos, rr) in zip(scores, todo):
+        for s, (dev, q, length, base, c, at, rr) in zip(scores, todo):
             s = jnp.where(tok < length, s * (WIDTH ** -0.5), NEG)
             m = jnp.max(s, axis=-1, keepdims=True)
             w = jnp.where(tok < length, jnp.exp(s - m), 0.0).astype(BF)
             l = jnp.sum(w.astype(F32), axis=-1, keepdims=True)
             soft.append((m, w, l))
-        for (m, w, l), (dev, q, length, base, pos, rr) in zip(soft, todo):
+        for (m, w, l), (dev, q, length, base, c, at, rr) in zip(soft, todo):
             vb = kv[1, pl.ds(base, BLOCK_TOKENS), :]
             vc = jnp.concatenate([vb[:, k * WIDTH:(k + 1) * WIDTH] for k in range(KV_HEADS)], axis=0)
-            of[pl.ds(pos, HEADS, stride=pairs), :] = jnp.dot(
-                w, vc, preferred_element_type=F32)
-        top, tot, who = carry
-        for (m, w, l), (dev, q, length, base, pos, rr) in zip(soft, todo):
-            here = lane == pos
-            top = jnp.where(here, m, top)
-            tot = jnp.where(here, l, tot)
-            who = jnp.where(here[0:1], rr.astype(F32), who)
-        return top, tot, who
-
-    zero = jnp.zeros((HEADS, LANES), F32)
-    top, tot, who = lax.fori_loop(0, n // BATCH, some, (zero, zero, zero[0:1]))
-
-    who = jnp.broadcast_to(who, top.shape)
-    hi = top.astype(BF).astype(F32)
-    mid = (top - hi).astype(BF).astype(F32)
-    big = tot.astype(BF).astype(F32)
-    copies = LANES // span
-    for t, v in enumerate((hi, mid, top - hi - mid, big, tot - big, who)):
-        mx[...] = v
-        for i in range(g):
-            row = jnp.concatenate(
-                [mx[pl.ds(hh, ngrp, stride=hg), :][:, i * per:(i + 1) * per] for hh in range(hg)] * copies, axis=1)
-            sg[pl.ds(i * STATS + t, ngrp, stride=g * STATS), :] = row
+            o = jnp.dot(w, vc, preferred_element_type=F32)
+            for grp in range(ngrp):
+                ob[grp * g + step * CLASSES + c, at * hg:(at + 1) * hg, :] = o[grp * hg:(grp + 1) * hg].astype(BF)
+        for grp in range(ngrp):
+            send(step, grp).start()
+        for c in range(CLASSES):
+            top = jnp.zeros((HEADS, LANES), F32)
+            tot = jnp.zeros((HEADS, LANES), F32)
+            who = jnp.zeros((1, LANES), F32)
+            for (m, w, l), (dev, q, length, base, cc, at, rr) in zip(soft, todo):
+                if cc == c:
+                    here = spot == at
+                    top = jnp.where(here, m, top)
+                    tot = jnp.where(here, l, tot)
+                    who = jnp.where(here[0:1], rr.astype(F32), who)
+            top = lump(top)
+            tot = lump(tot)
+            hi = top.astype(BF).astype(F32)
+            mid = (top - hi).astype(BF).astype(F32)
+            big = tot.astype(BF).astype(F32)
+            for t, v in enumerate((hi, mid, top - hi - mid, big, tot - big, jnp.broadcast_to(who, top.shape))):
+                sg[pl.ds((step * CLASSES + c) * STATS + t, ngrp, stride=g * STATS), :] = v
+        return carry
+
+    steps = g // CLASSES
+    lax.fori_loop(0, steps, some, 0)
     ob[:, span:, :] = sg[...].reshape(n, STATS, LANES).astype(BF)
-    sends = []
-    for grp in range(ngrp):
-        for hh in range(hg):
-            h = grp * hg + hh
-            for i in range(g):
-                at = h * pairs + i * per
-                ob[grp * g + i, hh * per:(hh + 1) * per, :] = of[at:at + per, :].astype(BF)
-        sends.append(pltpu.make_async_copy(
-            ob.at[pl.ds(grp * g, g)], out.at[pl.ds(grp * g, g)], so.at[grp]))
-        sends[-1].start()
-    for c in sends:
-        c.wait()
+    last = pltpu.make_async_copy(ob.at[:, span:], out.at[:, span:], st)
+    last.start()
+    for step in range(steps):
+        for grp in range(ngrp):
+            send(step, grp).wait()
+    last.wait()
 
 
 def attend(n, slots, g, hg, block_len, asked, key_value_cache):
@@ -196,12 +204,11 @@
             pltpu.SMEM(block_len.shape, jnp.int32),
             pltpu.VMEM((slots * 8, LANES), jnp.int32),
             pltpu.SMEM((slots * 8, LANES), jnp.int32),
-            pltpu.VMEM((pairs * HEADS, LANES), F32),
-            pltpu.VMEM((HEADS, LANES), F32),
             pltpu.VMEM((n * STATS, LANES), F32),
             pltpu.VMEM((n, span + STATS, LANES), BF),
             pltpu.SemaphoreType.DMA((2,)),
-            pltpu.SemaphoreType.DMA((n // g,)),
+            pltpu.SemaphoreType.DMA((g // CLASSES, n // g)),
+            pltpu.SemaphoreType.DMA,
         ],
         out=ANY, flops=4 * HEADS * pairs * BLOCK_TOKENS * WIDTH, nbytes=COST,
     )(block_len, asked, key_value_cache)
@@ -243,8 +250,8 @@
     c = f / den
     lane = lax.broadcasted_iota(jnp.int32, (n, LANES), 1)
     inner = lax.rem(lane, span)
-    hh = lax.div(inner, per)
-    pl_ = lax.rem(inner, per)
+    hh = lax.rem(inner, hg)
+    pl_ = lax.div(inner, hg)
     q = lax.div(pl_, cnt)
     s = lax.rem(pl_, cnt)
     local = rows * cnt
@@ -274,7 +281,7 @@
         out[...] = sp[lax.bitwise_xor(mine_group, j)].astype(BF)
 
 
-def norm_kernel(count, eid, slot, *refs):
+def norm_kernel(count, index, *refs):
     x = refs[:count]
     res, gain, proj, out, nf = refs[count:]
     rows, width = res.shape
@@ -289,17 +296,16 @@
     tiles = width // LANES
     for c in range(tiles):
         nf[pl.ds(c, rows, stride=tiles), :] = nrm[:, c * LANES:(c + 1) * LANES]
-    if rows * eid.shape[1] != out.shape[0] * CAP:
+    if rows * index.shape[1] != out.shape[0]:
         out[...] = jnp.zeros_like(out)
     for r in range(rows):
         tile = nf[r * tiles:(r + 1) * tiles, :].astype(BF)
-        for k in range(eid.shape[1]):
-            out[eid[r, k], slot[r, k]] = tile
+        for k in range(index.shape[1]):
+            out[index[r, k]] = tile
 
 
 def expert_kernel(x, wu, wg, wd, out, xf, xb, of, gb, db, sg, sd):
-    n, cap, tiles, _ = x.shape
-    m = n * cap
+    m, tiles, _ = x.shape
     width, ffe = wu.shape
     gc = ffe // GATE_PARTS
     dc = width // DOWN_PARTS
@@ -324,16 +330,16 @@
         o = jnp.dot(h, db[:, i * dc:(i + 1) * dc], preferred_element_type=F32)
         for t in range(dc // LANES):
             of[pl.ds(i * dc // LANES + t, m, stride=tiles), :] = o[:, t * LANES:(t + 1) * LANES]
-    out[...] = of[...].astype(BF).reshape(n, cap, tiles, LANES)
-
-
-def finish_kernel(eid, slot, rw, x, res, proj, out, acc):
+    out[...] = of[...].astype(BF).reshape(m, tiles, LANES)
+
+
+def finish_kernel(index, rw, x, res, proj, out, acc):
     rows, width = res.shape
     tiles = width // LANES
     for r in range(rows):
         a = jnp.zeros((tiles, LANES), F32)
-        for k in range(eid.shape[1]):
-            a = a + rw[r, k] * x[eid[r, k], slot[r, k]].astype(F32)
+        for k in range(index.shape[1]):
+            a = a + rw[r, k] * x[index[r, k]].astype(F32)
         acc[r * tiles:(r + 1) * tiles, :] = a
     for c in range(tiles):
         sl = slice(c * LANES, (c + 1) * LANES)
@@ -387,7 +393,8 @@
     place = jnp.arange(flat.shape[0])
     slot = jnp.sum(
         (flat[:, None] == flat[None, :]) & (place[:, None] > place[None, :]), axis=1
-    ).astype(jnp.int32).reshape(expert_ids.shape)
+    ).astype(jnp.int32)
+    index = (flat * CAP + slot).reshape(expert_ids.shape)
 
     chunk = slots * HEADS + 8
     sent = call(
@@ -418,25 +425,25 @@
         ],
         flops=2 * local * g * fw * width, nbytes=COST, room=PROJECT_ROOM,
     )(back, *pieces)
+    (up_w,) = stage(w_up, after=(partial[0],))
     summed = [partial[0]]
-    for j in range(1, cnt):
+    for j in range(cnt - 1, 0, -1):
         summed.append(lax.ppermute(partial[j], "section", [(i, i ^ (j * g)) for i in range(n)]))
     experts = n * w_gate.shape[0]
     attn_proj, routed = call(
         functools.partial(norm_kernel, cnt),
-        (sds((rows, width), BF), sds((experts, CAP, tiles, LANES), BF)), [SM, SM] + [VM] * (cnt + 2),
+        (sds((rows, width), BF), sds((experts * CAP, tiles, LANES), BF)), [SM] + [VM] * (cnt + 2),
         [pltpu.VMEM((rows * tiles, LANES), F32)],
         nbytes=COST,
-    )(expert_ids, slot, *summed, residual_in, norm_gain.reshape(1, width))
+    )(index, *summed, residual_in, norm_gain.reshape(1, width))
     arrived = a2a(routed)
-    (up_w,) = stage(w_up, after=(attn_proj,))
     ffe = w_gate.shape[2]
     slots_in = n * CAP
 
     def run_expert(xin, wu, wg, wd):
         return call(
             expert_kernel,
-            sds((n, CAP, tiles, LANES), BF), [VM, VM, ANY, ANY],
+            sds((slots_in, tiles, LANES), BF), [VM, VM, ANY, ANY],
             [
                 pltpu.VMEM((slots_in * tiles, LANES), F32),
                 pltpu.VMEM((slots_in, width), BF),
@@ -454,16 +461,16 @@
         done = run_expert(arrived, up_w[0], w_gate[0], w_down[0])
     else:
         split = arrived.reshape(n, per_device, CAP, tiles, LANES)
-        done = jnp.stack(
-            [run_expert(split[:, e], up_w[e], w_gate[e], w_down[e]) for e in range(per_device)], axis=1
-        ).reshape(arrived.shape)
+        done = jnp.stack([
+            run_expert(split[:, e].reshape(slots_in, tiles, LANES), up_w[e], w_gate[e], w_down[e])
+            .reshape(n, CAP, tiles, LANES) for e in range(per_device)], axis=1).reshape(arrived.shape)
     returned = a2a(done)
     layer_out = call(
         finish_kernel,
-        sds((rows, width), BF), [SM, SM, SM, VM, VM, VM],
+        sds((rows, width), BF), [SM, SM, VM, VM, VM],
         [pltpu.VMEM((rows * tiles, LANES), F32)],
         nbytes=1 << 19,
-    )(expert_ids, slot, route_weight, returned, residual_in, attn_proj)
+    )(index, route_weight, returned, residual_in, attn_proj)
     return (attn_proj, layer_out)
 
 

time: 116 us -> 112 us (0.966)
  Pallas kernels: 17.2 us -> 15.5 us
    pallas_call x1, Pallas kernels: 5.39 us -> 3.89 us  [attend(): call(functools.partial(attend_kernel, n, slots, g, hg), sds((n, span + ST...]
    ppermute x3, waiting for transfers between devices: 4.95 us -> 3.74 us  [shards(): lax.ppermute(partial[j], 'section', [(i, i ^ j * g) for i in range(n)])]
    unnamed x20 -> x18, local copies, waits for them, and re-layouts: 4.27 us -> 3.51 us
where the time goes in v4:
time: 112 us
  waiting for transfers between devices  57.3 us (51%)
  starting transfers between devices  21.6 us (19%)
  Pallas kernels  15.5 us (14%)
  blocking collectives  12.7 us (11%)
  local copies, waits for them, and re-layouts  3.66 us (3%)
    ppermute x3, waiting for transfers between devices, shards(): lax.ppermute(out_weight, 'section', [(i, i ^ far) for i in range(n)])  28.4 us
    all_to_all x1, waiting for transfers between devices, shards(): asked = a2a(sent)  15 us
    all_to_all x1, blocking collectives, shards(): returned = a2a(done)  12.7 us
    all_to_all x1, waiting for transfers between devices, shards(): arrived = a2a(routed)  8.45 us
    all_to_all x1, starting transfers between devices, shards(): asked = a2a(sent)  7.33 us
    ppermute x3, starting transfers between devices, shards(): lax.ppermute(partial[j], 'section', [(i, i ^ j * g) for i in range(n)])  4.45 us
    pallas_call x1, Pallas kernels, attend(): call(functools.partial(attend_kernel, n, slots, g, hg), sds((n, span + ST...  3.89 us
    pallas_call x1, Pallas kernels, run_expert(): call(expert_kernel, sds((slots_in, tiles, LANES), BF), [VM, VM, ANY, ANY]...  3.78 us
  transfers between devices with their start and end apart: 13, of which 7 were waited for; matrix products, arithmetic and copies ran while one was open for 0% of the time, Pallas kernels for 0%

profile of v4, /device:TPU:0, one launch (start us, length us, event | category | flops | bytes accessed | tf_op | source)
XLA Modules:
  0.0 111.8 jit_solution(17602951598941926904)
XLA Ops:
  0.6 0.0 copy-start.7
  0.6 2.0 %shard_map.131 = bf16[32,72,128]{2,1,0:T(8,128)(2,1)} custom-call(s32[8,8]{1,0:T(8,128)} %ids_in.1, bf16[8,4096]{1,0:T(8,128)(2,1)} %q_in.1), custom_call_target="tpu_custom_call" | custom-call | bytes 67108864 | tf_op jit(solution)/shard_map/pallas_call | solution.py:400
  2.7 7.3 %all-to-all-start = ((bf16[32,72,128]{2,1,0:T(8,128)(2,1)}), bf16[32,72,128]{2,1,0:T(8,128)(2,1)S(1)}, u32[]{:S(2)}, u32[]{:S(2)}) async-start(bf16[32,72,128]{2,1,0:T(8,128)(2,1)} %shard_map.131), calls=%async_computation | async-start | bytes 1179648 | tf_op jit(solution)/shard_map/all_to_all | solution.py:412
  10.0 0.0 copy-start.1
  10.0 1.6 %copy-done.1 = bf16[2,1024,512]{2,1,0:T(8,128)(2,1)S(1)} copy-done((bf16[2,1024,512]{2,1,0:T(8,128)(2,1)S(1)}, bf16[2,1024,512]{2,1,0:T(8,128)(2,1)}, u32[]{:S(2)}) %copy-start.1) | copy-done | bytes 2097176
  11.6 0.1 shard_map.132.kv
  11.8 0.0 copy-start.2
  11.8 0.0 copy-start.8
  11.8 15.0 %all-to-all-done.x = bf16[32,72,128]{2,1,0:T(8,128)(2,1)S(1)} async-done(((bf16[32,72,128]{2,1,0:T(8,128)(2,1)}), bf16[32,72,128]{2,1,0:T(8,128)(2,1)S(1)}, u32[]{:S(2)}, u32[]{:S(2)}) %all-to-all-start) | async-done | bytes 589856 | tf_op jit(solution)/shard_map/all_to_all | solution.py:412
  26.8 0.0 copy-done.7
  26.8 3.9 %shard_map.133 = bf16[32,72,128]{2,1,0:T(8,128)(2,1)} custom-call(s32[16]{0:T(128)S(1)} %copy-done.7, bf16[32,72,128]{2,1,0:T(8,128)(2,1)S(1)} %all-to-all-done.x, bf16[2,1024,512]{2,1,0:T(8,128)(2,1)S(1)} %shard_map.132.kv), custom_call_target="tpu_custom_call" | custom-call | flops 67108864 | bytes 67108864 | tf_op jit(solution)/shard_map/pallas_call | solution.py:200
  30.7 0.0 copy-start.3
  30.7 0.0 copy-start.5
  30.7 3.2 %all-to-all-start.1 = ((bf16[32,72,128]{2,1,0:T(8,128)(2,1)}), bf16[32,72,128]{2,1,0:T(8,128)(2,1)S(1)}, u32[]{:S(2)}, u32[]{:S(2)}) async-start(bf16[32,72,128]{2,1,0:T(8,128)(2,1)} %shard_map.133), calls=%async_computation.1 | async-start | bytes 1179648 | tf_op jit(solution)/shard_map/all_to_all | solution.py:414
  33.9 0.0 copy-done.2
  33.9 1.8 %collective-permute-start.1 = (bf16[128,2048]{1,0:T(8,128)(2,1)S(1)}, bf16[128,2048]{1,0:T(8,128)(2,1)S(1)}, u32[]{:S(2)}, u32[]{:S(2)}) collective-permute-start(bf16[128,2048]{1,0:T(8,128)(2,1)S(1)} %copy-done.2), channel_id=1, source_target_pairs={{0,2},{1,3},{2,0},{3,1},{4,6},{5,7},{6,4},{7,5},{8,10},{9,11},{10,... | collective-permute-start | bytes 1572872 | tf_op jit(solution)/shard_map/ppermute | solution.py:386
  35.8 1.5 %collective-permute-start.3 = (bf16[128,2048]{1,0:T(8,128)(2,1)S(1)}, bf16[128,2048]{1,0:T(8,128)(2,1)S(1)}, u32[]{:S(2)}, u32[]{:S(2)}) collective-permute-start(bf16[128,2048]{1,0:T(8,128)(2,1)S(1)} %copy-done.2), channel_id=1, source_target_pairs={{0,4},{1,5},{2,6},{3,7},{4,0},{5,1},{6,2},{7,3},{8,12},{9,13},{10,... | collective-permute-start | bytes 1572872 | tf_op jit(solution)/shard_map/ppermute | solution.py:386
  37.2 0.3 collective-permute-start.5
  37.5 0.0 collective-permute-start
  37.5 17.4 %collective-permute-done.1.refs_2_ = bf16[128,2048]{1,0:T(8,128)(2,1)S(1)} collective-permute-done((bf16[128,2048]{1,0:T(8,128)(2,1)S(1)}, bf16[128,2048]{1,0:T(8,128)(2,1)S(1)}, u32[]{:S(2)}, u32[]{:S(2)}) %collective-permute-start.1) | collective-permute-done | bytes 524320 | tf_op jit(solution)/shard_map/ppermute | solution.py:386
  54.9 0.0 collective-permute-start.2
  54.9 0.0 collective-permute-done.3.refs_4_
  54.9 0.5 collective-permute-start.4
  55.4 11.0 %collective-permute-done.5.refs_6_ = bf16[128,2048]{1,0:T(8,128)(2,1)S(1)} collective-permute-done((bf16[128,2048]{1,0:T(8,128)(2,1)S(1)}, bf16[128,2048]{1,0:T(8,128)(2,1)S(1)}, u32[]{:S(2)}, u32[]{:S(2)}) %collective-permute-start.5) | collective-permute-done | bytes 524320 | tf_op jit(solution)/shard_map/ppermute | solution.py:386
  66.5 0.0 collective-permute-start.6
  66.5 0.0 copy-done.8
  66.5 0.1 eq.15
  66.5 0.2 convert_reduce_fusion
  66.7 0.1 reduce_sum.12
  66.8 0.0 collective-permute-done.refs_1_
  66.8 0.0 collective-permute-done.2.refs_3_
  66.8 0.0 collective-permute-done.4.refs_5_
  66.8 1.7 %collective-permute-done.6.refs_7_ = bf16[128,2048]{1,0:T(8,128)(2,1)} collective-permute-done((bf16[128,2048]{1,0:T(8,128)(2,1)S(1)}, bf16[128,2048]{1,0:T(8,128)(2,1)}, u32[]{:S(2)}, u32[]{:S(2)}) %collective-permute-start.6) | collective-permute-done | bytes 524320 | tf_op jit(solution)/shard_map/ppermute | solution.py:390
  68.5 0.0 all-to-all-done.1.x
  68.5 2.5 %shard_map.134 = (bf16[8,2048]{1,0:T(8,128)(2,1)S(1)}, bf16[8,2048]{1,0:T(8,128)(2,1)S(1)}, bf16[8,2048]{1,0:T(8,128)(2,1)S(1)}, bf16[8,2048]{1,0:T(8,128)(2,1)S(1)}) custom-call(bf16[32,72,128]{2,1,0:T(8,128)(2,1)S(1)} %all-to-all-done.1.x, bf16[128,2048]{1,0:T(8,128)(2,1)S(1)} %copy-done.2, bf16[128,2048]{1,0:T(8,128)(2,1)S(1)} %collective-permute-done.refs_1_, ...), custom_call_target="tpu_custom_call" | custom-call | flops 134217728 | bytes 67108864 | tf_op jit(solution)/shard_map/pallas_call | solution.py:416
  71.0 3.4 %collective-permute-start.7 = (bf16[8,2048]{1,0:T(8,128)(2,1)S(1)}, bf16[8,2048]{1,0:T(8,128)(2,1)S(1)}, u32[]{:S(2)}, u32[]{:S(2)}) collective-permute-start(bf16[8,2048]{1,0:T(8,128)(2,1)S(1)} %get-tuple-element.9), channel_id=1, source_target_pairs={{0,24},{1,25},{2,26},{3,27},{4,28},{5,29},{6,30},{7,31},{8,16},{9,... | collective-permute-start | bytes 98312 | tf_op jit(solution)/shard_map/ppermute | solution.py:431
  74.4 0.0 collective-permute-start.8
  74.4 1.1 collective-permute-start.9
  75.5 1.3 %collective-permute-done.7.refs_1_ = bf16[8,2048]{1,0:T(8,128)(2,1)S(1)} collective-permute-done((bf16[8,2048]{1,0:T(8,128)(2,1)S(1)}, bf16[8,2048]{1,0:T(8,128)(2,1)S(1)}, u32[]{:S(2)}, u32[]{:S(2)}) %collective-permute-start.7) | collective-permute-done | bytes 32800 | tf_op jit(solution)/shard_map/ppermute | solution.py:431
  76.8 2.4 %collective-permute-done.8.refs_2_ = bf16[8,2048]{1,0:T(8,128)(2,1)S(1)} collective-permute-done((bf16[8,2048]{1,0:T(8,128)(2,1)S(1)}, bf16[8,2048]{1,0:T(8,128)(2,1)S(1)}, u32[]{:S(2)}, u32[]{:S(2)}) %collective-permute-start.8) | collective-permute-done | bytes 32800 | tf_op jit(solution)/shard_map/ppermute | solution.py:431
  79.2 0.0 collective-permute-done.9.refs_3_
  79.2 0.0 copy-done.3
  79.2 0.0 copy-done.5
  79.2 1.5 %shard_map.135 = (bf16[8,2048]{1,0:T(8,128)(2,1)}, bf16[64,16,128]{2,1,0:T(8,128)(2,1)}) custom-call(s32[8,8]{1,0:T(8,128)S(1)} %multiply_add_fusion.index, bf16[8,2048]{1,0:T(8,128)(2,1)S(1)} %get-tuple-element.8.refs_0_.refs_1_, bf16[8,2048]{1,0:T(8,128)(2,1)S(1)} %collective-permute-done.7.refs_1_, bf16[8,2048]{1,0:T(8,128)(2,1)S(1)} %collective-permute-done.8.refs_2_, ...), custom_call_target="tpu_custom_call" | custom-call | bytes 67108864 | tf_op jit(solution)/shard_map/pallas_call | solution.py:433
  80.8 2.6 %all-to-all-start.2 = ((bf16[64,16,128]{2,1,0:T(8,128)(2,1)}), bf16[64,16,128]{2,1,0:T(8,128)(2,1)S(1)}, u32[]{:S(2)}, u32[]{:S(2)}) async-start(bf16[64,16,128]{2,1,0:T(8,128)(2,1)} %get-tuple-element.13), calls=%async_computation.2 | async-start | bytes 524288 | tf_op jit(solution)/shard_map/all_to_all | solution.py:439
  83.3 0.0 copy-start
  83.4 1.9 %copy-done = bf16[1,2048,768]{2,1,0:T(8,128)(2,1)S(1)} copy-done((bf16[1,2048,768]{2,1,0:T(8,128)(2,1)S(1)}, bf16[1,2048,768]{2,1,0:T(8,128)(2,1)}, u32[]{:S(2)}) %copy-start) | copy-done | bytes 3145752
  85.2 0.2 shard_map.136
  85.5 8.5 %all-to-all-done.2.x = bf16[64,16,128]{2,1,0:T(8,128)(2,1)S(1)} async-done(((bf16[64,16,128]{2,1,0:T(8,128)(2,1)}), bf16[64,16,128]{2,1,0:T(8,128)(2,1)S(1)}, u32[]{:S(2)}, u32[]{:S(2)}) %all-to-all-start.2) | async-done | bytes 262176 | tf_op jit(solution)/shard_map/all_to_all | solution.py:439
  93.9 0.0 copy-start.4
  93.9 0.0 copy-start.6
  93.9 3.8 %shard_map.137 = bf16[64,16,128]{2,1,0:T(8,128)(2,1)S(1)} custom-call(bf16[64,16,128]{2,1,0:T(8,128)(2,1)S(1)} %all-to-all-done.2.x, bf16[2048,768]{1,0:T(8,128)(2,1)S(1)} %bitcast.4, bf16[2048,768]{1,0:T(8,128)(2,1)} %bitcast.6, bf16[768,2048]{1,0:T(8,128)(2,1)} %bitcast.7), custom_call_target="tpu_custom_call" | custom-call | flops 603979776 | bytes 9437184 | tf_op jit(solution)/shard_map/pallas_call | solution.py:444
  97.7 12.7 %all_to_all.20.x = bf16[64,16,128]{2,1,0:T(8,128)(2,1)S(1)} all-to-all(bf16[64,16,128]{2,1,0:T(8,128)(2,1)S(1)} %shard_map.137), channel_id=1, replica_groups=mesh['groups'=1,'section'=32] {'section'}, dimensions={0} | all-to-all | bytes 524288 | tf_op jit(solution)/shard_map/all_to_all | solution.py:467
  110.4 0.0 copy-done.4
  110.4 0.0 copy-done.6
  110.4 1.4 %shard_map.138 = bf16[8,2048]{1,0:T(8,128)(2,1)} custom-call(s32[8,8]{1,0:T(8,128)S(1)} %multiply_add_fusion.index, f32[8,8]{1,0:T(8,128)S(1)} %copy-done.6, bf16[64,16,128]{2,1,0:T(8,128)(2,1)S(1)} %all_to_all.20.x, bf16[8,2048]{1,0:T(8,128)(2,1)S(1)} %copy-done.3, bf16[8,2048]{1,0:T(8,128)(2,1)S(1)} %copy-done.4), custom_call_target="tpu_custom_call" | custom-call | bytes 524288 | tf_op jit(solution)/shard_map/pallas_call | solution.py:468
  (1 shorter events, 0.0 us)
Async XLA Ops:
  0.6 26.2 %copy-start.7 = (s32[16]{0:T(128)S(1)}, s32[16]{0:T(128)}, u32[]{:S(2)}) copy-start(s32[16]{0:T(128)} %lens_in.1) | copy-start | bytes 196
  2.7 24.1 %all-to-all-start = ((bf16[32,72,128]{2,1,0:T(8,128)(2,1)}), bf16[32,72,128]{2,1,0:T(8,128)(2,1)S(1)}, u32[]{:S(2)}, u32[]{:S(2)}) async-start(bf16[32,72,128]{2,1,0:T(8,128)(2,1)} %shard_map.131), calls=%async_computation | async-start | bytes 1179648 | tf_op jit(solution)/shard_map/all_to_all | solution.py:412
  10.0 1.6 %copy-start.1 = (bf16[2,1024,512]{2,1,0:T(8,128)(2,1)S(1)}, bf16[2,1024,512]{2,1,0:T(8,128)(2,1)}, u32[]{:S(2)}) copy-start(bf16[2,1024,512]{2,1,0:T(8,128)(2,1)} %refs_0_.3) | copy-start | bytes 6291460
  11.8 22.2 %copy-start.2 = (bf16[128,2048]{1,0:T(8,128)(2,1)S(1)}, bf16[128,2048]{1,0:T(8,128)(2,1)}, u32[]{:S(2)}) copy-start(bf16[128,2048]{1,0:T(8,128)(2,1)} %refs_0_.4) | copy-start | bytes 1572868
  11.8 54.7 %copy-start.8 = (s32[8,8]{1,0:T(8,128)S(1)}, s32[8,8]{1,0:T(8,128)}, u32[]{:S(2)}) copy-start(s32[8,8]{1,0:T(8,128)} %param.19) | copy-start | bytes 772
  30.7 48.5 %copy-start.3 = (bf16[8,2048]{1,0:T(8,128)(2,1)S(1)}, bf16[8,2048]{1,0:T(8,128)(2,1)}, u32[]{:S(2)}) copy-start(bf16[8,2048]{1,0:T(8,128)(2,1)} %res.1) | copy-start | bytes 98308
  30.7 48.5 %copy-start.5 = (f32[2048]{0:T(1024)S(1)}, f32[2048]{0:T(1024)}, u32[]{:S(2)}) copy-start(f32[2048]{0:T(1024)} %param.18) | copy-start | bytes 24580
  30.7 37.8 %all-to-all-start.1 = ((bf16[32,72,128]{2,1,0:T(8,128)(2,1)}), bf16[32,72,128]{2,1,0:T(8,128)(2,1)S(1)}, u32[]{:S(2)}, u32[]{:S(2)}) async-start(bf16[32,72,128]{2,1,0:T(8,128)(2,1)} %shard_map.133), calls=%async_computation.1 | async-start | bytes 1179648 | tf_op jit(solution)/shard_map/all_to_all | solution.py:414
  33.9 20.9 %collective-permute-start.1 = (bf16[128,2048]{1,0:T(8,128)(2,1)S(1)}, bf16[128,2048]{1,0:T(8,128)(2,1)S(1)}, u32[]{:S(2)}, u32[]{:S(2)}) collective-permute-start(bf16[128,2048]{1,0:T(8,128)(2,1)S(1)} %copy-done.2), channel_id=1, source_target_pairs={{0,2},{1,3},{2,0},{3,1},{4,6},{5,7},{6,4},{7,5},{8,10},{9,11},{10,... | collective-permute-start | bytes 1572872 | tf_op jit(solution)/shard_map/ppermute | solution.py:386
  35.8 19.1 %collective-permute-start.3 = (bf16[128,2048]{1,0:T(8,128)(2,1)S(1)}, bf16[128,2048]{1,0:T(8,128)(2,1)S(1)}, u32[]{:S(2)}, u32[]{:S(2)}) collective-permute-start(bf16[128,2048]{1,0:T(8,128)(2,1)S(1)} %copy-done.2), channel_id=1, source_target_pairs={{0,4},{1,5},{2,6},{3,7},{4,0},{5,1},{6,2},{7,3},{8,12},{9,13},{10,... | collective-permute-start | bytes 1572872 | tf_op jit(solution)/shard_map/ppermute | solution.py:386
  37.2 29.2 %collective-permute-start.5 = (bf16[128,2048]{1,0:T(8,128)(2,1)S(1)}, bf16[128,2048]{1,0:T(8,128)(2,1)S(1)}, u32[]{:S(2)}, u32[]{:S(2)}) collective-permute-start(bf16[128,2048]{1,0:T(8,128)(2,1)S(1)} %copy-done.2), channel_id=1, source_target_pairs={{0,6},{1,7},{2,4},{3,5},{4,2},{5,3},{6,0},{7,1},{8,14},{9,15},{10,... | collective-permute-start | bytes 1572872 | tf_op jit(solution)/shard_map/ppermute | solution.py:386
  37.5 29.3 %collective-permute-start = (bf16[128,2048]{1,0:T(8,128)(2,1)S(1)}, bf16[128,2048]{1,0:T(8,128)(2,1)S(1)}, u32[]{:S(2)}, u32[]{:S(2)}) collective-permute-start(bf16[128,2048]{1,0:T(8,128)(2,1)S(1)} %copy-done.2), channel_id=1, source_target_pairs={{0,1},{1,0},{2,3},{3,2},{4,5},{5,4},{6,7},{7,6},{8,9},{9,8},{10,11... | collective-permute-start | bytes 1572872 | tf_op jit(solution)/shard_map/ppermute | solution.py:390
  54.9 11.9 %collective-permute-start.2 = (bf16[128,2048]{1,0:T(8,128)(2,1)S(1)}, bf16[128,2048]{1,0:T(8,128)(2,1)}, u32[]{:S(2)}, u32[]{:S(2)}) collective-permute-start(bf16[128,2048]{1,0:T(8,128)(2,1)S(1)} %collective-permute-done.1.refs_2_), channel_id=1, source_target_pairs={{0,1},{1,0},{2,3},{3,2},{4,5},{5,4},{6,7},{7,6},{8,9},{9,8},{10,11... | collective-permute-start | bytes 1572872 | tf_op jit(solution)/shard_map/ppermute | solution.py:390
  54.9 11.9 %collective-permute-start.4 = (bf16[128,2048]{1,0:T(8,128)(2,1)S(1)}, bf16[128,2048]{1,0:T(8,128)(2,1)}, u32[]{:S(2)}, u32[]{:S(2)}) collective-permute-start(bf16[128,2048]{1,0:T(8,128)(2,1)S(1)} %collective-permute-done.3.refs_4_), channel_id=1, source_target_pairs={{0,1},{1,0},{2,3},{3,2},{4,5},{5,4},{6,7},{7,6},{8,9},{9,8},{10,11... | collective-permute-start | bytes 1572872 | tf_op jit(solution)/shard_map/ppermute | solution.py:390
  66.5 2.0 %collective-permute-start.6 = (bf16[128,2048]{1,0:T(8,128)(2,1)S(1)}, bf16[128,2048]{1,0:T(8,128)(2,1)}, u32[]{:S(2)}, u32[]{:S(2)}) collective-permute-start(bf16[128,2048]{1,0:T(8,128)(2,1)S(1)} %collective-permute-done.5.refs_6_), channel_id=1, source_target_pairs={{0,1},{1,0},{2,3},{3,2},{4,5},{5,4},{6,7},{7,6},{8,9},{9,8},{10,11... | collective-permute-start | bytes 1572872 | tf_op jit(solution)/shard_map/ppermute | solution.py:390
  71.0 5.8 %collective-permute-start.7 = (bf16[8,2048]{1,0:T(8,128)(2,1)S(1)}, bf16[8,2048]{1,0:T(8,128)(2,1)S(1)}, u32[]{:S(2)}, u32[]{:S(2)}) collective-permute-start(bf16[8,2048]{1,0:T(8,128)(2,1)S(1)} %get-tuple-element.9), channel_id=1, source_target_pairs={{0,24},{1,25},{2,26},{3,27},{4,28},{5,29},{6,30},{7,31},{8,16},{9,... | collective-permute-start | bytes 98312 | tf_op jit(solution)/shard_map/ppermute | solution.py:431
  74.4 4.8 %collective-permute-start.8 = (bf16[8,2048]{1,0:T(8,128)(2,1)S(1)}, bf16[8,2048]{1,0:T(8,128)(2,1)S(1)}, u32[]{:S(2)}, u32[]{:S(2)}) collective-permute-start(bf16[8,2048]{1,0:T(8,128)(2,1)S(1)} %get-tuple-element.10), channel_id=1, source_target_pairs={{0,16},{1,17},{2,18},{3,19},{4,20},{5,21},{6,22},{7,23},{8,24},{9,... | collective-permute-start | bytes 98312 | tf_op jit(solution)/shard_map/ppermute | solution.py:431
  74.4 4.8 %collective-permute-start.9 = (bf16[8,2048]{1,0:T(8,128)(2,1)S(1)}, bf16[8,2048]{1,0:T(8,128)(2,1)S(1)}, u32[]{:S(2)}, u32[]{:S(2)}) collective-permute-start(bf16[8,2048]{1,0:T(8,128)(2,1)S(1)} %get-tuple-element.11), channel_id=1, source_target_pairs={{0,8},{1,9},{2,10},{3,11},{4,12},{5,13},{6,14},{7,15},{8,0},{9,1},... | collective-permute-start | bytes 98312 | tf_op jit(solution)/shard_map/ppermute | solution.py:431
  80.8 13.2 %all-to-all-start.2 = ((bf16[64,16,128]{2,1,0:T(8,128)(2,1)}), bf16[64,16,128]{2,1,0:T(8,128)(2,1)S(1)}, u32[]{:S(2)}, u32[]{:S(2)}) async-start(bf16[64,16,128]{2,1,0:T(8,128)(2,1)} %get-tuple-element.13), calls=%async_computation.2 | async-start | bytes 524288 | tf_op jit(solution)/shard_map/all_to_all | solution.py:439
  83.3 1.9 %copy-start = (bf16[1,2048,768]{2,1,0:T(8,128)(2,1)S(1)}, bf16[1,2048,768]{2,1,0:T(8,128)(2,1)}, u32[]{:S(2)}) copy-start(bf16[1,2048,768]{2,1,0:T(8,128)(2,1)} %refs_0_.5) | copy-start | bytes 9437188
  93.9 16.5 %copy-start.4 = (bf16[8,2048]{1,0:T(8,128)(2,1)S(1)}, bf16[8,2048]{1,0:T(8,128)(2,1)}, u32[]{:S(2)}) copy-start(bf16[8,2048]{1,0:T(8,128)(2,1)} %get-tuple-element.6.proj) | copy-start | bytes 98308
  93.9 16.5 %copy-start.6 = (f32[8,8]{1,0:T(8,128)S(1)}, f32[8,8]{1,0:T(8,128)}, u32[]{:S(2)}) copy-start(f32[8,8]{1,0:T(8,128)} %rw.1) | copy-start | bytes 772

commit v5 on v4

--- a/solution.py
+++ b/solution.py
@@ -64,21 +64,22 @@
     )(*arrays, *after)
 
 
-def pack_kernel(run, slots, blocks, ids_in, q_in, out, ids, q, qs, meta, sem):
+def pack_kernel(run, slots, blocks, ids_in, q_in, out, ids, q, qs, meta, ob, sem, so):
     rows = q.shape[0]
     picks = ids.shape[1]
     get_ids = pltpu.make_async_copy(ids_in, ids, sem.at[0])
     get_q = pltpu.make_async_copy(q_in, q, sem.at[1])
     get_ids.start()
     get_q.start()
+    meta[...] = jnp.zeros_like(meta)
+    if rows * picks != out.shape[0] * slots:
+        ob[...] = jnp.zeros_like(ob)
     get_q.wait()
     for h in range(HEADS):
         qs[pl.ds(h, rows, stride=HEADS), :] = q[:, h * WIDTH:(h + 1) * WIDTH].astype(F32)
-    meta[...] = jnp.zeros_like(meta)
     get_ids.wait()
-    if rows * picks != out.shape[0] * slots:
-        out[...] = jnp.zeros_like(out)
     lane = lax.broadcasted_iota(jnp.int32, (1, LANES), 1)
+    sends = []
     for r in range(rows):
         tile = qs[r * HEADS:(r + 1) * HEADS, :].astype(BF)
         slot = r // run
@@ -86,11 +87,20 @@
             b = ids[r, j]
             dev = lax.div(b, blocks)
             local = b - dev * blocks
-            out[dev, slot * HEADS:(slot + 1) * HEADS, :] = tile
+            ob[dev, slot * HEADS:(slot + 1) * HEADS, :] = tile
             meta[dev, slot:slot + 1, :] = jnp.where(
                 lane == 0, local + 1, jnp.where(lane == 1, r % run, 0)
             ).astype(F32)
-    out[:, slots * HEADS:, :] = meta[...].astype(BF)
+        if r % run == run - 1 or r == rows - 1:
+            if r == rows - 1:
+                ob[:, slots * HEADS:, :] = meta[...].astype(BF)
+                part = slice(slot * HEADS, slots * HEADS + 8)
+            else:
+                part = slice(slot * HEADS, (slot + 1) * HEADS)
+            sends.append(pltpu.make_async_copy(ob.at[:, part], out.at[:, part], so.at[slot]))
+            sends[-1].start()
+    for c in sends:
+        c.wait()
 
 
 def attend_kernel(n, slots, g, hg, lens_in, x, kv, out, lens, mv, ms, sg, ob, sem, so, st):
@@ -113,9 +123,10 @@
     lane = lax.broadcasted_iota(jnp.int32, (HEADS, LANES), 1)
     spot = lax.rem(lax.div(lane, hg), per)
     own = lax.rem(lane, hg) == lax.rem(lax.broadcasted_iota(jnp.int32, lane.shape, 0), hg)
-    column = lax.broadcasted_iota(jnp.int32, (HEADS, KV_HEADS * BLOCK_TOKENS), 1)
-    owner = lax.div(lax.broadcasted_iota(jnp.int32, column.shape, 0), gw)
-    tok = jnp.where(lax.div(column, BLOCK_TOKENS) == owner, lax.rem(column, BLOCK_TOKENS), BLOCK_TOKENS)
+    held = LANES // BLOCK_TOKENS
+    owner = lax.rem(lax.div(lax.broadcasted_iota(jnp.int32, lane.shape, 0), gw), held)
+    tok = jnp.where(lax.div(lane, BLOCK_TOKENS) == owner, lax.rem(lane, BLOCK_TOKENS), BLOCK_TOKENS)
+    blank = jnp.zeros((held * gw, LANES), BF)
     table.wait()
     get_lens.wait()
 
@@ -150,6 +161,9 @@
                 (((1,), (1,)), ((), ())), preferred_element_type=F32))
         soft = []
         for s, (dev, q, length, base, c, at, rr) in zip(scores, todo):
+            s = jnp.concatenate([
+                s[a * held * gw:(a + 1) * held * gw, a * LANES:(a + 1) * LANES]
+                for a in range(KV_HEADS // held)], axis=0)
             s = jnp.where(tok < length, s * (WIDTH ** -0.5), NEG)
             m = jnp.max(s, axis=-1, keepdims=True)
             w = jnp.where(tok < length, jnp.exp(s - m), 0.0).astype(BF)
@@ -158,7 +172,12 @@
         for (m, w, l), (dev, q, length, base, c, at, rr) in zip(soft, todo):
             vb = kv[1, pl.ds(base, BLOCK_TOKENS), :]
             vc = jnp.concatenate([vb[:, k * WIDTH:(k + 1) * WIDTH] for k in range(KV_HEADS)], axis=0)
-            o = jnp.dot(w, vc, preferred_element_type=F32)
+            wide = jnp.concatenate([
+                jnp.concatenate([
+                    w[a * held * gw:(a + 1) * held * gw] if b == a else blank
+                    for b in range(KV_HEADS // held)], axis=1)
+                for a in range(KV_HEADS // held)], axis=0)
+            o = jnp.dot(wide, vc, preferred_element_type=F32)
             for grp in range(ngrp):
                 ob[grp * g + step * CLASSES + c, at * hg:(at + 1) * hg, :] = o[grp * hg:(grp + 1) * hg].astype(BF)
         for grp in range(ngrp):
@@ -217,15 +236,15 @@
 def project_kernel(n, slots, g, hg, run, rows, x, *refs):
     pieces = refs[:g]
     outs = refs[g:g + n // g]
-    sf, cm, ws, sp, sem = refs[g + n // g:]
+    sf, cm, ws, sp, ab, sem = refs[g + n // g:]
     fw = pieces[0].shape[0]
     me = lax.rem(lax.axis_index("section"), g)
     mine_group = lax.div(lax.axis_index("section"), g)
-    loads = []
-    for i, piece in enumerate(pieces):
+    loads = {}
+    for i in list(range(2, g, 2)) + list(range(3, g, 2)) + [0, 1]:
         at = pl.multiple_of(lax.bitwise_xor(me, i) * fw, fw)
-        loads.append(pltpu.make_async_copy(piece, ws.at[pl.ds(at, fw)], sem.at[i]))
-        loads[-1].start()
+        loads[i] = pltpu.make_async_copy(pieces[i], ws.at[pl.ds(at, fw)], sem.at[i])
+        loads[i].start()
     pairs = n * slots
     per = pairs // g
     span = hg * per
@@ -270,26 +289,35 @@
         cm[:, t * LANES:(t + 1) * LANES] = jnp.where(row == blk_t, blk_c, 0.0).astype(BF)
     a = x[:, 0:span, :].reshape(n * span, LANES)
     att = jnp.dot(cm[...], a, preferred_element_type=F32).astype(BF)
-    att = jnp.concatenate([att[i * local:(i + 1) * local, :] for i in range(hg)], axis=1)
-    for c in loads:
-        c.wait()
-    for col in range(0, ws.shape[1], 512):
-        p = jnp.dot(att, ws[:, col:col + 512], preferred_element_type=F32)
-        for s_ in range(cnt):
-            sp[s_, :, col:col + 512] = p[s_ * rows:(s_ + 1) * rows]
+    ab[...] = jnp.concatenate([att[i * local:(i + 1) * local, :] for i in range(hg)], axis=1)
+    for far in range(0, g, 2):
+        loads[far].wait()
+        loads[far + 1].wait()
+        at = pl.multiple_of(lax.div(lax.bitwise_xor(me, far), 2) * (2 * fw), 2 * fw)
+        for col in range(0, ws.shape[1], 512):
+            p = jnp.dot(
+                ab[:, pl.ds(at, 2 * fw)], ws[pl.ds(at, 2 * fw), col:col + 512],
+                preferred_element_type=F32).reshape(cnt, rows, 512)
+            if far:
+                p = p + sp[:, :, col:col + 512]
+            sp[:, :, col:col + 512] = p
     for j, out in enumerate(outs):
         out[...] = sp[lax.bitwise_xor(mine_group, j)].astype(BF)
 
 
-def norm_kernel(count, index, *refs):
+def norm_kernel(count, index_in, *refs):
     x = refs[:count]
-    res, gain, proj, out, nf = refs[count:]
+    res, gain, proj, out, nf, pb, ob, index, sem = refs[count:]
+    get = pltpu.make_async_copy(index_in, index, sem.at[0])
+    get.start()
     rows, width = res.shape
     acc = x[0][...].astype(F32)
     for i in range(1, count):
         acc = acc + x[i][...].astype(F32)
     p = acc.astype(BF)
-    proj[...] = p
+    pb[...] = p
+    put = pltpu.make_async_copy(pb, proj, sem.at[1])
+    put.start()
     stream = res[...].astype(F32) + p.astype(F32)
     ms = jnp.mean(stream * stream, axis=-1, keepdims=True)
     nrm = stream * lax.rsqrt(ms + 1e-06) * gain[...]
@@ -297,11 +325,16 @@
     for c in range(tiles):
         nf[pl.ds(c, rows, stride=tiles), :] = nrm[:, c * LANES:(c + 1) * LANES]
     if rows * index.shape[1] != out.shape[0]:
-        out[...] = jnp.zeros_like(out)
+        ob[...] = jnp.zeros_like(ob)
+    get.wait()
     for r in range(rows):
         tile = nf[r * tiles:(r + 1) * tiles, :].astype(BF)
         for k in range(index.shape[1]):
-            out[index[r, k]] = tile
+            ob[index[r, k]] = tile
+    send = pltpu.make_async_copy(ob, out, sem.at[2])
+    send.start()
+    put.wait()
+    send.wait()
 
 
 def expert_kernel(x, wu, wg, wd, out, xf, xb, of, gb, db, sg, sd):
@@ -333,9 +366,18 @@
     out[...] = of[...].astype(BF).reshape(m, tiles, LANES)
 
 
-def finish_kernel(index, rw, x, res, proj, out, acc):
+def finish_kernel(index_in, rw_in, x, res, proj, out, acc, base, index, rw, sem):
+    loads = [
+        pltpu.make_async_copy(index_in, index, sem.at[0]),
+        pltpu.make_async_copy(rw_in, rw, sem.at[1]),
+    ]
+    for c in loads:
+        c.start()
     rows, width = res.shape
     tiles = width // LANES
+    base[...] = res[...].astype(F32) + proj[...].astype(F32)
+    for c in loads:
+        c.wait()
     for r in range(rows):
         a = jnp.zeros((tiles, LANES), F32)
         for k in range(index.shape[1]):
@@ -343,8 +385,7 @@
         acc[r * tiles:(r + 1) * tiles, :] = a
     for c in range(tiles):
         sl = slice(c * LANES, (c + 1) * LANES)
-        stream = res[:, sl].astype(F32) + proj[:, sl].astype(F32)
-        out[:, sl] = (stream + acc[pl.ds(c, rows, stride=tiles), :]).astype(BF)
+        out[:, sl] = (base[:, sl] + acc[pl.ds(c, rows, stride=tiles), :]).astype(BF)
 
 
 def shards(
@@ -405,9 +446,11 @@
             pltpu.VMEM(queries.shape, BF),
             pltpu.VMEM((rows * HEADS, LANES), F32),
             pltpu.VMEM((n, 8, LANES), F32),
+            pltpu.VMEM((n, chunk, LANES), BF),
             pltpu.SemaphoreType.DMA((2,)),
+            pltpu.SemaphoreType.DMA((slots,)),
         ],
-        nbytes=COST, room=60,
+        nbytes=COST, room=60, out=ANY,
     )(block_ids, queries)
     asked = a2a(sent)
     parts = attend(n, slots, g, hg, block_len, asked, cache)
@@ -421,6 +464,7 @@
             pltpu.VMEM((hg * local, n * span), BF),
             pltpu.VMEM((g * fw, width), BF),
             pltpu.VMEM((cnt, rows, width), F32),
+            pltpu.VMEM((local, g * fw), BF),
             pltpu.SemaphoreType.DMA((g,)),
         ],
         flops=2 * local * g * fw * width, nbytes=COST, room=PROJECT_ROOM,
@@ -432,9 +476,15 @@
     experts = n * w_gate.shape[0]
     attn_proj, routed = call(
         functools.partial(norm_kernel, cnt),
-        (sds((rows, width), BF), sds((experts * CAP, tiles, LANES), BF)), [SM] + [VM] * (cnt + 2),
-        [pltpu.VMEM((rows * tiles, LANES), F32)],
-        nbytes=COST,
+        (sds((rows, width), BF), sds((experts * CAP, tiles, LANES), BF)), [ANY] + [VM] * (cnt + 2),
+        [
+            pltpu.VMEM((rows * tiles, LANES), F32),
+            pltpu.VMEM((rows, width), BF),
+            pltpu.VMEM((experts * CAP, tiles, LANES), BF),
+            pltpu.SMEM(index.shape, jnp.int32),
+            pltpu.SemaphoreType.DMA((3,)),
+        ],
+        out=(ANY, ANY), nbytes=COST,
     )(index, *summed, residual_in, norm_gain.reshape(1, width))
     arrived = a2a(routed)
     ffe = w_gate.shape[2]
@@ -467,8 +517,14 @@
     returned = a2a(done)
     layer_out = call(
         finish_kernel,
-        sds((rows, width), BF), [SM, SM, VM, VM, VM],
-        [pltpu.VMEM((rows * tiles, LANES), F32)],
+        sds((rows, width), BF), [ANY, ANY, VM, VM, VM],
+        [
+            pltpu.VMEM((rows * tiles, LANES), F32),
+            pltpu.VMEM((rows, width), F32),
+            pltpu.SMEM(index.shape, jnp.int32),
+            pltpu.SMEM(route_weight.shape, F32),
+            pltpu.SemaphoreType.DMA((2,)),
+        ],
         nbytes=1 << 19,
     )(index, route_weight, returned, residual_in, attn_proj)
     return (attn_proj, layer_out)

time: 112 us -> 111 us (level)
  no operation moved by 1% of the time
where the time goes in v5:
time: 111 us
  waiting for transfers between devices  57.3 us (52%)
  starting transfers between devices  21.7 us (20%)
  Pallas kernels  14.6 us (13%)
  blocking collectives  12.7 us (11%)
  local copies, waits for them, and re-layouts  3.66 us (3%)
    ppermute x3, waiting for transfers between devices, shards(): lax.ppermute(out_weight, 'section', [(i, i ^ far) for i in range(n)])  28.4 us
    all_to_all x1, waiting for transfers between devices, shards(): asked = a2a(sent)  15 us
    all_to_all x1, blocking collectives, shards(): returned = a2a(done)  12.7 us
    all_to_all x1, waiting for transfers between devices, shards(): arrived = a2a(routed)  8.45 us
    all_to_all x1, starting transfers between devices, shards(): asked = a2a(sent)  7.33 us
    ppermute x3, starting transfers between devices, shards(): lax.ppermute(partial[j], 'section', [(i, i ^ j * g) for i in range(n)])  4.45 us
    pallas_call x1, Pallas kernels, attend(): call(functools.partial(attend_kernel, n, slots, g, hg), sds((n, span + ST...  3.79 us
    pallas_call x1, Pallas kernels, run_expert(): call(expert_kernel, sds((slots_in, tiles, LANES), BF), [VM, VM, ANY, ANY]...  3.78 us
  transfers between devices with their start and end apart: 13, of which 7 were waited for; matrix products, arithmetic and copies ran while one was open for 0% of the time, Pallas kernels for 0%

profile of v5, /device:TPU:0, one launch (start us, length us, event | category | flops | bytes accessed | tf_op | source)
XLA Modules:
  0.0 110.9 jit_solution(5402590788119020005)
XLA Ops:
  0.6 0.0 copy-start.7
  0.6 2.0 %shard_map.131 = bf16[32,72,128]{2,1,0:T(8,128)(2,1)} custom-call(s32[8,8]{1,0:T(8,128)} %ids_in.1, bf16[8,4096]{1,0:T(8,128)(2,1)} %q_in.1), custom_call_target="tpu_custom_call" | custom-call | bytes 67108864 | tf_op jit(solution)/shard_map/pallas_call | solution.py:441
  2.6 7.3 %all-to-all-start = ((bf16[32,72,128]{2,1,0:T(8,128)(2,1)}), bf16[32,72,128]{2,1,0:T(8,128)(2,1)S(1)}, u32[]{:S(2)}, u32[]{:S(2)}) async-start(bf16[32,72,128]{2,1,0:T(8,128)(2,1)} %shard_map.131), calls=%async_computation | async-start | bytes 1179648 | tf_op jit(solution)/shard_map/all_to_all | solution.py:455
  9.9 0.0 copy-start.1
  10.0 1.6 %copy-done.1 = bf16[2,1024,512]{2,1,0:T(8,128)(2,1)S(1)} copy-done((bf16[2,1024,512]{2,1,0:T(8,128)(2,1)S(1)}, bf16[2,1024,512]{2,1,0:T(8,128)(2,1)}, u32[]{:S(2)}) %copy-start.1) | copy-done | bytes 2097176
  11.5 0.1 shard_map.132.kv
  11.7 0.0 copy-start.2
  11.7 0.0 copy-start.8
  11.7 15.0 %all-to-all-done.x = bf16[32,72,128]{2,1,0:T(8,128)(2,1)S(1)} async-done(((bf16[32,72,128]{2,1,0:T(8,128)(2,1)}), bf16[32,72,128]{2,1,0:T(8,128)(2,1)S(1)}, u32[]{:S(2)}, u32[]{:S(2)}) %all-to-all-start) | async-done | bytes 589856 | tf_op jit(solution)/shard_map/all_to_all | solution.py:455
  26.7 0.0 copy-done.7
  26.7 3.8 %shard_map.133 = bf16[32,72,128]{2,1,0:T(8,128)(2,1)} custom-call(s32[16]{0:T(128)S(1)} %copy-done.7, bf16[32,72,128]{2,1,0:T(8,128)(2,1)S(1)} %all-to-all-done.x, bf16[2,1024,512]{2,1,0:T(8,128)(2,1)S(1)} %shard_map.132.kv), custom_call_target="tpu_custom_call" | custom-call | flops 67108864 | bytes 67108864 | tf_op jit(solution)/shard_map/pallas_call | solution.py:219
  30.5 0.0 copy-start.3
  30.6 0.0 copy-start.5
  30.6 3.2 %all-to-all-start.1 = ((bf16[32,72,128]{2,1,0:T(8,128)(2,1)}), bf16[32,72,128]{2,1,0:T(8,128)(2,1)S(1)}, u32[]{:S(2)}, u32[]{:S(2)}) async-start(bf16[32,72,128]{2,1,0:T(8,128)(2,1)} %shard_map.133), calls=%async_computation.1 | async-start | bytes 1179648 | tf_op jit(solution)/shard_map/all_to_all | solution.py:457
  33.8 0.0 copy-done.2
  33.8 1.8 %collective-permute-start.1 = (bf16[128,2048]{1,0:T(8,128)(2,1)S(1)}, bf16[128,2048]{1,0:T(8,128)(2,1)S(1)}, u32[]{:S(2)}, u32[]{:S(2)}) collective-permute-start(bf16[128,2048]{1,0:T(8,128)(2,1)S(1)} %copy-done.2), channel_id=1, source_target_pairs={{0,2},{1,3},{2,0},{3,1},{4,6},{5,7},{6,4},{7,5},{8,10},{9,11},{10,... | collective-permute-start | bytes 1572872 | tf_op jit(solution)/shard_map/ppermute | solution.py:427
  35.6 1.5 %collective-permute-start.3 = (bf16[128,2048]{1,0:T(8,128)(2,1)S(1)}, bf16[128,2048]{1,0:T(8,128)(2,1)S(1)}, u32[]{:S(2)}, u32[]{:S(2)}) collective-permute-start(bf16[128,2048]{1,0:T(8,128)(2,1)S(1)} %copy-done.2), channel_id=1, source_target_pairs={{0,4},{1,5},{2,6},{3,7},{4,0},{5,1},{6,2},{7,3},{8,12},{9,13},{10,... | collective-permute-start | bytes 1572872 | tf_op jit(solution)/shard_map/ppermute | solution.py:427
  37.1 0.3 collective-permute-start.5
  37.3 0.0 collective-permute-start
  37.3 17.4 %collective-permute-done.1.refs_2_ = bf16[128,2048]{1,0:T(8,128)(2,1)S(1)} collective-permute-done((bf16[128,2048]{1,0:T(8,128)(2,1)S(1)}, bf16[128,2048]{1,0:T(8,128)(2,1)S(1)}, u32[]{:S(2)}, u32[]{:S(2)}) %collective-permute-start.1) | collective-permute-done | bytes 524320 | tf_op jit(solution)/shard_map/ppermute | solution.py:427
  54.7 0.0 collective-permute-start.2
  54.7 0.0 collective-permute-done.3.refs_4_
  54.7 0.5 collective-permute-start.4
  55.2 11.0 %collective-permute-done.5.refs_6_ = bf16[128,2048]{1,0:T(8,128)(2,1)S(1)} collective-permute-done((bf16[128,2048]{1,0:T(8,128)(2,1)S(1)}, bf16[128,2048]{1,0:T(8,128)(2,1)S(1)}, u32[]{:S(2)}, u32[]{:S(2)}) %collective-permute-start.5) | collective-permute-done | bytes 524320 | tf_op jit(solution)/shard_map/ppermute | solution.py:427
  66.3 0.0 collective-permute-start.6
  66.3 0.0 copy-done.8
  66.3 0.1 eq.15
  66.4 0.2 convert_reduce_fusion
  66.6 0.1 reduce_sum.12
  66.6 0.0 collective-permute-done.refs_1_
  66.6 0.0 collective-permute-done.2.refs_3_
  66.7 0.0 collective-permute-done.4.refs_5_
  66.7 1.7 %collective-permute-done.6.refs_7_ = bf16[128,2048]{1,0:T(8,128)(2,1)} collective-permute-done((bf16[128,2048]{1,0:T(8,128)(2,1)S(1)}, bf16[128,2048]{1,0:T(8,128)(2,1)}, u32[]{:S(2)}, u32[]{:S(2)}) %collective-permute-start.6) | collective-permute-done | bytes 524320 | tf_op jit(solution)/shard_map/ppermute | solution.py:431
  68.3 0.0 all-to-all-done.1.x
  68.3 1.9 %shard_map.134 = (bf16[8,2048]{1,0:T(8,128)(2,1)S(1)}, bf16[8,2048]{1,0:T(8,128)(2,1)S(1)}, bf16[8,2048]{1,0:T(8,128)(2,1)S(1)}, bf16[8,2048]{1,0:T(8,128)(2,1)S(1)}) custom-call(bf16[32,72,128]{2,1,0:T(8,128)(2,1)S(1)} %all-to-all-done.1.x, bf16[128,2048]{1,0:T(8,128)(2,1)S(1)} %copy-done.2, bf16[128,2048]{1,0:T(8,128)(2,1)S(1)} %collective-permute-done.refs_1_, ...), custom_call_target="tpu_custom_call" | custom-call | flops 134217728 | bytes 67108864 | tf_op jit(solution)/shard_map/pallas_call | solution.py:459
  70.3 3.4 %collective-permute-start.7 = (bf16[8,2048]{1,0:T(8,128)(2,1)S(1)}, bf16[8,2048]{1,0:T(8,128)(2,1)S(1)}, u32[]{:S(2)}, u32[]{:S(2)}) collective-permute-start(bf16[8,2048]{1,0:T(8,128)(2,1)S(1)} %get-tuple-element.9), channel_id=1, source_target_pairs={{0,24},{1,25},{2,26},{3,27},{4,28},{5,29},{6,30},{7,31},{8,16},{9,... | collective-permute-start | bytes 98312 | tf_op jit(solution)/shard_map/ppermute | solution.py:475
  73.6 0.0 collective-permute-start.8
  73.6 1.1 collective-permute-start.9
  74.7 1.3 %collective-permute-done.7.refs_1_ = bf16[8,2048]{1,0:T(8,128)(2,1)S(1)} collective-permute-done((bf16[8,2048]{1,0:T(8,128)(2,1)S(1)}, bf16[8,2048]{1,0:T(8,128)(2,1)S(1)}, u32[]{:S(2)}, u32[]{:S(2)}) %collective-permute-start.7) | collective-permute-done | bytes 32800 | tf_op jit(solution)/shard_map/ppermute | solution.py:475
  76.0 2.4 %collective-permute-done.8.refs_2_ = bf16[8,2048]{1,0:T(8,128)(2,1)S(1)} collective-permute-done((bf16[8,2048]{1,0:T(8,128)(2,1)S(1)}, bf16[8,2048]{1,0:T(8,128)(2,1)S(1)}, u32[]{:S(2)}, u32[]{:S(2)}) %collective-permute-start.8) | collective-permute-done | bytes 32800 | tf_op jit(solution)/shard_map/ppermute | solution.py:475
  78.4 0.0 collective-permute-done.9.refs_3_
  78.5 0.0 copy-done.3
  78.5 0.0 copy-done.5
  78.5 1.4 %shard_map.135 = (bf16[8,2048]{1,0:T(8,128)(2,1)}, bf16[64,16,128]{2,1,0:T(8,128)(2,1)}) custom-call(s32[8,8]{1,0:T(8,128)S(1)} %multiply_add_fusion.index_in, bf16[8,2048]{1,0:T(8,128)(2,1)S(1)} %get-tuple-element.8.refs_0_.refs_1_, bf16[8,2048]{1,0:T(8,128)(2,1)S(1)} %collective-permute-done.7.refs_1_, bf16[8,2048]{1,0:T(8,128)(2,1)S(1)} %collective-permute-done.8.refs_2_, ...), custom_call_target="tpu_custom_call" | custom-call | bytes 67108864 | tf_op jit(solution)/shard_map/pallas_call | solution.py:477
  79.9 2.6 %all-to-all-start.2 = ((bf16[64,16,128]{2,1,0:T(8,128)(2,1)}), bf16[64,16,128]{2,1,0:T(8,128)(2,1)S(1)}, u32[]{:S(2)}, u32[]{:S(2)}) async-start(bf16[64,16,128]{2,1,0:T(8,128)(2,1)} %get-tuple-element.13), calls=%async_computation.2 | async-start | bytes 524288 | tf_op jit(solution)/shard_map/all_to_all | solution.py:489
  82.5 0.0 copy-start
  82.5 1.9 %copy-done = bf16[1,2048,768]{2,1,0:T(8,128)(2,1)S(1)} copy-done((bf16[1,2048,768]{2,1,0:T(8,128)(2,1)S(1)}, bf16[1,2048,768]{2,1,0:T(8,128)(2,1)}, u32[]{:S(2)}) %copy-start) | copy-done | bytes 3145752
  84.4 0.2 shard_map.136
  84.6 8.5 %all-to-all-done.2.x = bf16[64,16,128]{2,1,0:T(8,128)(2,1)S(1)} async-done(((bf16[64,16,128]{2,1,0:T(8,128)(2,1)}), bf16[64,16,128]{2,1,0:T(8,128)(2,1)S(1)}, u32[]{:S(2)}, u32[]{:S(2)}) %all-to-all-start.2) | async-done | bytes 262176 | tf_op jit(solution)/shard_map/all_to_all | solution.py:489
  93.0 0.0 copy-start.4
  93.0 0.0 copy-start.6
  93.0 3.8 %shard_map.137 = bf16[64,16,128]{2,1,0:T(8,128)(2,1)S(1)} custom-call(bf16[64,16,128]{2,1,0:T(8,128)(2,1)S(1)} %all-to-all-done.2.x, bf16[2048,768]{1,0:T(8,128)(2,1)S(1)} %bitcast.4, bf16[2048,768]{1,0:T(8,128)(2,1)} %bitcast.6, bf16[768,2048]{1,0:T(8,128)(2,1)} %bitcast.7), custom_call_target="tpu_custom_call" | custom-call | flops 603979776 | bytes 9437184 | tf_op jit(solution)/shard_map/pallas_call | solution.py:494
  96.8 12.7 %all_to_all.20.x = bf16[64,16,128]{2,1,0:T(8,128)(2,1)S(1)} all-to-all(bf16[64,16,128]{2,1,0:T(8,128)(2,1)S(1)} %shard_map.137), channel_id=1, replica_groups=mesh['groups'=1,'section'=32] {'section'}, dimensions={0} | all-to-all | bytes 524288 | tf_op jit(solution)/shard_map/all_to_all | solution.py:517
  109.5 0.0 copy-done.4
  109.5 0.0 copy-done.6
  109.5 1.4 %shard_map.138 = bf16[8,2048]{1,0:T(8,128)(2,1)} custom-call(s32[8,8]{1,0:T(8,128)S(1)} %multiply_add_fusion.index_in, f32[8,8]{1,0:T(8,128)S(1)} %copy-done.6, bf16[64,16,128]{2,1,0:T(8,128)(2,1)S(1)} %all_to_all.20.x, bf16[8,2048]{1,0:T(8,128)(2,1)S(1)} %copy-done.3, bf16[8,2048]{1,0:T(8,128)(2,1)S(1)} %copy-done.4), custom_call_target="tpu_custom_call" | custom-call | bytes 524288 | tf_op jit(solution)/shard_map/pallas_call | solution.py:518
  (1 shorter events, 0.0 us)
Async XLA Ops:
  0.6 26.1 %copy-start.7 = (s32[16]{0:T(128)S(1)}, s32[16]{0:T(128)}, u32[]{:S(2)}) copy-start(s32[16]{0:T(128)} %lens_in.1) | copy-start | bytes 196
  2.6 24.1 %all-to-all-start = ((bf16[32,72,128]{2,1,0:T(8,128)(2,1)}), bf16[32,72,128]{2,1,0:T(8,128)(2,1)S(1)}, u32[]{:S(2)}, u32[]{:S(2)}) async-start(bf16[32,72,128]{2,1,0:T(8,128)(2,1)} %shard_map.131), calls=%async_computation | async-start | bytes 1179648 | tf_op jit(solution)/shard_map/all_to_all | solution.py:455
  9.9 1.6 %copy-start.1 = (bf16[2,1024,512]{2,1,0:T(8,128)(2,1)S(1)}, bf16[2,1024,512]{2,1,0:T(8,128)(2,1)}, u32[]{:S(2)}) copy-start(bf16[2,1024,512]{2,1,0:T(8,128)(2,1)} %refs_0_.3) | copy-start | bytes 6291460
  11.7 22.1 %copy-start.2 = (bf16[128,2048]{1,0:T(8,128)(2,1)S(1)}, bf16[128,2048]{1,0:T(8,128)(2,1)}, u32[]{:S(2)}) copy-start(bf16[128,2048]{1,0:T(8,128)(2,1)} %refs_0_.4) | copy-start | bytes 1572868
  11.7 54.6 %copy-start.8 = (s32[8,8]{1,0:T(8,128)S(1)}, s32[8,8]{1,0:T(8,128)}, u32[]{:S(2)}) copy-start(s32[8,8]{1,0:T(8,128)} %param.19) | copy-start | bytes 772
  30.5 47.9 %copy-start.3 = (bf16[8,2048]{1,0:T(8,128)(2,1)S(1)}, bf16[8,2048]{1,0:T(8,128)(2,1)}, u32[]{:S(2)}) copy-start(bf16[8,2048]{1,0:T(8,128)(2,1)} %res.1) | copy-start | bytes 98308
  30.6 47.9 %copy-start.5 = (f32[2048]{0:T(1024)S(1)}, f32[2048]{0:T(1024)}, u32[]{:S(2)}) copy-start(f32[2048]{0:T(1024)} %param.18) | copy-start | bytes 24580
  30.6 37.8 %all-to-all-start.1 = ((bf16[32,72,128]{2,1,0:T(8,128)(2,1)}), bf16[32,72,128]{2,1,0:T(8,128)(2,1)S(1)}, u32[]{:S(2)}, u32[]{:S(2)}) async-start(bf16[32,72,128]{2,1,0:T(8,128)(2,1)} %shard_map.133), calls=%async_computation.1 | async-start | bytes 1179648 | tf_op jit(solution)/shard_map/all_to_all | solution.py:457
  33.8 20.9 %collective-permute-start.1 = (bf16[128,2048]{1,0:T(8,128)(2,1)S(1)}, bf16[128,2048]{1,0:T(8,128)(2,1)S(1)}, u32[]{:S(2)}, u32[]{:S(2)}) collective-permute-start(bf16[128,2048]{1,0:T(8,128)(2,1)S(1)} %copy-done.2), channel_id=1, source_target_pairs={{0,2},{1,3},{2,0},{3,1},{4,6},{5,7},{6,4},{7,5},{8,10},{9,11},{10,... | collective-permute-start | bytes 1572872 | tf_op jit(solution)/shard_map/ppermute | solution.py:427
  35.6 19.1 %collective-permute-start.3 = (bf16[128,2048]{1,0:T(8,128)(2,1)S(1)}, bf16[128,2048]{1,0:T(8,128)(2,1)S(1)}, u32[]{:S(2)}, u32[]{:S(2)}) collective-permute-start(bf16[128,2048]{1,0:T(8,128)(2,1)S(1)} %copy-done.2), channel_id=1, source_target_pairs={{0,4},{1,5},{2,6},{3,7},{4,0},{5,1},{6,2},{7,3},{8,12},{9,13},{10,... | collective-permute-start | bytes 1572872 | tf_op jit(solution)/shard_map/ppermute | solution.py:427
  37.1 29.2 %collective-permute-start.5 = (bf16[128,2048]{1,0:T(8,128)(2,1)S(1)}, bf16[128,2048]{1,0:T(8,128)(2,1)S(1)}, u32[]{:S(2)}, u32[]{:S(2)}) collective-permute-start(bf16[128,2048]{1,0:T(8,128)(2,1)S(1)} %copy-done.2), channel_id=1, source_target_pairs={{0,6},{1,7},{2,4},{3,5},{4,2},{5,3},{6,0},{7,1},{8,14},{9,15},{10,... | collective-permute-start | bytes 1572872 | tf_op jit(solution)/shard_map/ppermute | solution.py:427
  37.3 29.3 %collective-permute-start = (bf16[128,2048]{1,0:T(8,128)(2,1)S(1)}, bf16[128,2048]{1,0:T(8,128)(2,1)S(1)}, u32[]{:S(2)}, u32[]{:S(2)}) collective-permute-start(bf16[128,2048]{1,0:T(8,128)(2,1)S(1)} %copy-done.2), channel_id=1, source_target_pairs={{0,1},{1,0},{2,3},{3,2},{4,5},{5,4},{6,7},{7,6},{8,9},{9,8},{10,11... | collective-permute-start | bytes 1572872 | tf_op jit(solution)/shard_map/ppermute | solution.py:431
  54.7 11.9 %collective-permute-start.2 = (bf16[128,2048]{1,0:T(8,128)(2,1)S(1)}, bf16[128,2048]{1,0:T(8,128)(2,1)}, u32[]{:S(2)}, u32[]{:S(2)}) collective-permute-start(bf16[128,2048]{1,0:T(8,128)(2,1)S(1)} %collective-permute-done.1.refs_2_), channel_id=1, source_target_pairs={{0,1},{1,0},{2,3},{3,2},{4,5},{5,4},{6,7},{7,6},{8,9},{9,8},{10,11... | collective-permute-start | bytes 1572872 | tf_op jit(solution)/shard_map/ppermute | solution.py:431
  54.7 11.9 %collective-permute-start.4 = (bf16[128,2048]{1,0:T(8,128)(2,1)S(1)}, bf16[128,2048]{1,0:T(8,128)(2,1)}, u32[]{:S(2)}, u32[]{:S(2)}) collective-permute-start(bf16[128,2048]{1,0:T(8,128)(2,1)S(1)} %collective-permute-done.3.refs_4_), channel_id=1, source_target_pairs={{0,1},{1,0},{2,3},{3,2},{4,5},{5,4},{6,7},{7,6},{8,9},{9,8},{10,11... | collective-permute-start | bytes 1572872 | tf_op jit(solution)/shard_map/ppermute | solution.py:431
  66.3 2.0 %collective-permute-start.6 = (bf16[128,2048]{1,0:T(8,128)(2,1)S(1)}, bf16[128,2048]{1,0:T(8,128)(2,1)}, u32[]{:S(2)}, u32[]{:S(2)}) collective-permute-start(bf16[128,2048]{1,0:T(8,128)(2,1)S(1)} %collective-permute-done.5.refs_6_), channel_id=1, source_target_pairs={{0,1},{1,0},{2,3},{3,2},{4,5},{5,4},{6,7},{7,6},{8,9},{9,8},{10,11... | collective-permute-start | bytes 1572872 | tf_op jit(solution)/shard_map/ppermute | solution.py:431
  70.3 5.8 %collective-permute-start.7 = (bf16[8,2048]{1,0:T(8,128)(2,1)S(1)}, bf16[8,2048]{1,0:T(8,128)(2,1)S(1)}, u32[]{:S(2)}, u32[]{:S(2)}) collective-permute-start(bf16[8,2048]{1,0:T(8,128)(2,1)S(1)} %get-tuple-element.9), channel_id=1, source_target_pairs={{0,24},{1,25},{2,26},{3,27},{4,28},{5,29},{6,30},{7,31},{8,16},{9,... | collective-permute-start | bytes 98312 | tf_op jit(solution)/shard_map/ppermute | solution.py:475
  73.6 4.8 %collective-permute-start.8 = (bf16[8,2048]{1,0:T(8,128)(2,1)S(1)}, bf16[8,2048]{1,0:T(8,128)(2,1)S(1)}, u32[]{:S(2)}, u32[]{:S(2)}) collective-permute-start(bf16[8,2048]{1,0:T(8,128)(2,1)S(1)} %get-tuple-element.10), channel_id=1, source_target_pairs={{0,16},{1,17},{2,18},{3,19},{4,20},{5,21},{6,22},{7,23},{8,24},{9,... | collective-permute-start | bytes 98312 | tf_op jit(solution)/shard_map/ppermute | solution.py:475
  73.6 4.8 %collective-permute-start.9 = (bf16[8,2048]{1,0:T(8,128)(2,1)S(1)}, bf16[8,2048]{1,0:T(8,128)(2,1)S(1)}, u32[]{:S(2)}, u32[]{:S(2)}) collective-permute-start(bf16[8,2048]{1,0:T(8,128)(2,1)S(1)} %get-tuple-element.11), channel_id=1, source_target_pairs={{0,8},{1,9},{2,10},{3,11},{4,12},{5,13},{6,14},{7,15},{8,0},{9,1},... | collective-permute-start | bytes 98312 | tf_op jit(solution)/shard_map/ppermute | solution.py:475
  79.9 13.2 %all-to-all-start.2 = ((bf16[64,16,128]{2,1,0:T(8,128)(2,1)}), bf16[64,16,128]{2,1,0:T(8,128)(2,1)S(1)}, u32[]{:S(2)}, u32[]{:S(2)}) async-start(bf16[64,16,128]{2,1,0:T(8,128)(2,1)} %get-tuple-element.13), calls=%async_computation.2 | async-start | bytes 524288 | tf_op jit(solution)/shard_map/all_to_all | solution.py:489
  82.5 1.9 %copy-start = (bf16[1,2048,768]{2,1,0:T(8,128)(2,1)S(1)}, bf16[1,2048,768]{2,1,0:T(8,128)(2,1)}, u32[]{:S(2)}) copy-start(bf16[1,2048,768]{2,1,0:T(8,128)(2,1)} %refs_0_.5) | copy-start | bytes 9437188
  93.0 16.5 %copy-start.4 = (bf16[8,2048]{1,0:T(8,128)(2,1)S(1)}, bf16[8,2048]{1,0:T(8,128)(2,1)}, u32[]{:S(2)}) copy-start(bf16[8,2048]{1,0:T(8,128)(2,1)} %get-tuple-element.6.proj) | copy-start | bytes 98308
  93.0 16.5 %copy-start.6 = (f32[8,8]{1,0:T(8,128)S(1)}, f32[8,8]{1,0:T(8,128)}, u32[]{:S(2)}) copy-start(f32[8,8]{1,0:T(8,128)} %rw_in.1) | copy-start | bytes 772

commit v6 on v5

--- a/solution.py
+++ b/solution.py
@@ -16,6 +16,8 @@
 LANES = 128
 GROUP = 8
 STATS = 8
+TILE = 2
+PART = 4
 CLASSES = 4
 NEG = -1e30
 COST = 1 << 26
@@ -81,22 +83,22 @@
     lane = lax.broadcasted_iota(jnp.int32, (1, LANES), 1)
     sends = []
     for r in range(rows):
-        tile = qs[r * HEADS:(r + 1) * HEADS, :].astype(BF)
+        tile = qs[r * HEADS:(r + 1) * HEADS, :].astype(BF).reshape(HEADS // TILE, TILE, LANES)
         slot = r // run
         for j in range(picks):
             b = ids[r, j]
             dev = lax.div(b, blocks)
             local = b - dev * blocks
-            ob[dev, slot * HEADS:(slot + 1) * HEADS, :] = tile
+            ob[dev, slot * HEADS // TILE:(slot + 1) * HEADS // TILE] = tile
             meta[dev, slot:slot + 1, :] = jnp.where(
                 lane == 0, local + 1, jnp.where(lane == 1, r % run, 0)
             ).astype(F32)
         if r % run == run - 1 or r == rows - 1:
             if r == rows - 1:
-                ob[:, slots * HEADS:, :] = meta[...].astype(BF)
-                part = slice(slot * HEADS, slots * HEADS + 8)
+                ob[:, slots * HEADS // TILE] = meta[:, 0:TILE].astype(BF)
+                part = slice(slot * HEADS // TILE, slots * HEADS // TILE + 1)
             else:
-                part = slice(slot * HEADS, (slot + 1) * HEADS)
+                part = slice(slot * HEADS // TILE, (slot + 1) * HEADS // TILE)
             sends.append(pltpu.make_async_copy(ob.at[:, part], out.at[:, part], so.at[slot]))
             sends[-1].start()
     for c in sends:
@@ -113,10 +115,10 @@
     gw = HEADS // KV_HEADS
     span = hg * per
 
-    sg[...] = x[:, qrows:qrows + 8, :].astype(F32).reshape(n * 8, LANES)
     for q in range(slots):
-        mv[q * 8:(q + 1) * 8, 0:n] = jnp.transpose(
-            sg[pl.ds(q, n, stride=8), :])[0:8, :].astype(jnp.int32)
+        for d in range(n):
+            sg[d:d + 1, :] = x[d, qrows // TILE, q:q + 1, :].astype(F32)
+        mv[q * 8:(q + 1) * 8, 0:n] = jnp.transpose(sg[0:n, :])[0:8, :].astype(jnp.int32)
     table = pltpu.make_async_copy(mv, ms, sem.at[0])
     table.start()
     sg[...] = jnp.zeros_like(sg)
@@ -133,7 +135,8 @@
     def send(step, grp):
         first = grp * g + step * CLASSES
         return pltpu.make_async_copy(
-            ob.at[pl.ds(first, CLASSES), 0:span], out.at[pl.ds(first, CLASSES), 0:span], so.at[step, grp])
+            ob.at[pl.ds(first, CLASSES), 0:span // PART],
+            out.at[pl.ds(first, CLASSES), 0:span // PART], so.at[step, grp])
 
     def lump(v):
         v = jnp.where(own, v, 0.0)
@@ -157,7 +160,7 @@
             kb = kv[0, pl.ds(base, BLOCK_TOKENS), :]
             kc = jnp.concatenate([kb[:, k * WIDTH:(k + 1) * WIDTH] for k in range(KV_HEADS)], axis=0)
             scores.append(lax.dot_general(
-                x[dev, q * HEADS:(q + 1) * HEADS, :], kc,
+                x[dev, q * HEADS // TILE:(q + 1) * HEADS // TILE].reshape(HEADS, WIDTH), kc,
                 (((1,), (1,)), ((), ())), preferred_element_type=F32))
         soft = []
         for s, (dev, q, length, base, c, at, rr) in zip(scores, todo):
@@ -179,7 +182,8 @@
                 for a in range(KV_HEADS // held)], axis=0)
             o = jnp.dot(wide, vc, preferred_element_type=F32)
             for grp in range(ngrp):
-                ob[grp * g + step * CLASSES + c, at * hg:(at + 1) * hg, :] = o[grp * hg:(grp + 1) * hg].astype(BF)
+                ob[grp * g + step * CLASSES + c, at * hg // PART:(at + 1) * hg // PART] = (
+                    o[grp * hg:(grp + 1) * hg].astype(BF).reshape(hg // PART, PART, LANES))
         for grp in range(ngrp):
             send(step, grp).start()
         for c in range(CLASSES):
@@ -197,14 +201,16 @@
             hi = top.astype(BF).astype(F32)
             mid = (top - hi).astype(BF).astype(F32)
             big = tot.astype(BF).astype(F32)
-            for t, v in enumerate((hi, mid, top - hi - mid, big, tot - big, jnp.broadcast_to(who, top.shape))):
-                sg[pl.ds((step * CLASSES + c) * STATS + t, ngrp, stride=g * STATS), :] = v
+            lower = lane[0:ngrp] < LANES // 2
+            pairs_of = ((hi, big), (mid, tot - big), (top - hi - mid, jnp.broadcast_to(who, top.shape)))
+            for t, (u, v) in enumerate(pairs_of):
+                sg[pl.ds((step * CLASSES + c) * PART + t, ngrp, stride=g * PART), :] = jnp.where(lower, u, v)
         return carry
 
     steps = g // CLASSES
     lax.fori_loop(0, steps, some, 0)
-    ob[:, span:, :] = sg[...].reshape(n, STATS, LANES).astype(BF)
-    last = pltpu.make_async_copy(ob.at[:, span:], out.at[:, span:], st)
+    ob[:, span // PART] = sg[0:n * PART, :].reshape(n, PART, LANES).astype(BF)
+    last = pltpu.make_async_copy(ob.at[:, span // PART], out.at[:, span // PART], st)
     last.start()
     for step in range(steps):
         for grp in range(ngrp):
@@ -218,13 +224,13 @@
     sds = jax.ShapeDtypeStruct
     return call(
         functools.partial(attend_kernel, n, slots, g, hg),
-        sds((n, span + STATS, LANES), BF), [HB, VM, VM],
+        sds((n, span // PART + 1, PART, LANES), BF), [HB, VM, VM],
         [
             pltpu.SMEM(block_len.shape, jnp.int32),
             pltpu.VMEM((slots * 8, LANES), jnp.int32),
             pltpu.SMEM((slots * 8, LANES), jnp.int32),
             pltpu.VMEM((n * STATS, LANES), F32),
-            pltpu.VMEM((n, span + STATS, LANES), BF),
+            pltpu.VMEM((n, span // PART + 1, PART, LANES), BF),
             pltpu.SemaphoreType.DMA((2,)),
             pltpu.SemaphoreType.DMA((g // CLASSES, n // g)),
             pltpu.SemaphoreType.DMA,
@@ -249,11 +255,18 @@
     per = pairs // g
     span = hg * per
     cnt = n // g
-    sf[...] = x[:, span:, :].astype(F32).reshape(n * STATS, LANES)
-    m = (sf[pl.ds(0, n, stride=STATS), :] + sf[pl.ds(1, n, stride=STATS), :]
-         + sf[pl.ds(2, n, stride=STATS), :])
-    l = sf[pl.ds(3, n, stride=STATS), :] + sf[pl.ds(4, n, stride=STATS), :]
-    rid = sf[pl.ds(5, n, stride=STATS), :]
+    sf[...] = x[:, span // PART].astype(F32).reshape(n * PART, LANES)
+    first, second, third = (sf[pl.ds(t, n, stride=PART), :] for t in range(3))
+    lower = lax.broadcasted_iota(jnp.int32, (n, LANES), 1) < LANES // 2
+
+    def turn(v):
+        return pltpu.roll(v, LANES // 2, 1)
+
+    m = first + second + third
+    m = jnp.where(lower, m, turn(m))
+    l = first + second
+    l = jnp.where(lower, turn(l), l)
+    rid = jnp.where(lower, turn(third), third)
     peak = jnp.zeros_like(m)
     for r in range(run):
         mine = rid == r
@@ -287,7 +300,7 @@
             blk_c = jnp.where(side == u, c[d:d + 1, :], blk_c)
             blk_t = jnp.where(side == u, target[d:d + 1, :], blk_t)
         cm[:, t * LANES:(t + 1) * LANES] = jnp.where(row == blk_t, blk_c, 0.0).astype(BF)
-    a = x[:, 0:span, :].reshape(n * span, LANES)
+    a = x[:, 0:span // PART].reshape(n * span, LANES)
     att = jnp.dot(cm[...], a, preferred_element_type=F32).astype(BF)
     ab[...] = jnp.concatenate([att[i * local:(i + 1) * local, :] for i in range(hg)], axis=1)
     for far in range(0, g, 2):
@@ -437,16 +450,16 @@
     ).astype(jnp.int32)
     index = (flat * CAP + slot).reshape(expert_ids.shape)
 
-    chunk = slots * HEADS + 8
+    chunk = slots * HEADS // TILE + 1
     sent = call(
         functools.partial(pack_kernel, run, slots, blocks),
-        sds((n, chunk, LANES), BF), [HB, HB],
+        sds((n, chunk, TILE, LANES), BF), [HB, HB],
         [
             pltpu.SMEM(block_ids.shape, jnp.int32),
             pltpu.VMEM(queries.shape, BF),
             pltpu.VMEM((rows * HEADS, LANES), F32),
             pltpu.VMEM((n, 8, LANES), F32),
-            pltpu.VMEM((n, chunk, LANES), BF),
+            pltpu.VMEM((n, chunk, TILE, LANES), BF),
             pltpu.SemaphoreType.DMA((2,)),
             pltpu.SemaphoreType.DMA((slots,)),
         ],
@@ -460,7 +473,7 @@
         functools.partial(project_kernel, n, slots, g, hg, run, rows),
         (sds((rows, width), BF),) * cnt, [VM] + [ANY] * g,
         [
-            pltpu.VMEM((n * STATS, LANES), F32),
+            pltpu.VMEM((n * PART, LANES), F32),
             pltpu.VMEM((hg * local, n * span), BF),
             pltpu.VMEM((g * fw, width), BF),
             pltpu.VMEM((cnt, rows, width), F32),

time: 111 us -> 111 us (level)
  Pallas kernels: 14.6 us -> 15.8 us
  waiting for transfers between devices: 57.3 us -> 56.1 us
where the time goes in v6:
time: 111 us
  waiting for transfers between devices  56.1 us (51%)
  starting transfers between devices  21.5 us (19%)
  Pallas kernels  15.8 us (14%)
  blocking collectives  12.7 us (11%)
  local copies, waits for them, and re-layouts  3.66 us (3%)
    ppermute x3, waiting for transfers between devices, shards(): lax.ppermute(out_weight, 'section', [(i, i ^ far) for i in range(n)])  28.1 us
    all_to_all x1, waiting for transfers between devices, shards(): asked = a2a(sent)  14.1 us
    all_to_all x1, blocking collectives, shards(): returned = a2a(done)  12.7 us
    all_to_all x1, waiting for transfers between devices, shards(): arrived = a2a(routed)  8.45 us
    all_to_all x1, starting transfers between devices, shards(): asked = a2a(sent)  7.33 us
    ppermute x3, starting transfers between devices, shards(): lax.ppermute(partial[j], 'section', [(i, i ^ j * g) for i in range(n)])  4.45 us
    pallas_call x1, Pallas kernels, attend(): call(functools.partial(attend_kernel, n, slots, g, hg), sds((n, span // P...  3.87 us
    pallas_call x1, Pallas kernels, run_expert(): call(expert_kernel, sds((slots_in, tiles, LANES), BF), [VM, VM, ANY, ANY]...  3.78 us
  transfers between devices with their start and end apart: 13, of which 7 were waited for; matrix products, arithmetic and copies ran while one was open for 0% of the time, Pallas kernels for 0%

profile of v6, /device:TPU:0, one launch (start us, length us, event | category | flops | bytes accessed | tf_op | source)
XLA Modules:
  0.0 110.7 jit_solution(9076674223071205923)
XLA Ops:
  0.6 0.0 copy-start.7
  0.6 2.2 %shard_map.131 = bf16[32,33,2,128]{3,2,1,0:T(2,128)(2,1)} custom-call(s32[8,8]{1,0:T(8,128)} %ids_in.1, bf16[8,4096]{1,0:T(8,128)(2,1)} %q_in.1), custom_call_target="tpu_custom_call" | custom-call | bytes 67108864 | tf_op jit(solution)/shard_map/pallas_call | solution.py:454
  2.9 7.3 %all-to-all-start = ((bf16[32,33,2,128]{3,2,1,0:T(2,128)(2,1)}), bf16[32,33,2,128]{3,2,1,0:T(2,128)(2,1)S(1)}, u32[]{:S(2)}, u32[]{:S(2)}) async-start(bf16[32,33,2,128]{3,2,1,0:T(2,128)(2,1)} %shard_map.131), calls=%async_computation | async-start | bytes 1081344 | tf_op jit(solution)/shard_map/all_to_all | solution.py:468
  10.2 0.0 copy-start.1
  10.2 1.6 %copy-done.1 = bf16[2,1024,512]{2,1,0:T(8,128)(2,1)S(1)} copy-done((bf16[2,1024,512]{2,1,0:T(8,128)(2,1)S(1)}, bf16[2,1024,512]{2,1,0:T(8,128)(2,1)}, u32[]{:S(2)}) %copy-start.1) | copy-done | bytes 2097176
  11.8 0.1 shard_map.132.kv
  11.9 0.0 copy-start.2
  12.0 0.0 copy-start.8
  12.0 14.1 %all-to-all-done.x = bf16[32,33,2,128]{3,2,1,0:T(2,128)(2,1)S(1)} async-done(((bf16[32,33,2,128]{3,2,1,0:T(2,128)(2,1)}), bf16[32,33,2,128]{3,2,1,0:T(2,128)(2,1)S(1)}, u32[]{:S(2)}, u32[]{:S(2)}) %all-to-all-start) | async-done | bytes 540704 | tf_op jit(solution)/shard_map/all_to_all | solution.py:468
  26.1 0.0 copy-done.7
  26.1 3.9 %shard_map.133 = bf16[32,17,4,128]{3,2,1,0:T(4,128)(2,1)} custom-call(s32[16]{0:T(128)S(1)} %copy-done.7, bf16[32,33,2,128]{3,2,1,0:T(2,128)(2,1)S(1)} %all-to-all-done.x, bf16[2,1024,512]{2,1,0:T(8,128)(2,1)S(1)} %shard_map.132.kv), custom_call_target="tpu_custom_call" | custom-call | flops 67108864 | bytes 67108864 | tf_op jit(solution)/shard_map/pallas_call | solution.py:225
  30.0 0.0 copy-start.3
  30.0 0.0 copy-start.5
  30.0 3.0 %all-to-all-start.1 = ((bf16[32,17,4,128]{3,2,1,0:T(4,128)(2,1)}), bf16[32,17,4,128]{3,2,1,0:T(4,128)(2,1)S(1)}, u32[]{:S(2)}, u32[]{:S(2)}) async-start(bf16[32,17,4,128]{3,2,1,0:T(4,128)(2,1)} %shard_map.133), calls=%async_computation.1 | async-start | bytes 1114112 | tf_op jit(solution)/shard_map/all_to_all | solution.py:470
  33.1 0.0 copy-done.2
  33.1 1.8 %collective-permute-start.1 = (bf16[128,2048]{1,0:T(8,128)(2,1)S(1)}, bf16[128,2048]{1,0:T(8,128)(2,1)S(1)}, u32[]{:S(2)}, u32[]{:S(2)}) collective-permute-start(bf16[128,2048]{1,0:T(8,128)(2,1)S(1)} %copy-done.2), channel_id=1, source_target_pairs={{0,2},{1,3},{2,0},{3,1},{4,6},{5,7},{6,4},{7,5},{8,10},{9,11},{10,... | collective-permute-start | bytes 1572872 | tf_op jit(solution)/shard_map/ppermute | solution.py:440
  34.9 1.5 %collective-permute-start.3 = (bf16[128,2048]{1,0:T(8,128)(2,1)S(1)}, bf16[128,2048]{1,0:T(8,128)(2,1)S(1)}, u32[]{:S(2)}, u32[]{:S(2)}) collective-permute-start(bf16[128,2048]{1,0:T(8,128)(2,1)S(1)} %copy-done.2), channel_id=1, source_target_pairs={{0,4},{1,5},{2,6},{3,7},{4,0},{5,1},{6,2},{7,3},{8,12},{9,13},{10,... | collective-permute-start | bytes 1572872 | tf_op jit(solution)/shard_map/ppermute | solution.py:440
  36.4 0.3 collective-permute-start.5
  36.6 0.0 collective-permute-start
  36.6 17.0 %collective-permute-done.1.refs_2_ = bf16[128,2048]{1,0:T(8,128)(2,1)S(1)} collective-permute-done((bf16[128,2048]{1,0:T(8,128)(2,1)S(1)}, bf16[128,2048]{1,0:T(8,128)(2,1)S(1)}, u32[]{:S(2)}, u32[]{:S(2)}) %collective-permute-start.1) | collective-permute-done | bytes 524320 | tf_op jit(solution)/shard_map/ppermute | solution.py:440
  53.7 0.0 collective-permute-start.2
  53.7 0.0 collective-permute-done.3.refs_4_
  53.7 0.5 collective-permute-start.4
  54.2 11.0 %collective-permute-done.5.refs_6_ = bf16[128,2048]{1,0:T(8,128)(2,1)S(1)} collective-permute-done((bf16[128,2048]{1,0:T(8,128)(2,1)S(1)}, bf16[128,2048]{1,0:T(8,128)(2,1)S(1)}, u32[]{:S(2)}, u32[]{:S(2)}) %collective-permute-start.5) | collective-permute-done | bytes 524320 | tf_op jit(solution)/shard_map/ppermute | solution.py:440
  65.2 0.0 collective-permute-start.6
  65.2 0.0 copy-done.8
  65.2 0.1 eq.15
  65.3 0.2 convert_reduce_fusion
  65.5 0.1 reduce_sum.12
  65.6 0.0 collective-permute-done.refs_1_
  65.6 0.0 collective-permute-done.2.refs_3_
  65.6 0.0 collective-permute-done.4.refs_5_
  65.6 1.7 %collective-permute-done.6.refs_7_ = bf16[128,2048]{1,0:T(8,128)(2,1)} collective-permute-done((bf16[128,2048]{1,0:T(8,128)(2,1)S(1)}, bf16[128,2048]{1,0:T(8,128)(2,1)}, u32[]{:S(2)}, u32[]{:S(2)}) %collective-permute-start.6) | collective-permute-done | bytes 524320 | tf_op jit(solution)/shard_map/ppermute | solution.py:444
  67.3 0.0 all-to-all-done.1.x
  67.3 2.8 %shard_map.134 = (bf16[8,2048]{1,0:T(8,128)(2,1)S(1)}, bf16[8,2048]{1,0:T(8,128)(2,1)S(1)}, bf16[8,2048]{1,0:T(8,128)(2,1)S(1)}, bf16[8,2048]{1,0:T(8,128)(2,1)S(1)}) custom-call(bf16[32,17,4,128]{3,2,1,0:T(4,128)(2,1)S(1)} %all-to-all-done.1.x, bf16[128,2048]{1,0:T(8,128)(2,1)S(1)} %copy-done.2, bf16[128,2048]{1,0:T(8,128)(2,1)} %collective-permute-done.refs_1_, ...), custom_call_target="tpu_custom_call" | custom-call | flops 134217728 | bytes 67108864 | tf_op jit(solution)/shard_map/pallas_call | solution.py:472
  70.0 3.4 %collective-permute-start.7 = (bf16[8,2048]{1,0:T(8,128)(2,1)S(1)}, bf16[8,2048]{1,0:T(8,128)(2,1)S(1)}, u32[]{:S(2)}, u32[]{:S(2)}) collective-permute-start(bf16[8,2048]{1,0:T(8,128)(2,1)S(1)} %get-tuple-element.9), channel_id=1, source_target_pairs={{0,24},{1,25},{2,26},{3,27},{4,28},{5,29},{6,30},{7,31},{8,16},{9,... | collective-permute-start | bytes 98312 | tf_op jit(solution)/shard_map/ppermute | solution.py:488
  73.4 0.0 collective-permute-start.8
  73.4 1.1 collective-permute-start.9
  74.5 1.3 %collective-permute-done.7.refs_1_ = bf16[8,2048]{1,0:T(8,128)(2,1)S(1)} collective-permute-done((bf16[8,2048]{1,0:T(8,128)(2,1)S(1)}, bf16[8,2048]{1,0:T(8,128)(2,1)S(1)}, u32[]{:S(2)}, u32[]{:S(2)}) %collective-permute-start.7) | collective-permute-done | bytes 32800 | tf_op jit(solution)/shard_map/ppermute | solution.py:488
  75.8 2.4 %collective-permute-done.8.refs_2_ = bf16[8,2048]{1,0:T(8,128)(2,1)S(1)} collective-permute-done((bf16[8,2048]{1,0:T(8,128)(2,1)S(1)}, bf16[8,2048]{1,0:T(8,128)(2,1)S(1)}, u32[]{:S(2)}, u32[]{:S(2)}) %collective-permute-start.8) | collective-permute-done | bytes 32800 | tf_op jit(solution)/shard_map/ppermute | solution.py:488
  78.2 0.0 collective-permute-done.9.refs_3_
  78.2 0.0 copy-done.3
  78.2 0.0 copy-done.5
  78.2 1.4 %shard_map.135 = (bf16[8,2048]{1,0:T(8,128)(2,1)}, bf16[64,16,128]{2,1,0:T(8,128)(2,1)}) custom-call(s32[8,8]{1,0:T(8,128)S(1)} %multiply_add_fusion.index_in, bf16[8,2048]{1,0:T(8,128)(2,1)S(1)} %get-tuple-element.8.refs_0_.refs_1_, bf16[8,2048]{1,0:T(8,128)(2,1)S(1)} %collective-permute-done.7.refs_1_, bf16[8,2048]{1,0:T(8,128)(2,1)S(1)} %collective-permute-done.8.refs_2_, ...), custom_call_target="tpu_custom_call" | custom-call | bytes 67108864 | tf_op jit(solution)/shard_map/pallas_call | solution.py:490
  79.7 2.6 %all-to-all-start.2 = ((bf16[64,16,128]{2,1,0:T(8,128)(2,1)}), bf16[64,16,128]{2,1,0:T(8,128)(2,1)S(1)}, u32[]{:S(2)}, u32[]{:S(2)}) async-start(bf16[64,16,128]{2,1,0:T(8,128)(2,1)} %get-tuple-element.13), calls=%async_computation.2 | async-start | bytes 524288 | tf_op jit(solution)/shard_map/all_to_all | solution.py:502
  82.3 0.0 copy-start
  82.3 1.9 %copy-done = bf16[1,2048,768]{2,1,0:T(8,128)(2,1)S(1)} copy-done((bf16[1,2048,768]{2,1,0:T(8,128)(2,1)S(1)}, bf16[1,2048,768]{2,1,0:T(8,128)(2,1)}, u32[]{:S(2)}) %copy-start) | copy-done | bytes 3145752
  84.2 0.2 shard_map.136
  84.4 8.5 %all-to-all-done.2.x = bf16[64,16,128]{2,1,0:T(8,128)(2,1)S(1)} async-done(((bf16[64,16,128]{2,1,0:T(8,128)(2,1)}), bf16[64,16,128]{2,1,0:T(8,128)(2,1)S(1)}, u32[]{:S(2)}, u32[]{:S(2)}) %all-to-all-start.2) | async-done | bytes 262176 | tf_op jit(solution)/shard_map/all_to_all | solution.py:502
  92.8 0.0 copy-start.4
  92.8 0.0 copy-start.6
  92.8 3.8 %shard_map.137 = bf16[64,16,128]{2,1,0:T(8,128)(2,1)S(1)} custom-call(bf16[64,16,128]{2,1,0:T(8,128)(2,1)S(1)} %all-to-all-done.2.x, bf16[2048,768]{1,0:T(8,128)(2,1)S(1)} %bitcast.4, bf16[2048,768]{1,0:T(8,128)(2,1)} %bitcast.6, bf16[768,2048]{1,0:T(8,128)(2,1)} %bitcast.7), custom_call_target="tpu_custom_call" | custom-call | flops 603979776 | bytes 9437184 | tf_op jit(solution)/shard_map/pallas_call | solution.py:507
  96.6 12.7 %all_to_all.20.x = bf16[64,16,128]{2,1,0:T(8,128)(2,1)S(1)} all-to-all(bf16[64,16,128]{2,1,0:T(8,128)(2,1)S(1)} %shard_map.137), channel_id=1, replica_groups=mesh['groups'=1,'section'=32] {'section'}, dimensions={0} | all-to-all | bytes 524288 | tf_op jit(solution)/shard_map/all_to_all | solution.py:530
  109.3 0.0 copy-done.4
  109.3 0.0 copy-done.6
  109.3 1.4 %shard_map.138 = bf16[8,2048]{1,0:T(8,128)(2,1)} custom-call(s32[8,8]{1,0:T(8,128)S(1)} %multiply_add_fusion.index_in, f32[8,8]{1,0:T(8,128)S(1)} %copy-done.6, bf16[64,16,128]{2,1,0:T(8,128)(2,1)S(1)} %all_to_all.20.x, bf16[8,2048]{1,0:T(8,128)(2,1)S(1)} %copy-done.3, bf16[8,2048]{1,0:T(8,128)(2,1)S(1)} %copy-done.4), custom_call_target="tpu_custom_call" | custom-call | bytes 524288 | tf_op jit(solution)/shard_map/pallas_call | solution.py:531
  (1 shorter events, 0.0 us)
Async XLA Ops:
  0.6 25.5 %copy-start.7 = (s32[16]{0:T(128)S(1)}, s32[16]{0:T(128)}, u32[]{:S(2)}) copy-start(s32[16]{0:T(128)} %lens_in.1) | copy-start | bytes 196
  2.9 23.2 %all-to-all-start = ((bf16[32,33,2,128]{3,2,1,0:T(2,128)(2,1)}), bf16[32,33,2,128]{3,2,1,0:T(2,128)(2,1)S(1)}, u32[]{:S(2)}, u32[]{:S(2)}) async-start(bf16[32,33,2,128]{3,2,1,0:T(2,128)(2,1)} %shard_map.131), calls=%async_computation | async-start | bytes 1081344 | tf_op jit(solution)/shard_map/all_to_all | solution.py:468
  10.2 1.6 %copy-start.1 = (bf16[2,1024,512]{2,1,0:T(8,128)(2,1)S(1)}, bf16[2,1024,512]{2,1,0:T(8,128)(2,1)}, u32[]{:S(2)}) copy-start(bf16[2,1024,512]{2,1,0:T(8,128)(2,1)} %refs_0_.3) | copy-start | bytes 6291460
  11.9 21.1 %copy-start.2 = (bf16[128,2048]{1,0:T(8,128)(2,1)S(1)}, bf16[128,2048]{1,0:T(8,128)(2,1)}, u32[]{:S(2)}) copy-start(bf16[128,2048]{1,0:T(8,128)(2,1)} %refs_0_.4) | copy-start | bytes 1572868
  12.0 53.3 %copy-start.8 = (s32[8,8]{1,0:T(8,128)S(1)}, s32[8,8]{1,0:T(8,128)}, u32[]{:S(2)}) copy-start(s32[8,8]{1,0:T(8,128)} %param.19) | copy-start | bytes 772
  30.0 48.3 %copy-start.3 = (bf16[8,2048]{1,0:T(8,128)(2,1)S(1)}, bf16[8,2048]{1,0:T(8,128)(2,1)}, u32[]{:S(2)}) copy-start(bf16[8,2048]{1,0:T(8,128)(2,1)} %res.1) | copy-start | bytes 98308
  30.0 48.2 %copy-start.5 = (f32[2048]{0:T(1024)S(1)}, f32[2048]{0:T(1024)}, u32[]{:S(2)}) copy-start(f32[2048]{0:T(1024)} %param.18) | copy-start | bytes 24580
  30.0 37.3 %all-to-all-start.1 = ((bf16[32,17,4,128]{3,2,1,0:T(4,128)(2,1)}), bf16[32,17,4,128]{3,2,1,0:T(4,128)(2,1)S(1)}, u32[]{:S(2)}, u32[]{:S(2)}) async-start(bf16[32,17,4,128]{3,2,1,0:T(4,128)(2,1)} %shard_map.133), calls=%async_computation.1 | async-start | bytes 1114112 | tf_op jit(solution)/shard_map/all_to_all | solution.py:470
  33.1 20.6 %collective-permute-start.1 = (bf16[128,2048]{1,0:T(8,128)(2,1)S(1)}, bf16[128,2048]{1,0:T(8,128)(2,1)S(1)}, u32[]{:S(2)}, u32[]{:S(2)}) collective-permute-start(bf16[128,2048]{1,0:T(8,128)(2,1)S(1)} %copy-done.2), channel_id=1, source_target_pairs={{0,2},{1,3},{2,0},{3,1},{4,6},{5,7},{6,4},{7,5},{8,10},{9,11},{10,... | collective-permute-start | bytes 1572872 | tf_op jit(solution)/shard_map/ppermute | solution.py:440
  34.9 18.8 %collective-permute-start.3 = (bf16[128,2048]{1,0:T(8,128)(2,1)S(1)}, bf16[128,2048]{1,0:T(8,128)(2,1)S(1)}, u32[]{:S(2)}, u32[]{:S(2)}) collective-permute-start(bf16[128,2048]{1,0:T(8,128)(2,1)S(1)} %copy-done.2), channel_id=1, source_target_pairs={{0,4},{1,5},{2,6},{3,7},{4,0},{5,1},{6,2},{7,3},{8,12},{9,13},{10,... | collective-permute-start | bytes 1572872 | tf_op jit(solution)/shard_map/ppermute | solution.py:440
  36.4 28.9 %collective-permute-start.5 = (bf16[128,2048]{1,0:T(8,128)(2,1)S(1)}, bf16[128,2048]{1,0:T(8,128)(2,1)S(1)}, u32[]{:S(2)}, u32[]{:S(2)}) collective-permute-start(bf16[128,2048]{1,0:T(8,128)(2,1)S(1)} %copy-done.2), channel_id=1, source_target_pairs={{0,6},{1,7},{2,4},{3,5},{4,2},{5,3},{6,0},{7,1},{8,14},{9,15},{10,... | collective-permute-start | bytes 1572872 | tf_op jit(solution)/shard_map/ppermute | solution.py:440
  36.6 28.9 %collective-permute-start = (bf16[128,2048]{1,0:T(8,128)(2,1)S(1)}, bf16[128,2048]{1,0:T(8,128)(2,1)}, u32[]{:S(2)}, u32[]{:S(2)}) collective-permute-start(bf16[128,2048]{1,0:T(8,128)(2,1)S(1)} %copy-done.2), channel_id=1, source_target_pairs={{0,1},{1,0},{2,3},{3,2},{4,5},{5,4},{6,7},{7,6},{8,9},{9,8},{10,11... | collective-permute-start | bytes 1572872 | tf_op jit(solution)/shard_map/ppermute | solution.py:444
  53.7 11.9 %collective-permute-start.2 = (bf16[128,2048]{1,0:T(8,128)(2,1)S(1)}, bf16[128,2048]{1,0:T(8,128)(2,1)}, u32[]{:S(2)}, u32[]{:S(2)}) collective-permute-start(bf16[128,2048]{1,0:T(8,128)(2,1)S(1)} %collective-permute-done.1.refs_2_), channel_id=1, source_target_pairs={{0,1},{1,0},{2,3},{3,2},{4,5},{5,4},{6,7},{7,6},{8,9},{9,8},{10,11... | collective-permute-start | bytes 1572872 | tf_op jit(solution)/shard_map/ppermute | solution.py:444
  53.7 11.9 %collective-permute-start.4 = (bf16[128,2048]{1,0:T(8,128)(2,1)S(1)}, bf16[128,2048]{1,0:T(8,128)(2,1)}, u32[]{:S(2)}, u32[]{:S(2)}) collective-permute-start(bf16[128,2048]{1,0:T(8,128)(2,1)S(1)} %collective-permute-done.3.refs_4_), channel_id=1, source_target_pairs={{0,1},{1,0},{2,3},{3,2},{4,5},{5,4},{6,7},{7,6},{8,9},{9,8},{10,11... | collective-permute-start | bytes 1572872 | tf_op jit(solution)/shard_map/ppermute | solution.py:444
  65.2 2.0 %collective-permute-start.6 = (bf16[128,2048]{1,0:T(8,128)(2,1)S(1)}, bf16[128,2048]{1,0:T(8,128)(2,1)}, u32[]{:S(2)}, u32[]{:S(2)}) collective-permute-start(bf16[128,2048]{1,0:T(8,128)(2,1)S(1)} %collective-permute-done.5.refs_6_), channel_id=1, source_target_pairs={{0,1},{1,0},{2,3},{3,2},{4,5},{5,4},{6,7},{7,6},{8,9},{9,8},{10,11... | collective-permute-start | bytes 1572872 | tf_op jit(solution)/shard_map/ppermute | solution.py:444
  70.0 5.8 %collective-permute-start.7 = (bf16[8,2048]{1,0:T(8,128)(2,1)S(1)}, bf16[8,2048]{1,0:T(8,128)(2,1)S(1)}, u32[]{:S(2)}, u32[]{:S(2)}) collective-permute-start(bf16[8,2048]{1,0:T(8,128)(2,1)S(1)} %get-tuple-element.9), channel_id=1, source_target_pairs={{0,24},{1,25},{2,26},{3,27},{4,28},{5,29},{6,30},{7,31},{8,16},{9,... | collective-permute-start | bytes 98312 | tf_op jit(solution)/shard_map/ppermute | solution.py:488
  73.4 4.8 %collective-permute-start.8 = (bf16[8,2048]{1,0:T(8,128)(2,1)S(1)}, bf16[8,2048]{1,0:T(8,128)(2,1)S(1)}, u32[]{:S(2)}, u32[]{:S(2)}) collective-permute-start(bf16[8,2048]{1,0:T(8,128)(2,1)S(1)} %get-tuple-element.10), channel_id=1, source_target_pairs={{0,16},{1,17},{2,18},{3,19},{4,20},{5,21},{6,22},{7,23},{8,24},{9,... | collective-permute-start | bytes 98312 | tf_op jit(solution)/shard_map/ppermute | solution.py:488
  73.4 4.8 %collective-permute-start.9 = (bf16[8,2048]{1,0:T(8,128)(2,1)S(1)}, bf16[8,2048]{1,0:T(8,128)(2,1)S(1)}, u32[]{:S(2)}, u32[]{:S(2)}) collective-permute-start(bf16[8,2048]{1,0:T(8,128)(2,1)S(1)} %get-tuple-element.11), channel_id=1, source_target_pairs={{0,8},{1,9},{2,10},{3,11},{4,12},{5,13},{6,14},{7,15},{8,0},{9,1},... | collective-permute-start | bytes 98312 | tf_op jit(solution)/shard_map/ppermute | solution.py:488
  79.7 13.2 %all-to-all-start.2 = ((bf16[64,16,128]{2,1,0:T(8,128)(2,1)}), bf16[64,16,128]{2,1,0:T(8,128)(2,1)S(1)}, u32[]{:S(2)}, u32[]{:S(2)}) async-start(bf16[64,16,128]{2,1,0:T(8,128)(2,1)} %get-tuple-element.13), calls=%async_computation.2 | async-start | bytes 524288 | tf_op jit(solution)/shard_map/all_to_all | solution.py:502
  82.3 1.9 %copy-start = (bf16[1,2048,768]{2,1,0:T(8,128)(2,1)S(1)}, bf16[1,2048,768]{2,1,0:T(8,128)(2,1)}, u32[]{:S(2)}) copy-start(bf16[1,2048,768]{2,1,0:T(8,128)(2,1)} %refs_0_.5) | copy-start | bytes 9437188
  92.8 16.5 %copy-start.4 = (bf16[8,2048]{1,0:T(8,128)(2,1)S(1)}, bf16[8,2048]{1,0:T(8,128)(2,1)}, u32[]{:S(2)}) copy-start(bf16[8,2048]{1,0:T(8,128)(2,1)} %get-tuple-element.6.proj) | copy-start | bytes 98308
  92.8 16.5 %copy-start.6 = (f32[8,8]{1,0:T(8,128)S(1)}, f32[8,8]{1,0:T(8,128)}, u32[]{:S(2)}) copy-start(f32[8,8]{1,0:T(8,128)} %rw_in.1) | copy-start | bytes 772
